TPU v7x, 32 devices: a whole 2x2x4 slice. The times are simulated.
32 devices in a mesh: pts: 8 (over y, x, core), cen: 4 (over z).
Axes of the slice: x: 2, y: 2, z: 4, core: 2. Of those that a mesh axis runs over, the one named last changes fastest.
Arguments:
- embeddings: float32 [8192, 64], P('pts'), may hold values from -0.75 to 0.75
- centroids: float32 [8192, 64], P('cen'), may hold values from -0.75 to 0.75
- point_duals: float32 [8192], P('pts'), may hold values from -4 to 0.1
- centroid_duals: float32 [8192], P('cen'), may hold values from -1.5 to 2.6
- targets: float32 [8192, 64], P('pts'), may hold values from -6 to 6
Outputs:
- grad_emb: float32 [8192, 64], P('pts')
- grad_cen: float32 [8192, 64], P(('cen', 'pts'))
All inputs are finite; a program needn't handle non-finite values.
Results may differ from a plain program's by a relative error of at most 0.0003.
Values sent between devices are 32-bit elements; how exact they have to be, the bound alone decides.
No kernel may reach another device: no remote copies, remote signals or barrier semaphores. Data moves between devices by JAX's collectives and lax.ppermute only.
A program may use at most 64 MiB of HBM per device.

v0:
```python
import math

import jax
import jax.numpy as jnp
from jax import lax
from jax.experimental import pallas as pl
from jax.experimental.pallas import tpu as pltpu
from jax.sharding import PartitionSpec as P


EPSILON = 0.08
LANES = 128
F32 = jnp.float32
BF16 = jnp.bfloat16
VMEM = pl.BlockSpec(memory_space=pltpu.VMEM)


def bits_of(count):
    return [1 << b for b in range(count.bit_length() - 1)]


def reverse_bits(k, count):
    size = len(bits_of(count))
    return sum(((k >> b) & 1) << (size - 1 - b) for b in range(size))


def split2(x):
    high = x.astype(BF16)
    low = (x - high.astype(F32)).astype(BF16)
    return high, low


def split3(x):
    high = x.astype(BF16)
    rest = x - high.astype(F32)
    mid = rest.astype(BF16)
    low = (rest - mid.astype(F32)).astype(BF16)
    return high, mid, low


def dot(a, b):
    return jnp.dot(a, b, preferred_element_type=F32)


def flat_row(blocks, out_ref):
    for g in range(blocks.shape[0]):
        out_ref[:, g * LANES : (g + 1) * LANES] = blocks[g : g + 1, :]


def transpose_into(out_ref, source, out_at=0):
    for g in range(source.shape[1] // LANES):
        gs = slice(g * LANES, (g + 1) * LANES)
        out_ref[gs, out_at : out_at + source.shape[0]] = source[:, gs].T.astype(out_ref.dtype)


def spread_rows(row):
    return jnp.broadcast_to(row, (LANES, LANES)).T


def gather_rows(block):
    return jnp.sum(block.T, axis=0, keepdims=True)


def dual_rows(dual, own_first):
    high, mid, low = (part.astype(F32) for part in split3(dual))
    at = lax.broadcasted_iota(jnp.int32, (8, dual.shape[1]), 0)
    first = 0 if own_first else 3
    ones = jnp.where(at < 6, 1.0, 0.0)
    rows = jnp.where(
        at == first, high, jnp.where(at == first + 1, mid, jnp.where(at == first + 2, low, ones))
    )
    return jnp.concatenate([rows, jnp.zeros((56, dual.shape[1]), F32)], axis=0)


def first_kernel(total, emb_ref, tgt_ref, cen_ref, pd_ref, cd_ref, plan_ref, cot_ref, rows_ref, cols_ref,
                 lhs_ref, tlhs_ref, rhs_ref, rm_ref, rl_ref, cm_ref, cl_ref, pdual_ref, cdual_ref):
    rows, cols = plan_ref.shape
    flat_row(pd_ref[...], pdual_ref)
    flat_row(cd_ref[...] - math.log(total), cdual_ref)
    eh, el = (part.astype(F32) for part in split2(emb_ref[...] * (1.0 / EPSILON)))
    th, tl = (part.astype(F32) for part in split2(tgt_ref[...]))
    transpose_into(lhs_ref, jnp.concatenate([eh, eh], axis=0))
    transpose_into(lhs_ref, jnp.concatenate([el, dual_rows(pdual_ref[...], True)], axis=0), LANES)
    transpose_into(tlhs_ref, jnp.concatenate([th, th], axis=0))
    transpose_into(tlhs_ref, jnp.concatenate([tl, jnp.zeros_like(tl)], axis=0), LANES)
    ch, cl = split2(cen_ref[...])
    rhs_ref[...] = jnp.concatenate([ch, cl, ch, dual_rows(cdual_ref[...], False).astype(BF16)], axis=0)
    cm_ref[...] = jnp.zeros_like(cm_ref)
    cl_ref[...] = jnp.zeros_like(cl_ref)
    tm, tn = 128, 256

    @pl.loop(0, rows // tm)
    def _(i):
        at = pl.ds(pl.multiple_of(i * tm, tm), tm)
        left = lhs_ref[at, :]
        tleft = tlhs_ref[at, :]
        mass = jnp.zeros((tm, LANES), F32)
        load = jnp.zeros((tm, LANES), F32)
        for j in range(cols // tn):
            js = slice(j * tn, (j + 1) * tn)
            right = rhs_ref[:, js]
            plan = jnp.exp(dot(left, right))
            cot = dot(tleft, right)
            plan_ref[at, js] = plan
            cot_ref[at, js] = cot
            weighted = plan * cot
            for h in range(tn // LANES):
                hs = slice(h * LANES, (h + 1) * LANES)
                mass = mass + plan[:, hs]
                load = load + weighted[:, hs]
            cm_ref[:, js] += jnp.sum(plan.reshape(tm // 8, 8, tn), axis=0)
            cl_ref[:, js] += jnp.sum(weighted.reshape(tm // 8, 8, tn), axis=0)
        rm_ref[at, :] = mass
        rl_ref[at, :] = load

    groups = rows // LANES
    for g in range(groups):
        gs = slice(g * LANES, (g + 1) * LANES)
        rows_ref[g : g + 1, :] = gather_rows(rm_ref[gs, :])
        rows_ref[groups + g : groups + g + 1, :] = gather_rows(rl_ref[gs, :])
    tiles = cols // LANES
    for t in range(tiles):
        ts = slice(t * LANES, (t + 1) * LANES)
        cols_ref[t : t + 1, :] = jnp.sum(cm_ref[:, ts], axis=0, keepdims=True)
        cols_ref[tiles + t : tiles + t + 1, :] = jnp.sum(cl_ref[:, ts], axis=0, keepdims=True)


def columns_of(plan_ref, scales, spread_ref, out_ref):
    rows, cols = plan_ref.shape
    tiles = cols // LANES
    count = len(scales)
    for k, scale in enumerate(scales):
        for g in range(rows // LANES):
            spread_ref[k, g * LANES : (g + 1) * LANES, :] = spread_rows(scale[g : g + 1, :])
    wide = 16 // count
    for t0 in range(0, tiles, wide):
        span = min(wide, tiles - t0)

        def step(i, acc, t0=t0, span=span):
            acc = list(acc)
            for r in range(2):
                at = pl.ds(pl.multiple_of(i * 16 + r * 8, 8), 8)
                scale_rows = [spread_ref[k, at, :] for k in range(count)]
                for t in range(span):
                    tile = plan_ref[at, (t0 + t) * LANES : (t0 + t + 1) * LANES]
                    for k in range(count):
                        acc[k * span + t] = acc[k * span + t] + tile * scale_rows[k]
            return tuple(acc)

        zero = jnp.zeros((8, LANES), F32)
        acc = lax.fori_loop(0, rows // 16, step, (zero,) * (count * span))
        for k in range(count):
            for t in range(span):
                at = k * tiles + t0 + t
                out_ref[at : at + 1, :] = jnp.sum(acc[k * span + t], axis=0, keepdims=True)


def rows_of(plan_ref, scales, part_ref, out_ref):
    rows, cols = plan_ref.shape
    tiles = cols // LANES
    groups = rows // LANES
    count = len(scales)
    spread = [
        [jnp.broadcast_to(scale[t : t + 1, :], (8, LANES)) for t in range(tiles)] for scale in scales
    ]

    @pl.loop(0, rows // 16)
    def _(i):
        for r in range(2):
            at = pl.ds(pl.multiple_of(i * 16 + r * 8, 8), 8)
            sums = [[None, None] for _ in range(count)]
            for t in range(tiles):
                tile = plan_ref[at, t * LANES : (t + 1) * LANES]
                for k in range(count):
                    term = tile * spread[k][t]
                    old = sums[k][t % 2]
                    sums[k][t % 2] = term if old is None else old + term
            for k in range(count):
                one, two = sums[k]
                part_ref[k, at, :] = one if two is None else one + two

    for k in range(count):
        for g in range(groups):
            at = k * groups + g
            out_ref[at : at + 1, :] = gather_rows(part_ref[k, g * LANES : (g + 1) * LANES, :])


def second_kernel(plan_ref, rows_ref, cols_ref, out_ref, own_ref, spread_ref):
    groups = rows_ref.shape[0] // 2
    tiles = own_ref.shape[0]
    scale = rows_ref[groups:, :] / rows_ref[:groups, :]
    columns_of(plan_ref, [scale], spread_ref, own_ref)
    out_ref[: 2 * tiles, :] = cols_ref[...]
    out_ref[2 * tiles :, :] = own_ref[...]


def third_kernel(plan_ref, cols_ref, out_ref, part_ref):
    tiles = cols_ref.shape[0] // 3
    mass = cols_ref[:tiles, :]
    load = cols_ref[tiles : 2 * tiles, :]
    beta = load - cols_ref[2 * tiles :, :]
    rows_of(plan_ref, [load / mass, beta / mass], part_ref, out_ref)


def fourth_kernel(plan_ref, rows_ref, terms_ref, out_ref, spread_ref):
    groups = rows_ref.shape[0] // 2
    mass = rows_ref[:groups, :]
    load = rows_ref[groups:, :]
    scales = [(load - terms_ref[k * groups : (k + 1) * groups, :]) / mass for k in range(2)]
    columns_of(plan_ref, scales, spread_ref, out_ref)


def fifth_kernel(plan_ref, cols_ref, terms_ref, out_ref, part_ref):
    tiles = cols_ref.shape[0] // 3
    beta = cols_ref[tiles : 2 * tiles, :] - terms_ref[:tiles, :]
    rows_of(plan_ref, [beta / cols_ref[:tiles, :]], part_ref, out_ref)


def weights_of(plan_ref, cot_ref, spread_ref, low, at, js):
    tn = js.stop - js.start
    spread = spread_ref[at, :]
    tm = spread.shape[0]
    shift = jnp.tile(spread, (1, tn // LANES)).reshape(tm // 8, 8, tn) + low[None]
    return split2(plan_ref[at, js] * (cot_ref[at, js] - shift.reshape(tm, tn)))


def scales_of(rows_ref, aterms_ref, cols_ref, bterms_ref, spread_ref, beta_ref):
    groups = rows_ref.shape[0] // 2
    tiles = cols_ref.shape[0] // 3
    alpha = (rows_ref[groups:, :] - aterms_ref[...]) / rows_ref[:groups, :]
    for g in range(groups):
        spread_ref[g * LANES : (g + 1) * LANES, :] = spread_rows(alpha[g : g + 1, :])
    beta = (cols_ref[tiles : 2 * tiles, :] - bterms_ref[tiles:, :]) / cols_ref[:tiles, :]
    for t in range(tiles):
        beta_ref[:, t * LANES : (t + 1) * LANES] = jnp.broadcast_to(beta[t : t + 1, :], (8, LANES))


def emb_kernel(plan_ref, cot_ref, cen_ref, rows_ref, aterms_ref, cols_ref, bterms_ref,
               keep_ref, send_ref, spread_out_ref, beta_ref, right_ref):
    _, cols = plan_ref.shape
    scales_of(rows_ref, aterms_ref, cols_ref, bterms_ref, spread_out_ref, beta_ref)
    ch, cl = split2(cen_ref[...])
    transpose_into(right_ref, jnp.concatenate([ch.astype(F32), cl.astype(F32)], axis=0))
    tn = 256
    half, width, span = keep_ref.shape
    chunks = 2 * half
    me = lax.axis_index("cen") & (half - 1)
    for q in range(chunks):
        at = pl.ds(pl.multiple_of((me ^ reverse_bits(q, chunks)) * span, span), span)
        acc = jnp.zeros((span, LANES), F32)
        for j in range(cols // tn):
            js = slice(j * tn, (j + 1) * tn)
            wh, wl = weights_of(plan_ref, cot_ref, spread_out_ref, beta_ref[:, js], at, js)
            right = right_ref[js, :]
            acc = acc + dot(wh, right) + dot(wl, right)
        flipped = acc.T
        to_ref = keep_ref if q < half else send_ref
        to_ref[q % half] = flipped[:width] + flipped[width:]


def cen_kernel(plan_ref, cot_ref, emb_ref, spread_ref, beta_ref, gcen_ref):
    rows, cols = plan_ref.shape
    left = jnp.concatenate(split2(emb_ref[...]), axis=0)
    tn = 256
    tm = 256
    chunks, width, chunk_cols = gcen_ref.shape
    me = lax.axis_index("pts")
    for j in range(cols // tn):
        js = slice(j * tn, (j + 1) * tn)
        gcen = jnp.zeros((2 * width, tn), F32)
        for i in range(rows // tm):
            at = slice(i * tm, (i + 1) * tm)
            wh, wl = weights_of(plan_ref, cot_ref, spread_ref, beta_ref[:, js], at, js)
            gcen = gcen + dot(left[:, at], wh) + dot(left[:, at], wl)
        gcen = gcen[:width] + gcen[width:]
        span = min(chunk_cols, tn)
        for s in range(tn // span):
            col = j * tn + s * span
            gcen_ref[reverse_bits(me ^ (col // chunk_cols), chunks), :, pl.ds(col % chunk_cols, span)] = gcen[
                :, s * span : (s + 1) * span
            ]


def last_kernel(gemb_ref, emb_ref):
    chunks, _, span = gemb_ref.shape
    me = lax.axis_index("cen") & (chunks // 2 - 1)
    for q in range(chunks):
        emb_ref[:, q * span : (q + 1) * span] = gemb_ref[reverse_bits(me ^ q, chunks)]


def swap(value, axis, count, bit):
    return lax.ppermute(value, axis, [(i, i ^ bit) for i in range(count)])


def sum_all(value, axis, count):
    for bit in bits_of(count):
        value = value + swap(value, axis, count, bit)
    return value


def shards(embeddings, centroids, point_duals, centroid_duals, targets):
    pts = lax.axis_size("pts")
    cen = lax.axis_size("cen")
    rows, width = embeddings.shape
    cols = centroids.shape[0]
    emb, tgt, ctr = embeddings.T, targets.T, centroids.T
    groups, tiles = rows // LANES, cols // LANES
    sds = jax.ShapeDtypeStruct

    def call(body, outs, scratch, mib, specs, *args, flops=1 << 30):
        return pl.pallas_call(
            body,
            out_shape=outs,
            in_specs=specs,
            out_specs=jax.tree.map(lambda _: VMEM, outs),
            scratch_shapes=scratch,
            cost_estimate=pl.CostEstimate(flops=flops, transcendentals=0, bytes_accessed=1 << 20),
            compiler_params=pltpu.CompilerParams(vmem_limit_bytes=mib << 20),
        )(*args)

    def first(*args):
        return first_kernel(float(cols * cen), *args)

    plan, cot, row_sums, col_sums = call(
        first,
        (
            pltpu.VMEM((rows, cols), F32),
            pltpu.VMEM((rows, cols), F32),
            pltpu.VMEM((2 * groups, LANES), F32),
            pltpu.VMEM((2 * tiles, LANES), F32),
        ),
        [
            pltpu.VMEM((rows, 256), BF16),
            pltpu.VMEM((rows, 256), BF16),
            pltpu.VMEM((256, cols), BF16),
            pltpu.VMEM((rows, LANES), F32),
            pltpu.VMEM((rows, LANES), F32),
            pltpu.VMEM((8, cols), F32),
            pltpu.VMEM((8, cols), F32),
            pltpu.VMEM((1, rows), F32),
            pltpu.VMEM((1, cols), F32),
        ],
        24,
        [VMEM] * 5,
        emb,
        tgt,
        ctr,
        point_duals.reshape(groups, LANES),
        centroid_duals.reshape(tiles, LANES),
    )
    row_sums = sum_all(row_sums, "cen", cen)
    col_all = call(
        second_kernel,
        pltpu.VMEM((3 * tiles, LANES), F32),
        [pltpu.VMEM((tiles, LANES), F32), pltpu.VMEM((1, rows, LANES), F32)],
        6,
        [VMEM] * 3,
        plan,
        row_sums,
        col_sums,
    )
    col_all = sum_all(col_all, "pts", pts)
    row_terms = call(
        third_kernel,
        pltpu.VMEM((2 * groups, LANES), F32),
        [pltpu.VMEM((2, rows, LANES), F32)],
        6,
        [VMEM] * 2,
        plan,
        col_all,
    )
    row_terms = sum_all(row_terms, "cen", cen)
    col_terms = call(
        fourth_kernel,
        pltpu.VMEM((2 * tiles, LANES), F32),
        [pltpu.VMEM((2, rows, LANES), F32)],
        6,
        [VMEM] * 3,
        plan,
        row_sums,
        row_terms,
    )
    col_terms = sum_all(col_terms, "pts", pts)
    last_terms = call(
        fifth_kernel,
        pltpu.VMEM((groups, LANES), F32),
        [pltpu.VMEM((1, rows, LANES), F32)],
        6,
        [VMEM] * 3,
        plan,
        col_all,
        col_terms,
    )
    last_terms = sum_all(last_terms, "cen", cen)
    gemb, sent, spread, beta = call(
        emb_kernel,
        (
            pltpu.VMEM((cen // 2, width, rows // cen), F32),
            pltpu.VMEM((cen // 2, width, rows // cen), F32),
            pltpu.VMEM((rows, LANES), F32),
            pltpu.VMEM((8, cols), F32),
        ),
        [pltpu.VMEM((cols, LANES), BF16)],
        12,
        [VMEM] * 7,
        plan,
        cot,
        ctr,
        row_sums,
        last_terms,
        col_all,
        col_terms,
    )
    sent = swap(sent, "cen", cen, 1)
    gcen = call(
        cen_kernel,
        pltpu.VMEM((pts, width, cols // pts), F32),
        [],
        12,
        [VMEM] * 5,
        plan,
        cot,
        emb,
        spread,
        beta,
        flops=1 << 33,
    )
    cbits, pbits = bits_of(cen), bits_of(pts)
    gemb = gemb + sent
    for bit in cbits[1:-1]:
        keep = gemb.shape[0] // 2
        gemb = gemb[:keep] + swap(gemb[keep:], "cen", cen, bit)
    gemb = gemb + swap(gemb, "cen", cen, cbits[-1])
    for bit in reversed(cbits[:-1]):
        gemb = jnp.concatenate([gemb, swap(gemb, "cen", cen, bit)], axis=0)
    for bit in pbits:
        keep = gcen.shape[0] // 2
        gcen = gcen[:keep] + swap(gcen[keep:], "pts", pts, bit)
    grad_emb = call(last_kernel, sds((width, rows), F32), [], 6, [VMEM], gemb)
    return grad_emb.T, gcen[0].T


def solution(mesh):
    in_specs = (P("pts", None), P("cen", None), P("pts"), P("cen"), P("pts", None))
    out_specs = (P("pts", None), P(("cen", "pts"), None))
    return jax.shard_map(shards, mesh=mesh, in_specs=in_specs, out_specs=out_specs, check_vma=False)
```

profile of v0, /device:TPU:0, one launch (start us, length us, event | category | flops | bytes accessed | tf_op | source)
XLA Modules:
  0.0 86.9 jit_solution(3890809670562335930)
XLA Ops:
  0.6 0.0 copy-start
  0.6 1.0 %copy-done = f32[2048,64]{0,1:T(8,128)S(1)} copy-done((f32[2048,64]{0,1:T(8,128)S(1)}, f32[2048,64]{0,1:T(8,128)}, u32[]{:S(2)}) %copy-start) | copy-done | bytes 524312
  1.7 0.0 copy-start.1
  1.7 0.9 %copy-done.1 = f32[1024,64]{0,1:T(8,128)S(1)} copy-done((f32[1024,64]{0,1:T(8,128)S(1)}, f32[1024,64]{0,1:T(8,128)}, u32[]{:S(2)}) %copy-start.1) | copy-done | bytes 262168
  2.6 0.0 copy-start.2
  2.6 0.9 %copy-done.2 = f32[1024,64]{0,1:T(8,128)S(1)} copy-done((f32[1024,64]{0,1:T(8,128)S(1)}, f32[1024,64]{0,1:T(8,128)}, u32[]{:S(2)}) %copy-start.2) | copy-done | bytes 262168
  3.6 0.0 copy-start.3
  3.6 0.7 copy-done.3
  4.3 0.0 copy-start.4
  4.3 0.7 copy-done.4
  5.0 4.6 %shard_map.68 = (f32[1024,2048]{1,0:T(8,128)S(1)}, f32[1024,2048]{1,0:T(8,128)S(1)}, f32[16,128]{1,0:T(8,128)S(1)}, f32[32,128]{1,0:T(8,128)S(1)}) custom-call(f32[64,1024]{1,0:T(8,128)S(1)} %bitcast.13, f32[64,1024]{1,0:T(8,128)S(1)} %bitcast.12, f32[64,2048]{1,0:T(8,128)S(1)} %bitcast.10, f32[8,128]{1,0:T(8,128)S(1)} %bitcast.16, f32[16,128]{1,0:T(8,128)S(1)} %bitcast.15), custom_call_target="tpu_custom_call" | custom-call | flops 1073741824 | bytes 1048576 | tf_op jit(solution)/shard_map/pallas_call | solution.py:311
  9.6 3.1 %collective-permute-start = (f32[16,128]{1,0:T(8,128)S(1)}, f32[16,128]{1,0:T(8,128)S(1)}, u32[]{:S(2)}, u32[]{:S(2)}) collective-permute-start(f32[16,128]{1,0:T(8,128)S(1)} %get-tuple-element.12), channel_id=1, source_target_pairs={{0,1},{1,0},{2,3},{3,2},{4,5},{5,4},{6,7},{7,6},{8,9},{9,8},{10,11... | collective-permute-start | bytes 24584 | tf_op jit(solution)/shard_map/ppermute | solution.py:292
  12.7 1.6 %collective-permute-done = f32[16,128]{1,0:T(8,128)S(1)} collective-permute-done((f32[16,128]{1,0:T(8,128)S(1)}, f32[16,128]{1,0:T(8,128)S(1)}, u32[]{:S(2)}, u32[]{:S(2)}) %collective-permute-start) | collective-permute-done | bytes 8224 | tf_op jit(solution)/shard_map/ppermute | solution.py:292
  14.3 3.0 %collective-permute-start.1 = (f32[16,128]{1,0:T(8,128)S(1)}, f32[16,128]{1,0:T(8,128)S(1)}, u32[]{:S(2)}, u32[]{:S(2)}) collective-permute-start(f32[16,128]{1,0:T(8,128)S(1)} %add.51), channel_id=1, source_target_pairs={{0,2},{1,3},{2,0},{3,1},{4,6},{5,7},{6,4},{7,5},{8,10},{9,11},{10,... | collective-permute-start | bytes 24584 | tf_op jit(solution)/shard_map/ppermute | solution.py:292
  17.4 1.6 %collective-permute-done.1 = f32[16,128]{1,0:T(8,128)S(1)} collective-permute-done((f32[16,128]{1,0:T(8,128)S(1)}, f32[16,128]{1,0:T(8,128)S(1)}, u32[]{:S(2)}, u32[]{:S(2)}) %collective-permute-start.1) | collective-permute-done | bytes 8224 | tf_op jit(solution)/shard_map/ppermute | solution.py:292
  19.0 1.2 %shard_map.69 = f32[48,128]{1,0:T(8,128)S(1)} custom-call(f32[1024,2048]{1,0:T(8,128)S(1)} %get-tuple-element.10.plan_ref, f32[16,128]{1,0:T(8,128)S(1)} %add.52.rows_ref, f32[32,128]{1,0:T(8,128)S(1)} %get-tuple-element.13.cols_ref), custom_call_target="tpu_custom_call" | custom-call | flops 1073741824 | bytes 1048576 | tf_op jit(solution)/shard_map/pallas_call | solution.py:311
  20.2 0.1 collective-permute-start.2
  20.3 1.2 %collective-permute-done.2 = f32[48,128]{1,0:T(8,128)S(1)} collective-permute-done((f32[48,128]{1,0:T(8,128)S(1)}, f32[48,128]{1,0:T(8,128)S(1)}, u32[]{:S(2)}, u32[]{:S(2)}) %collective-permute-start.2) | collective-permute-done | bytes 24608 | tf_op jit(solution)/shard_map/ppermute | solution.py:292
  21.5 1.8 %collective-permute-start.3 = (f32[48,128]{1,0:T(8,128)S(1)}, f32[48,128]{1,0:T(8,128)S(1)}, u32[]{:S(2)}, u32[]{:S(2)}) collective-permute-start(f32[48,128]{1,0:T(8,128)S(1)} %add.53), channel_id=1, source_target_pairs={{0,8},{4,12},{8,0},{12,4},{16,24},{20,28},{24,16},{28,20},{1,9},{5... | collective-permute-start | bytes 73736 | tf_op jit(solution)/shard_map/ppermute | solution.py:292
  23.3 2.0 %collective-permute-done.3 = f32[48,128]{1,0:T(8,128)S(1)} collective-permute-done((f32[48,128]{1,0:T(8,128)S(1)}, f32[48,128]{1,0:T(8,128)S(1)}, u32[]{:S(2)}, u32[]{:S(2)}) %collective-permute-start.3) | collective-permute-done | bytes 24608 | tf_op jit(solution)/shard_map/ppermute | solution.py:292
  25.3 1.9 %collective-permute-start.4 = (f32[48,128]{1,0:T(8,128)S(1)}, f32[48,128]{1,0:T(8,128)S(1)}, u32[]{:S(2)}, u32[]{:S(2)}) collective-permute-start(f32[48,128]{1,0:T(8,128)S(1)} %add.54), channel_id=1, source_target_pairs={{0,16},{4,20},{8,24},{12,28},{16,0},{20,4},{24,8},{28,12},{1,17},{... | collective-permute-start | bytes 73736 | tf_op jit(solution)/shard_map/ppermute | solution.py:292
  27.2 2.0 %collective-permute-done.4 = f32[48,128]{1,0:T(8,128)S(1)} collective-permute-done((f32[48,128]{1,0:T(8,128)S(1)}, f32[48,128]{1,0:T(8,128)S(1)}, u32[]{:S(2)}, u32[]{:S(2)}) %collective-permute-start.4) | collective-permute-done | bytes 24608 | tf_op jit(solution)/shard_map/ppermute | solution.py:292
  29.1 2.0 %shard_map.70 = f32[16,128]{1,0:T(8,128)S(1)} custom-call(f32[1024,2048]{1,0:T(8,128)S(1)} %get-tuple-element.10.plan_ref, f32[48,128]{1,0:T(8,128)S(1)} %add.55.cols_ref), custom_call_target="tpu_custom_call" | custom-call | flops 1073741824 | bytes 1048576 | tf_op jit(solution)/shard_map/pallas_call | solution.py:311
  31.2 2.0 %collective-permute-start.5 = (f32[16,128]{1,0:T(8,128)S(1)}, f32[16,128]{1,0:T(8,128)S(1)}, u32[]{:S(2)}, u32[]{:S(2)}) collective-permute-start(f32[16,128]{1,0:T(8,128)S(1)} %shard_map.70), channel_id=1, source_target_pairs={{0,1},{1,0},{2,3},{3,2},{4,5},{5,4},{6,7},{7,6},{8,9},{9,8},{10,11... | collective-permute-start | bytes 24584 | tf_op jit(solution)/shard_map/ppermute | solution.py:292
  33.1 1.7 %collective-permute-done.5 = f32[16,128]{1,0:T(8,128)S(1)} collective-permute-done((f32[16,128]{1,0:T(8,128)S(1)}, f32[16,128]{1,0:T(8,128)S(1)}, u32[]{:S(2)}, u32[]{:S(2)}) %collective-permute-start.5) | collective-permute-done | bytes 8224 | tf_op jit(solution)/shard_map/ppermute | solution.py:292
  34.9 2.9 %collective-permute-start.6 = (f32[16,128]{1,0:T(8,128)S(1)}, f32[16,128]{1,0:T(8,128)S(1)}, u32[]{:S(2)}, u32[]{:S(2)}) collective-permute-start(f32[16,128]{1,0:T(8,128)S(1)} %add.56), channel_id=1, source_target_pairs={{0,2},{1,3},{2,0},{3,1},{4,6},{5,7},{6,4},{7,5},{8,10},{9,11},{10,... | collective-permute-start | bytes 24584 | tf_op jit(solution)/shard_map/ppermute | solution.py:292
  37.8 1.6 %collective-permute-done.6 = f32[16,128]{1,0:T(8,128)S(1)} collective-permute-done((f32[16,128]{1,0:T(8,128)S(1)}, f32[16,128]{1,0:T(8,128)S(1)}, u32[]{:S(2)}, u32[]{:S(2)}) %collective-permute-start.6) | collective-permute-done | bytes 8224 | tf_op jit(solution)/shard_map/ppermute | solution.py:292
  39.4 2.3 %shard_map.71 = f32[32,128]{1,0:T(8,128)S(1)} custom-call(f32[1024,2048]{1,0:T(8,128)S(1)} %get-tuple-element.10.plan_ref, f32[16,128]{1,0:T(8,128)S(1)} %add.52.rows_ref, f32[16,128]{1,0:T(8,128)S(1)} %add.57.terms_ref), custom_call_target="tpu_custom_call" | custom-call | flops 1073741824 | bytes 1048576 | tf_op jit(solution)/shard_map/pallas_call | solution.py:311
  41.7 0.1 collective-permute-start.7
  41.8 1.2 %collective-permute-done.7 = f32[32,128]{1,0:T(8,128)S(1)} collective-permute-done((f32[32,128]{1,0:T(8,128)S(1)}, f32[32,128]{1,0:T(8,128)S(1)}, u32[]{:S(2)}, u32[]{:S(2)}) %collective-permute-start.7) | collective-permute-done | bytes 16416 | tf_op jit(solution)/shard_map/ppermute | solution.py:292
  43.0 1.8 %collective-permute-start.8 = (f32[32,128]{1,0:T(8,128)S(1)}, f32[32,128]{1,0:T(8,128)S(1)}, u32[]{:S(2)}, u32[]{:S(2)}) collective-permute-start(f32[32,128]{1,0:T(8,128)S(1)} %add.58), channel_id=1, source_target_pairs={{0,8},{4,12},{8,0},{12,4},{16,24},{20,28},{24,16},{28,20},{1,9},{5... | collective-permute-start | bytes 49160 | tf_op jit(solution)/shard_map/ppermute | solution.py:292
  44.8 1.9 %collective-permute-done.8 = f32[32,128]{1,0:T(8,128)S(1)} collective-permute-done((f32[32,128]{1,0:T(8,128)S(1)}, f32[32,128]{1,0:T(8,128)S(1)}, u32[]{:S(2)}, u32[]{:S(2)}) %collective-permute-start.8) | collective-permute-done | bytes 16416 | tf_op jit(solution)/shard_map/ppermute | solution.py:292
  46.7 1.9 %collective-permute-start.9 = (f32[32,128]{1,0:T(8,128)S(1)}, f32[32,128]{1,0:T(8,128)S(1)}, u32[]{:S(2)}, u32[]{:S(2)}) collective-permute-start(f32[32,128]{1,0:T(8,128)S(1)} %add.59), channel_id=1, source_target_pairs={{0,16},{4,20},{8,24},{12,28},{16,0},{20,4},{24,8},{28,12},{1,17},{... | collective-permute-start | bytes 49160 | tf_op jit(solution)/shard_map/ppermute | solution.py:292
  48.6 1.9 %collective-permute-done.9 = f32[32,128]{1,0:T(8,128)S(1)} collective-permute-done((f32[32,128]{1,0:T(8,128)S(1)}, f32[32,128]{1,0:T(8,128)S(1)}, u32[]{:S(2)}, u32[]{:S(2)}) %collective-permute-start.9) | collective-permute-done | bytes 16416 | tf_op jit(solution)/shard_map/ppermute | solution.py:292
  50.5 1.2 %shard_map.72 = f32[8,128]{1,0:T(8,128)S(1)} custom-call(f32[1024,2048]{1,0:T(8,128)S(1)} %get-tuple-element.10.plan_ref, f32[48,128]{1,0:T(8,128)S(1)} %add.55.cols_ref, f32[32,128]{1,0:T(8,128)S(1)} %add.60.terms_ref.bterms_ref), custom_call_target="tpu_custom_call" | custom-call | flops 1073741824 | bytes 1048576 | tf_op jit(solution)/shard_map/pallas_call | solution.py:311
  51.7 2.0 %collective-permute-start.10 = (f32[8,128]{1,0:T(8,128)S(1)}, f32[8,128]{1,0:T(8,128)S(1)}, u32[]{:S(2)}, u32[]{:S(2)}) collective-permute-start(f32[8,128]{1,0:T(8,128)S(1)} %shard_map.72), channel_id=1, source_target_pairs={{0,1},{1,0},{2,3},{3,2},{4,5},{5,4},{6,7},{7,6},{8,9},{9,8},{10,11... | collective-permute-start | bytes 12296 | tf_op jit(solution)/shard_map/ppermute | solution.py:292
  53.7 1.7 %collective-permute-done.10 = f32[8,128]{1,0:T(8,128)S(1)} collective-permute-done((f32[8,128]{1,0:T(8,128)S(1)}, f32[8,128]{1,0:T(8,128)S(1)}, u32[]{:S(2)}, u32[]{:S(2)}) %collective-permute-start.10) | collective-permute-done | bytes 4128 | tf_op jit(solution)/shard_map/ppermute | solution.py:292
  55.4 2.9 %collective-permute-start.11 = (f32[8,128]{1,0:T(8,128)S(1)}, f32[8,128]{1,0:T(8,128)S(1)}, u32[]{:S(2)}, u32[]{:S(2)}) collective-permute-start(f32[8,128]{1,0:T(8,128)S(1)} %add.61), channel_id=1, source_target_pairs={{0,2},{1,3},{2,0},{3,1},{4,6},{5,7},{6,4},{7,5},{8,10},{9,11},{10,... | collective-permute-start | bytes 12296 | tf_op jit(solution)/shard_map/ppermute | solution.py:292
  58.3 1.6 %collective-permute-done.11 = f32[8,128]{1,0:T(8,128)S(1)} collective-permute-done((f32[8,128]{1,0:T(8,128)S(1)}, f32[8,128]{1,0:T(8,128)S(1)}, u32[]{:S(2)}, u32[]{:S(2)}) %collective-permute-start.11) | collective-permute-done | bytes 4128 | tf_op jit(solution)/shard_map/ppermute | solution.py:292
  59.9 3.1 %shard_map.73 = (f32[2,64,256]{2,1,0:T(8,128)S(1)}, f32[2,64,256]{2,1,0:T(8,128)S(1)}, f32[1024,128]{1,0:T(8,128)S(1)}, f32[8,2048]{1,0:T(8,128)S(1)}) custom-call(f32[1024,2048]{1,0:T(8,128)S(1)} %get-tuple-element.10.plan_ref, f32[1024,2048]{1,0:T(8,128)S(1)} %get-tuple-element.11.cot_ref, f32[64,2048]{1,0:T(8,128)S(1)} %bitcast.11, ...), custom_call_target="tpu_custom_call" | custom-call | flops 1073741824 | bytes 1048576 | tf_op jit(solution)/shard_map/pallas_call | solution.py:311
  63.0 2.4 %shard_map.75 = f32[8,64,256]{2,1,0:T(8,128)S(1)} custom-call(f32[1024,2048]{1,0:T(8,128)S(1)} %get-tuple-element.10.plan_ref, f32[1024,2048]{1,0:T(8,128)S(1)} %get-tuple-element.11.cot_ref, f32[64,1024]{1,0:T(8,128)S(1)} %bitcast.14, f32[1024,128]{1,0:T(8,128)S(1)} %get-tuple-element.16.spread_ref, f32[8,2048]{1,0:T(8,128)S(1)} %get-tuple-element.17.beta_ref), custom_call_target="tpu_custom_call" | custom-call | flops 8589934592 | bytes 1048576 | tf_op jit(solution)/shard_map/pallas_call | solution.py:311
  65.4 0.1 collective-permute-start.15
  65.5 2.0 %collective-permute-start.12 = (f32[2,64,256]{2,1,0:T(8,128)S(1)}, f32[2,64,256]{2,1,0:T(8,128)S(1)}, u32[]{:S(2)}, u32[]{:S(2)}) collective-permute-start(f32[2,64,256]{2,1,0:T(8,128)S(1)} %get-tuple-element.15), channel_id=1, source_target_pairs={{0,1},{1,0},{2,3},{3,2},{4,5},{5,4},{6,7},{7,6},{8,9},{9,8},{10,11... | collective-permute-start | bytes 393224 | tf_op jit(solution)/shard_map/ppermute | solution.py:292
  67.4 4.1 %collective-permute-done.12 = f32[2,64,256]{2,1,0:T(8,128)S(1)} collective-permute-done((f32[2,64,256]{2,1,0:T(8,128)S(1)}, f32[2,64,256]{2,1,0:T(8,128)S(1)}, u32[]{:S(2)}, u32[]{:S(2)}) %collective-permute-start.12) | collective-permute-done | bytes 131104 | tf_op jit(solution)/shard_map/ppermute | solution.py:292
  71.5 2.8 %collective-permute-start.13 = (f32[2,64,256]{2,1,0:T(8,128)S(1)}, f32[2,64,256]{2,1,0:T(8,128)S(1)}, u32[]{:S(2)}, u32[]{:S(2)}) collective-permute-start(f32[2,64,256]{2,1,0:T(8,128)S(1)} %add.63), channel_id=1, source_target_pairs={{0,2},{1,3},{2,0},{3,1},{4,6},{5,7},{6,4},{7,5},{8,10},{9,11},{10,... | collective-permute-start | bytes 393224 | tf_op jit(solution)/shard_map/ppermute | solution.py:292
  74.4 0.0 collective-permute-done.15
  74.4 1.6 %collective-permute-start.16 = (f32[2,64,256]{2,1,0:T(8,128)S(1)}, f32[2,64,256]{2,1,0:T(8,128)S(1)}, u32[]{:S(2)}, u32[]{:S(2)}) collective-permute-start(f32[2,64,256]{2,1,0:T(8,128)S(1)} %slice.27), channel_id=1, source_target_pairs={{0,8},{4,12},{8,0},{12,4},{16,24},{20,28},{24,16},{28,20},{1,9},{5... | collective-permute-start | bytes 393224 | tf_op jit(solution)/shard_map/ppermute | solution.py:292
  76.0 4.5 %collective-permute-done.13 = f32[2,64,256]{2,1,0:T(8,128)S(1)} collective-permute-done((f32[2,64,256]{2,1,0:T(8,128)S(1)}, f32[2,64,256]{2,1,0:T(8,128)S(1)}, u32[]{:S(2)}, u32[]{:S(2)}) %collective-permute-start.13) | collective-permute-done | bytes 131104 | tf_op jit(solution)/shard_map/ppermute | solution.py:292
  80.5 0.7 collective-permute-start.14
  81.2 0.0 collective-permute-done.16
  81.3 1.6 %collective-permute-start.17 = (f32[1,64,256]{2,1,0:T(8,128)S(1)}, f32[1,64,256]{2,1,0:T(8,128)S(1)}, u32[]{:S(2)}, u32[]{:S(2)}) collective-permute-start(f32[1,64,256]{2,1,0:T(8,128)S(1)} %slice.29), channel_id=1, source_target_pairs={{0,16},{4,20},{8,24},{12,28},{16,0},{20,4},{24,8},{28,12},{1,17},{... | collective-permute-start | bytes 196616 | tf_op jit(solution)/shard_map/ppermute | solution.py:292
  82.8 2.7 %collective-permute-done.14 = f32[2,64,256]{2,1,0:T(8,128)S(1)} collective-permute-done((f32[2,64,256]{2,1,0:T(8,128)S(1)}, f32[2,64,256]{2,1,0:T(8,128)S(1)}, u32[]{:S(2)}, u32[]{:S(2)}) %collective-permute-start.14) | collective-permute-done | bytes 131104 | tf_op jit(solution)/shard_map/ppermute | solution.py:292
  85.5 0.7 shard_map.74
  86.3 0.0 collective-permute-done.17
  86.3 0.6 fusion
  (20 shorter events, 0.2 us)
Async XLA Ops:
  0.6 1.0 %copy-start = (f32[2048,64]{0,1:T(8,128)S(1)}, f32[2048,64]{0,1:T(8,128)}, u32[]{:S(2)}) copy-start(f32[2048,64]{0,1:T(8,128)} %param.6) | copy-start | bytes 1572868
  1.7 0.9 %copy-start.1 = (f32[1024,64]{0,1:T(8,128)S(1)}, f32[1024,64]{0,1:T(8,128)}, u32[]{:S(2)}) copy-start(f32[1024,64]{0,1:T(8,128)} %param.9) | copy-start | bytes 786436
  2.6 0.9 %copy-start.2 = (f32[1024,64]{0,1:T(8,128)S(1)}, f32[1024,64]{0,1:T(8,128)}, u32[]{:S(2)}) copy-start(f32[1024,64]{0,1:T(8,128)} %param.5) | copy-start | bytes 786436
  3.6 0.7 copy-start.3
  4.3 0.7 copy-start.4
  9.6 4.7 %collective-permute-start = (f32[16,128]{1,0:T(8,128)S(1)}, f32[16,128]{1,0:T(8,128)S(1)}, u32[]{:S(2)}, u32[]{:S(2)}) collective-permute-start(f32[16,128]{1,0:T(8,128)S(1)} %get-tuple-element.12), channel_id=1, source_target_pairs={{0,1},{1,0},{2,3},{3,2},{4,5},{5,4},{6,7},{7,6},{8,9},{9,8},{10,11... | collective-permute-start | bytes 24584 | tf_op jit(solution)/shard_map/ppermute | solution.py:292
  14.3 4.7 %collective-permute-start.1 = (f32[16,128]{1,0:T(8,128)S(1)}, f32[16,128]{1,0:T(8,128)S(1)}, u32[]{:S(2)}, u32[]{:S(2)}) collective-permute-start(f32[16,128]{1,0:T(8,128)S(1)} %add.51), channel_id=1, source_target_pairs={{0,2},{1,3},{2,0},{3,1},{4,6},{5,7},{6,4},{7,5},{8,10},{9,11},{10,... | collective-permute-start | bytes 24584 | tf_op jit(solution)/shard_map/ppermute | solution.py:292
  20.2 1.3 %collective-permute-start.2 = (f32[48,128]{1,0:T(8,128)S(1)}, f32[48,128]{1,0:T(8,128)S(1)}, u32[]{:S(2)}, u32[]{:S(2)}) collective-permute-start(f32[48,128]{1,0:T(8,128)S(1)} %shard_map.69), channel_id=1, source_target_pairs={{0,4},{4,0},{8,12},{12,8},{16,20},{20,16},{24,28},{28,24},{1,5},{5... | collective-permute-start | bytes 73736 | tf_op jit(solution)/shard_map/ppermute | solution.py:292
  21.5 3.8 %collective-permute-start.3 = (f32[48,128]{1,0:T(8,128)S(1)}, f32[48,128]{1,0:T(8,128)S(1)}, u32[]{:S(2)}, u32[]{:S(2)}) collective-permute-start(f32[48,128]{1,0:T(8,128)S(1)} %add.53), channel_id=1, source_target_pairs={{0,8},{4,12},{8,0},{12,4},{16,24},{20,28},{24,16},{28,20},{1,9},{5... | collective-permute-start | bytes 73736 | tf_op jit(solution)/shard_map/ppermute | solution.py:292
  25.3 3.8 %collective-permute-start.4 = (f32[48,128]{1,0:T(8,128)S(1)}, f32[48,128]{1,0:T(8,128)S(1)}, u32[]{:S(2)}, u32[]{:S(2)}) collective-permute-start(f32[48,128]{1,0:T(8,128)S(1)} %add.54), channel_id=1, source_target_pairs={{0,16},{4,20},{8,24},{12,28},{16,0},{20,4},{24,8},{28,12},{1,17},{... | collective-permute-start | bytes 73736 | tf_op jit(solution)/shard_map/ppermute | solution.py:292
  31.2 3.7 %collective-permute-start.5 = (f32[16,128]{1,0:T(8,128)S(1)}, f32[16,128]{1,0:T(8,128)S(1)}, u32[]{:S(2)}, u32[]{:S(2)}) collective-permute-start(f32[16,128]{1,0:T(8,128)S(1)} %shard_map.70), channel_id=1, source_target_pairs={{0,1},{1,0},{2,3},{3,2},{4,5},{5,4},{6,7},{7,6},{8,9},{9,8},{10,11... | collective-permute-start | bytes 24584 | tf_op jit(solution)/shard_map/ppermute | solution.py:292
  34.9 4.5 %collective-permute-start.6 = (f32[16,128]{1,0:T(8,128)S(1)}, f32[16,128]{1,0:T(8,128)S(1)}, u32[]{:S(2)}, u32[]{:S(2)}) collective-permute-start(f32[16,128]{1,0:T(8,128)S(1)} %add.56), channel_id=1, source_target_pairs={{0,2},{1,3},{2,0},{3,1},{4,6},{5,7},{6,4},{7,5},{8,10},{9,11},{10,... | collective-permute-start | bytes 24584 | tf_op jit(solution)/shard_map/ppermute | solution.py:292
  41.7 1.2 %collective-permute-start.7 = (f32[32,128]{1,0:T(8,128)S(1)}, f32[32,128]{1,0:T(8,128)S(1)}, u32[]{:S(2)}, u32[]{:S(2)}) collective-permute-start(f32[32,128]{1,0:T(8,128)S(1)} %shard_map.71), channel_id=1, source_target_pairs={{0,4},{4,0},{8,12},{12,8},{16,20},{20,16},{24,28},{28,24},{1,5},{5... | collective-permute-start | bytes 49160 | tf_op jit(solution)/shard_map/ppermute | solution.py:292
  43.0 3.7 %collective-permute-start.8 = (f32[32,128]{1,0:T(8,128)S(1)}, f32[32,128]{1,0:T(8,128)S(1)}, u32[]{:S(2)}, u32[]{:S(2)}) collective-permute-start(f32[32,128]{1,0:T(8,128)S(1)} %add.58), channel_id=1, source_target_pairs={{0,8},{4,12},{8,0},{12,4},{16,24},{20,28},{24,16},{28,20},{1,9},{5... | collective-permute-start | bytes 49160 | tf_op jit(solution)/shard_map/ppermute | solution.py:292
  46.7 3.7 %collective-permute-start.9 = (f32[32,128]{1,0:T(8,128)S(1)}, f32[32,128]{1,0:T(8,128)S(1)}, u32[]{:S(2)}, u32[]{:S(2)}) collective-permute-start(f32[32,128]{1,0:T(8,128)S(1)} %add.59), channel_id=1, source_target_pairs={{0,16},{4,20},{8,24},{12,28},{16,0},{20,4},{24,8},{28,12},{1,17},{... | collective-permute-start | bytes 49160 | tf_op jit(solution)/shard_map/ppermute | solution.py:292
  51.7 3.7 %collective-permute-start.10 = (f32[8,128]{1,0:T(8,128)S(1)}, f32[8,128]{1,0:T(8,128)S(1)}, u32[]{:S(2)}, u32[]{:S(2)}) collective-permute-start(f32[8,128]{1,0:T(8,128)S(1)} %shard_map.72), channel_id=1, source_target_pairs={{0,1},{1,0},{2,3},{3,2},{4,5},{5,4},{6,7},{7,6},{8,9},{9,8},{10,11... | collective-permute-start | bytes 12296 | tf_op jit(solution)/shard_map/ppermute | solution.py:292
  55.4 4.5 %collective-permute-start.11 = (f32[8,128]{1,0:T(8,128)S(1)}, f32[8,128]{1,0:T(8,128)S(1)}, u32[]{:S(2)}, u32[]{:S(2)}) collective-permute-start(f32[8,128]{1,0:T(8,128)S(1)} %add.61), channel_id=1, source_target_pairs={{0,2},{1,3},{2,0},{3,1},{4,6},{5,7},{6,4},{7,5},{8,10},{9,11},{10,... | collective-permute-start | bytes 12296 | tf_op jit(solution)/shard_map/ppermute | solution.py:292
  65.4 9.0 %collective-permute-start.15 = (f32[4,64,256]{2,1,0:T(8,128)S(1)}, f32[4,64,256]{2,1,0:T(8,128)S(1)}, u32[]{:S(2)}, u32[]{:S(2)}) collective-permute-start(f32[4,64,256]{2,1,0:T(8,128)S(1)} %slice.25), channel_id=1, source_target_pairs={{0,4},{4,0},{8,12},{12,8},{16,20},{20,16},{24,28},{28,24},{1,5},{5... | collective-permute-start | bytes 786440 | tf_op jit(solution)/shard_map/ppermute | solution.py:292
  65.5 6.1 %collective-permute-start.12 = (f32[2,64,256]{2,1,0:T(8,128)S(1)}, f32[2,64,256]{2,1,0:T(8,128)S(1)}, u32[]{:S(2)}, u32[]{:S(2)}) collective-permute-start(f32[2,64,256]{2,1,0:T(8,128)S(1)} %get-tuple-element.15), channel_id=1, source_target_pairs={{0,1},{1,0},{2,3},{3,2},{4,5},{5,4},{6,7},{7,6},{8,9},{9,8},{10,11... | collective-permute-start | bytes 393224 | tf_op jit(solution)/shard_map/ppermute | solution.py:292
  71.5 8.9 %collective-permute-start.13 = (f32[2,64,256]{2,1,0:T(8,128)S(1)}, f32[2,64,256]{2,1,0:T(8,128)S(1)}, u32[]{:S(2)}, u32[]{:S(2)}) collective-permute-start(f32[2,64,256]{2,1,0:T(8,128)S(1)} %add.63), channel_id=1, source_target_pairs={{0,2},{1,3},{2,0},{3,1},{4,6},{5,7},{6,4},{7,5},{8,10},{9,11},{10,... | collective-permute-start | bytes 393224 | tf_op jit(solution)/shard_map/ppermute | solution.py:292
  74.4 6.8 %collective-permute-start.16 = (f32[2,64,256]{2,1,0:T(8,128)S(1)}, f32[2,64,256]{2,1,0:T(8,128)S(1)}, u32[]{:S(2)}, u32[]{:S(2)}) collective-permute-start(f32[2,64,256]{2,1,0:T(8,128)S(1)} %slice.27), channel_id=1, source_target_pairs={{0,8},{4,12},{8,0},{12,4},{16,24},{20,28},{24,16},{28,20},{1,9},{5... | collective-permute-start | bytes 393224 | tf_op jit(solution)/shard_map/ppermute | solution.py:292
  80.5 5.0 %collective-permute-start.14 = (f32[2,64,256]{2,1,0:T(8,128)S(1)}, f32[2,64,256]{2,1,0:T(8,128)S(1)}, u32[]{:S(2)}, u32[]{:S(2)}) collective-permute-start(f32[2,64,256]{2,1,0:T(8,128)S(1)} %add.64), channel_id=1, source_target_pairs={{0,1},{1,0},{2,3},{3,2},{4,5},{5,4},{6,7},{7,6},{8,9},{9,8},{10,11... | collective-permute-start | bytes 393224 | tf_op jit(solution)/shard_map/ppermute | solution.py:292
  81.3 5.0 %collective-permute-start.17 = (f32[1,64,256]{2,1,0:T(8,128)S(1)}, f32[1,64,256]{2,1,0:T(8,128)S(1)}, u32[]{:S(2)}, u32[]{:S(2)}) collective-permute-start(f32[1,64,256]{2,1,0:T(8,128)S(1)} %slice.29), channel_id=1, source_target_pairs={{0,16},{4,20},{8,24},{12,28},{16,0},{20,4},{24,8},{28,12},{1,17},{... | collective-permute-start | bytes 196616 | tf_op jit(solution)/shard_map/ppermute | solution.py:292
where the time goes:
time: 87.2 us; the launch traced here: 86.9 us
  starting transfers between devices  32.2 us (37%)
  waiting for transfers between devices  31.3 us (36%)
  Pallas kernels  17.5 us (20%)
  local copies, waits for them, and re-layouts  4.35 us (5%)
    ppermute x18, starting transfers between devices, swap(): return lax.ppermute(value, axis, [(i, i ^ bit) for i in range(count)])  32.2 us
    ppermute x18, waiting for transfers between devices, swap(): return lax.ppermute(value, axis, [(i, i ^ bit) for i in range(count)])  31.3 us
    pallas_call x8, Pallas kernels, call(): pl.pallas_call(body, out_shape=outs, in_specs=specs, out_specs=jax.tree.m...  17.5 us
    unnamed x10, local copies, waits for them, and re-layouts  4.32 us
  transfers between devices with their start and end apart: 18, of which 15 were waited for; matrix products, arithmetic and copies ran while one was open for 0% of the time, Pallas kernels for 1%

commit v1 on v0

--- a/solution.py
+++ b/solution.py
@@ -72,9 +72,21 @@
     return jnp.concatenate([rows, jnp.zeros((56, dual.shape[1]), F32)], axis=0)
 
 
-def first_kernel(total, emb_ref, tgt_ref, cen_ref, pd_ref, cd_ref, plan_ref, cot_ref, rows_ref, cols_ref,
-                 lhs_ref, tlhs_ref, rhs_ref, rm_ref, rl_ref, cm_ref, cl_ref, pdual_ref, cdual_ref):
+def first_kernel(total, emb_hbm, tgt_hbm, cen_hbm, pd_hbm, cd_hbm, plan_ref, cot_ref, rows_ref, cols_ref,
+                 emb_ref, tgt_ref, cen_ref, pd_ref, cd_ref, sems, lhs_ref, tlhs_ref, rhs_ref, rm_ref, rl_ref, cm_ref, cl_ref, pdual_ref, cdual_ref):
     rows, cols = plan_ref.shape
+    copies = [
+        pltpu.make_async_copy(source, target, sems.at[k])
+        for k, (source, target) in enumerate(
+            [(cen_hbm, cen_ref), (cd_hbm, cd_ref), (emb_hbm, emb_ref), (pd_hbm, pd_ref), (tgt_hbm, tgt_ref)]
+        )
+    ]
+    for copy in copies:
+        copy.start()
+    cm_ref[...] = jnp.zeros_like(cm_ref)
+    cl_ref[...] = jnp.zeros_like(cl_ref)
+    for copy in copies:
+        copy.wait()
     flat_row(pd_ref[...], pdual_ref)
     flat_row(cd_ref[...] - math.log(total), cdual_ref)
     eh, el = (part.astype(F32) for part in split2(emb_ref[...] * (1.0 / EPSILON)))
@@ -85,8 +97,6 @@
     transpose_into(tlhs_ref, jnp.concatenate([tl, jnp.zeros_like(tl)], axis=0), LANES)
     ch, cl = split2(cen_ref[...])
     rhs_ref[...] = jnp.concatenate([ch, cl, ch, dual_rows(cdual_ref[...], False).astype(BF16)], axis=0)
-    cm_ref[...] = jnp.zeros_like(cm_ref)
-    cl_ref[...] = jnp.zeros_like(cl_ref)
     tm, tn = 128, 256
 
     @pl.loop(0, rows // tm)
@@ -281,20 +291,34 @@
             ]
 
 
-def last_kernel(gemb_ref, emb_ref):
-    chunks, _, span = gemb_ref.shape
-    me = lax.axis_index("cen") & (chunks // 2 - 1)
+def last_kernel(own_ref, got_ref, mine_ref, theirs_ref, emb_ref, cen_ref):
+    half, _, span = own_ref.shape
+    chunks = 2 * half
+    me = lax.axis_index("cen") & (half - 1)
     for q in range(chunks):
-        emb_ref[:, q * span : (q + 1) * span] = gemb_ref[reverse_bits(me ^ q, chunks)]
+        place = me ^ reverse_bits(q, chunks)
+        at = pl.ds(pl.multiple_of(place * span, span), span)
+        from_ref = own_ref if q < half else got_ref
+        emb_ref[:, at] = from_ref[q % half]
+    cen_ref[...] = mine_ref[...] + theirs_ref[...]
 
 
 def swap(value, axis, count, bit):
     return lax.ppermute(value, axis, [(i, i ^ bit) for i in range(count)])
 
 
-def sum_all(value, axis, count):
-    for bit in bits_of(count):
-        value = value + swap(value, axis, count, bit)
+def sum_all(value, axis, count, first):
+    bits = bits_of(count)
+    groups = [bits[:first]] + [bits[at : at + 2] for at in range(first, len(bits), 2)]
+    for group in groups:
+        if len(group) == 1:
+            value = value + swap(value, axis, count, group[0])
+        else:
+            one, two = group
+            near = swap(value, axis, count, one)
+            far = swap(value, axis, count, two)
+            both = swap(value, axis, count, one + two)
+            value = (value + near) + (far + both)
     return value
 
 
@@ -330,6 +354,12 @@
             pltpu.VMEM((2 * tiles, LANES), F32),
         ),
         [
+            pltpu.VMEM((width, rows), F32),
+            pltpu.VMEM((width, rows), F32),
+            pltpu.VMEM((width, cols), F32),
+            pltpu.VMEM((groups, LANES), F32),
+            pltpu.VMEM((tiles, LANES), F32),
+            pltpu.SemaphoreType.DMA((5,)),
             pltpu.VMEM((rows, 256), BF16),
             pltpu.VMEM((rows, 256), BF16),
             pltpu.VMEM((256, cols), BF16),
@@ -341,14 +371,14 @@
             pltpu.VMEM((1, cols), F32),
         ],
         24,
-        [VMEM] * 5,
+        [pl.BlockSpec(memory_space=pltpu.HBM)] * 5,
         emb,
         tgt,
         ctr,
         point_duals.reshape(groups, LANES),
         centroid_duals.reshape(tiles, LANES),
     )
-    row_sums = sum_all(row_sums, "cen", cen)
+    row_sums = sum_all(row_sums, "cen", cen, 2)
     col_all = call(
         second_kernel,
         pltpu.VMEM((3 * tiles, LANES), F32),
@@ -359,7 +389,7 @@
         row_sums,
         col_sums,
     )
-    col_all = sum_all(col_all, "pts", pts)
+    col_all = sum_all(col_all, "pts", pts, 1)
     row_terms = call(
         third_kernel,
         pltpu.VMEM((2 * groups, LANES), F32),
@@ -369,7 +399,7 @@
         plan,
         col_all,
     )
-    row_terms = sum_all(row_terms, "cen", cen)
+    row_terms = sum_all(row_terms, "cen", cen, 2)
     col_terms = call(
         fourth_kernel,
         pltpu.VMEM((2 * tiles, LANES), F32),
@@ -380,7 +410,7 @@
         row_sums,
         row_terms,
     )
-    col_terms = sum_all(col_terms, "pts", pts)
+    col_terms = sum_all(col_terms, "pts", pts, 1)
     last_terms = call(
         fifth_kernel,
         pltpu.VMEM((groups, LANES), F32),
@@ -391,7 +421,7 @@
         col_all,
         col_terms,
     )
-    last_terms = sum_all(last_terms, "cen", cen)
+    last_terms = sum_all(last_terms, "cen", cen, 2)
     gemb, sent, spread, beta = call(
         emb_kernel,
         (
@@ -431,13 +461,25 @@
         keep = gemb.shape[0] // 2
         gemb = gemb[:keep] + swap(gemb[keep:], "cen", cen, bit)
     gemb = gemb + swap(gemb, "cen", cen, cbits[-1])
-    for bit in reversed(cbits[:-1]):
+    for bit in reversed(cbits[1:-1]):
         gemb = jnp.concatenate([gemb, swap(gemb, "cen", cen, bit)], axis=0)
-    for bit in pbits:
+    got = swap(gemb, "cen", cen, cbits[0])
+    for bit in pbits[:-1]:
         keep = gcen.shape[0] // 2
         gcen = gcen[:keep] + swap(gcen[keep:], "pts", pts, bit)
-    grad_emb = call(last_kernel, sds((width, rows), F32), [], 6, [VMEM], gemb)
-    return grad_emb.T, gcen[0].T
+    theirs = swap(gcen[1], "pts", pts, pbits[-1])
+    grad_emb, grad_cen = call(
+        last_kernel,
+        (sds((width, rows), F32), sds((width, cols // pts), F32)),
+        [],
+        6,
+        [VMEM] * 4,
+        gemb,
+        got,
+        gcen[0],
+        theirs,
+    )
+    return grad_emb.T, grad_cen.T
 
 
 def solution(mesh):

time: 87.2 us -> 81.7 us (0.937)
  starting transfers between devices: 32.2 us -> 24.3 us
  waiting for transfers between devices: 31.3 us -> 34 us
    ppermute x18 -> x23, starting transfers between devices: 32.2 us -> 24.3 us  [swap(): return lax.ppermute(value, axis, [(i, i ^ bit) for i in range(count)])]
    ppermute x18 -> x23, waiting for transfers between devices: 31.3 us -> 34 us  [swap(): return lax.ppermute(value, axis, [(i, i ^ bit) for i in range(count)])]
  transfers between devices with their start and end apart: 18 -> 23, of which waited for: 15 -> 16; matrix products, arithmetic and copies ran while one was open for 0% -> 0% of each run, Pallas kernels for 1% -> 0%
where the time goes in v1:
time: 81.7 us; the launch traced here: 81.4 us
  waiting for transfers between devices  34 us (42%)
  starting transfers between devices  24.3 us (30%)
  Pallas kernels  17.8 us (22%)
  local copies, waits for them, and re-layouts  4.36 us (5%)
    ppermute x23, waiting for transfers between devices, swap(): return lax.ppermute(value, axis, [(i, i ^ bit) for i in range(count)])  34 us
    ppermute x23, starting transfers between devices, swap(): return lax.ppermute(value, axis, [(i, i ^ bit) for i in range(count)])  24.3 us
    pallas_call x8, Pallas kernels, call(): pl.pallas_call(body, out_shape=outs, in_specs=specs, out_specs=jax.tree.m...  17.8 us
    unnamed x10, local copies, waits for them, and re-layouts  4.32 us
  transfers between devices with their start and end apart: 23, of which 16 were waited for; matrix products, arithmetic and copies ran while one was open for 0% of the time, Pallas kernels for 0%

profile of v1, /device:TPU:0, one launch (start us, length us, event | category | flops | bytes accessed | tf_op | source)
XLA Modules:
  0.0 81.4 jit_solution(11431837319989430741)
XLA Ops:
  0.6 0.0 copy-start
  0.6 1.0 %copy-done = f32[2048,64]{0,1:T(8,128)S(1)} copy-done((f32[2048,64]{0,1:T(8,128)S(1)}, f32[2048,64]{0,1:T(8,128)}, u32[]{:S(2)}) %copy-start) | copy-done | bytes 524312
  1.7 0.0 copy-start.1
  1.7 0.9 %copy-done.1 = f32[1024,64]{0,1:T(8,128)S(1)} copy-done((f32[1024,64]{0,1:T(8,128)S(1)}, f32[1024,64]{0,1:T(8,128)}, u32[]{:S(2)}) %copy-start.1) | copy-done | bytes 262168
  2.6 0.0 copy-start.2
  2.6 0.9 %copy-done.2 = f32[1024,64]{0,1:T(8,128)S(1)} copy-done((f32[1024,64]{0,1:T(8,128)S(1)}, f32[1024,64]{0,1:T(8,128)}, u32[]{:S(2)}) %copy-start.2) | copy-done | bytes 262168
  3.6 0.0 copy-start.3
  3.6 0.7 copy-done.3
  4.3 0.0 copy-start.4
  4.3 0.7 copy-done.4
  5.0 4.8 %shard_map.68 = (f32[1024,2048]{1,0:T(8,128)S(1)}, f32[1024,2048]{1,0:T(8,128)S(1)}, f32[16,128]{1,0:T(8,128)S(1)}, f32[32,128]{1,0:T(8,128)S(1)}) custom-call(f32[64,1024]{1,0:T(8,128)S(1)} %bitcast.14, f32[64,1024]{1,0:T(8,128)S(1)} %bitcast.13, f32[64,2048]{1,0:T(8,128)S(1)} %bitcast.11, f32[8,128]{1,0:T(8,128)S(1)} %bitcast.17, f32[16,128]{1,0:T(8,128)S(1)} %bitcast.16), custom_call_target="tpu_custom_call" | custom-call | flops 1073741824 | bytes 1048576 | tf_op jit(solution)/shard_map/pallas_call | solution.py:335
  9.8 4.1 %collective-permute-start.1 = (f32[16,128]{1,0:T(8,128)S(1)}, f32[16,128]{1,0:T(8,128)S(1)}, u32[]{:S(2)}, u32[]{:S(2)}) collective-permute-start(f32[16,128]{1,0:T(8,128)S(1)} %get-tuple-element.14), channel_id=1, source_target_pairs={{0,2},{1,3},{2,0},{3,1},{4,6},{5,7},{6,4},{7,5},{8,10},{9,11},{10,... | collective-permute-start | bytes 24584 | tf_op jit(solution)/shard_map/ppermute | solution.py:307
  13.9 1.4 %collective-permute-start.2 = (f32[16,128]{1,0:T(8,128)S(1)}, f32[16,128]{1,0:T(8,128)S(1)}, u32[]{:S(2)}, u32[]{:S(2)}) collective-permute-start(f32[16,128]{1,0:T(8,128)S(1)} %get-tuple-element.14), channel_id=1, source_target_pairs={{0,3},{1,2},{2,1},{3,0},{4,7},{5,6},{6,5},{7,4},{8,11},{9,10},{10,... | collective-permute-start | bytes 24584 | tf_op jit(solution)/shard_map/ppermute | solution.py:307
  15.3 0.2 collective-permute-start
  15.5 0.1 collective-permute-done.1
  15.6 3.8 %collective-permute-done.2 = f32[16,128]{1,0:T(8,128)S(1)} collective-permute-done((f32[16,128]{1,0:T(8,128)S(1)}, f32[16,128]{1,0:T(8,128)S(1)}, u32[]{:S(2)}, u32[]{:S(2)}) %collective-permute-start.2) | collective-permute-done | bytes 8224 | tf_op jit(solution)/shard_map/ppermute | solution.py:307
  19.4 0.0 collective-permute-done
  19.4 1.2 %shard_map.69 = f32[48,128]{1,0:T(8,128)S(1)} custom-call(f32[1024,2048]{1,0:T(8,128)S(1)} %get-tuple-element.12.plan_ref, f32[16,128]{1,0:T(8,128)S(1)} %add_add_fusion.3.rows_ref, f32[32,128]{1,0:T(8,128)S(1)} %get-tuple-element.15.cols_ref), custom_call_target="tpu_custom_call" | custom-call | flops 1073741824 | bytes 1048576 | tf_op jit(solution)/shard_map/pallas_call | solution.py:335
  20.6 0.1 collective-permute-start.3
  20.7 1.2 %collective-permute-done.3 = f32[48,128]{1,0:T(8,128)S(1)} collective-permute-done((f32[48,128]{1,0:T(8,128)S(1)}, f32[48,128]{1,0:T(8,128)S(1)}, u32[]{:S(2)}, u32[]{:S(2)}) %collective-permute-start.3) | collective-permute-done | bytes 24608 | tf_op jit(solution)/shard_map/ppermute | solution.py:307
  21.9 1.5 %collective-permute-start.5 = (f32[48,128]{1,0:T(8,128)S(1)}, f32[48,128]{1,0:T(8,128)S(1)}, u32[]{:S(2)}, u32[]{:S(2)}) collective-permute-start(f32[48,128]{1,0:T(8,128)S(1)} %add.66), channel_id=1, source_target_pairs={{0,16},{4,20},{8,24},{12,28},{16,0},{20,4},{24,8},{28,12},{1,17},{... | collective-permute-start | bytes 73736 | tf_op jit(solution)/shard_map/ppermute | solution.py:307
  23.4 1.4 %collective-permute-start.6 = (f32[48,128]{1,0:T(8,128)S(1)}, f32[48,128]{1,0:T(8,128)S(1)}, u32[]{:S(2)}, u32[]{:S(2)}) collective-permute-start(f32[48,128]{1,0:T(8,128)S(1)} %add.66), channel_id=1, source_target_pairs={{0,24},{4,28},{8,16},{12,20},{16,8},{20,12},{24,0},{28,4},{1,25},{... | collective-permute-start | bytes 73736 | tf_op jit(solution)/shard_map/ppermute | solution.py:307
  24.8 0.5 collective-permute-start.4
  25.4 0.3 collective-permute-done.5
  25.7 2.6 %collective-permute-done.6 = f32[48,128]{1,0:T(8,128)S(1)} collective-permute-done((f32[48,128]{1,0:T(8,128)S(1)}, f32[48,128]{1,0:T(8,128)S(1)}, u32[]{:S(2)}, u32[]{:S(2)}) %collective-permute-start.6) | collective-permute-done | bytes 24608 | tf_op jit(solution)/shard_map/ppermute | solution.py:307
  28.3 0.4 collective-permute-done.4
  28.7 2.0 %shard_map.70 = f32[16,128]{1,0:T(8,128)S(1)} custom-call(f32[1024,2048]{1,0:T(8,128)S(1)} %get-tuple-element.12.plan_ref, f32[48,128]{1,0:T(8,128)S(1)} %add_add_fusion.cols_ref), custom_call_target="tpu_custom_call" | custom-call | flops 1073741824 | bytes 1048576 | tf_op jit(solution)/shard_map/pallas_call | solution.py:335
  30.7 1.3 %collective-permute-start.8 = (f32[16,128]{1,0:T(8,128)S(1)}, f32[16,128]{1,0:T(8,128)S(1)}, u32[]{:S(2)}, u32[]{:S(2)}) collective-permute-start(f32[16,128]{1,0:T(8,128)S(1)} %shard_map.70), channel_id=1, source_target_pairs={{0,2},{1,3},{2,0},{3,1},{4,6},{5,7},{6,4},{7,5},{8,10},{9,11},{10,... | collective-permute-start | bytes 24584 | tf_op jit(solution)/shard_map/ppermute | solution.py:307
  32.0 0.9 %collective-permute-start.9 = (f32[16,128]{1,0:T(8,128)S(1)}, f32[16,128]{1,0:T(8,128)S(1)}, u32[]{:S(2)}, u32[]{:S(2)}) collective-permute-start(f32[16,128]{1,0:T(8,128)S(1)} %shard_map.70), channel_id=1, source_target_pairs={{0,3},{1,2},{2,1},{3,0},{4,7},{5,6},{6,5},{7,4},{8,11},{9,10},{10,... | collective-permute-start | bytes 24584 | tf_op jit(solution)/shard_map/ppermute | solution.py:307
  32.9 1.3 %collective-permute-start.7 = (f32[16,128]{1,0:T(8,128)S(1)}, f32[16,128]{1,0:T(8,128)S(1)}, u32[]{:S(2)}, u32[]{:S(2)}) collective-permute-start(f32[16,128]{1,0:T(8,128)S(1)} %shard_map.70), channel_id=1, source_target_pairs={{0,1},{1,0},{2,3},{3,2},{4,5},{5,4},{6,7},{7,6},{8,9},{9,8},{10,11... | collective-permute-start | bytes 24584 | tf_op jit(solution)/shard_map/ppermute | solution.py:307
  34.2 1.1 %collective-permute-done.8 = f32[16,128]{1,0:T(8,128)S(1)} collective-permute-done((f32[16,128]{1,0:T(8,128)S(1)}, f32[16,128]{1,0:T(8,128)S(1)}, u32[]{:S(2)}, u32[]{:S(2)}) %collective-permute-start.8) | collective-permute-done | bytes 8224 | tf_op jit(solution)/shard_map/ppermute | solution.py:307
  35.3 2.1 %collective-permute-done.9 = f32[16,128]{1,0:T(8,128)S(1)} collective-permute-done((f32[16,128]{1,0:T(8,128)S(1)}, f32[16,128]{1,0:T(8,128)S(1)}, u32[]{:S(2)}, u32[]{:S(2)}) %collective-permute-start.9) | collective-permute-done | bytes 8224 | tf_op jit(solution)/shard_map/ppermute | solution.py:307
  37.4 0.0 collective-permute-done.7
  37.4 2.3 %shard_map.71 = f32[32,128]{1,0:T(8,128)S(1)} custom-call(f32[1024,2048]{1,0:T(8,128)S(1)} %get-tuple-element.12.plan_ref, f32[16,128]{1,0:T(8,128)S(1)} %add_add_fusion.3.rows_ref, f32[16,128]{1,0:T(8,128)S(1)} %add_add_fusion.2.terms_ref), custom_call_target="tpu_custom_call" | custom-call | flops 1073741824 | bytes 1048576 | tf_op jit(solution)/shard_map/pallas_call | solution.py:335
  39.7 0.1 collective-permute-start.10
  39.8 1.2 %collective-permute-done.10 = f32[32,128]{1,0:T(8,128)S(1)} collective-permute-done((f32[32,128]{1,0:T(8,128)S(1)}, f32[32,128]{1,0:T(8,128)S(1)}, u32[]{:S(2)}, u32[]{:S(2)}) %collective-permute-start.10) | collective-permute-done | bytes 16416 | tf_op jit(solution)/shard_map/ppermute | solution.py:307
  41.0 1.5 %collective-permute-start.12 = (f32[32,128]{1,0:T(8,128)S(1)}, f32[32,128]{1,0:T(8,128)S(1)}, u32[]{:S(2)}, u32[]{:S(2)}) collective-permute-start(f32[32,128]{1,0:T(8,128)S(1)} %add.73), channel_id=1, source_target_pairs={{0,16},{4,20},{8,24},{12,28},{16,0},{20,4},{24,8},{28,12},{1,17},{... | collective-permute-start | bytes 49160 | tf_op jit(solution)/shard_map/ppermute | solution.py:307
  42.5 0.9 %collective-permute-start.13 = (f32[32,128]{1,0:T(8,128)S(1)}, f32[32,128]{1,0:T(8,128)S(1)}, u32[]{:S(2)}, u32[]{:S(2)}) collective-permute-start(f32[32,128]{1,0:T(8,128)S(1)} %add.73), channel_id=1, source_target_pairs={{0,24},{4,28},{8,16},{12,20},{16,8},{20,12},{24,0},{28,4},{1,25},{... | collective-permute-start | bytes 49160 | tf_op jit(solution)/shard_map/ppermute | solution.py:307
  43.4 1.1 %collective-permute-start.11 = (f32[32,128]{1,0:T(8,128)S(1)}, f32[32,128]{1,0:T(8,128)S(1)}, u32[]{:S(2)}, u32[]{:S(2)}) collective-permute-start(f32[32,128]{1,0:T(8,128)S(1)} %add.73), channel_id=1, source_target_pairs={{0,8},{4,12},{8,0},{12,4},{16,24},{20,28},{24,16},{28,20},{1,9},{5... | collective-permute-start | bytes 49160 | tf_op jit(solution)/shard_map/ppermute | solution.py:307
  44.5 0.2 collective-permute-done.12
  44.7 2.4 %collective-permute-done.13 = f32[32,128]{1,0:T(8,128)S(1)} collective-permute-done((f32[32,128]{1,0:T(8,128)S(1)}, f32[32,128]{1,0:T(8,128)S(1)}, u32[]{:S(2)}, u32[]{:S(2)}) %collective-permute-start.13) | collective-permute-done | bytes 16416 | tf_op jit(solution)/shard_map/ppermute | solution.py:307
  47.1 0.0 collective-permute-done.11
  47.2 1.2 %shard_map.72 = f32[8,128]{1,0:T(8,128)S(1)} custom-call(f32[1024,2048]{1,0:T(8,128)S(1)} %get-tuple-element.12.plan_ref, f32[48,128]{1,0:T(8,128)S(1)} %add_add_fusion.cols_ref, f32[32,128]{1,0:T(8,128)S(1)} %add_add_fusion.1.terms_ref.bterms_ref), custom_call_target="tpu_custom_call" | custom-call | flops 1073741824 | bytes 1048576 | tf_op jit(solution)/shard_map/pallas_call | solution.py:335
  48.4 1.1 %collective-permute-start.15 = (f32[8,128]{1,0:T(8,128)S(1)}, f32[8,128]{1,0:T(8,128)S(1)}, u32[]{:S(2)}, u32[]{:S(2)}) collective-permute-start(f32[8,128]{1,0:T(8,128)S(1)} %shard_map.72), channel_id=1, source_target_pairs={{0,2},{1,3},{2,0},{3,1},{4,6},{5,7},{6,4},{7,5},{8,10},{9,11},{10,... | collective-permute-start | bytes 12296 | tf_op jit(solution)/shard_map/ppermute | solution.py:307
  49.5 1.8 %collective-permute-start.16 = (f32[8,128]{1,0:T(8,128)S(1)}, f32[8,128]{1,0:T(8,128)S(1)}, u32[]{:S(2)}, u32[]{:S(2)}) collective-permute-start(f32[8,128]{1,0:T(8,128)S(1)} %shard_map.72), channel_id=1, source_target_pairs={{0,3},{1,2},{2,1},{3,0},{4,7},{5,6},{6,5},{7,4},{8,11},{9,10},{10,... | collective-permute-start | bytes 12296 | tf_op jit(solution)/shard_map/ppermute | solution.py:307
  51.3 0.7 collective-permute-start.14
  52.0 1.0 %collective-permute-done.15 = f32[8,128]{1,0:T(8,128)S(1)} collective-permute-done((f32[8,128]{1,0:T(8,128)S(1)}, f32[8,128]{1,0:T(8,128)S(1)}, u32[]{:S(2)}, u32[]{:S(2)}) %collective-permute-start.15) | collective-permute-done | bytes 4128 | tf_op jit(solution)/shard_map/ppermute | solution.py:307
  53.0 1.9 %collective-permute-done.16 = f32[8,128]{1,0:T(8,128)S(1)} collective-permute-done((f32[8,128]{1,0:T(8,128)S(1)}, f32[8,128]{1,0:T(8,128)S(1)}, u32[]{:S(2)}, u32[]{:S(2)}) %collective-permute-start.16) | collective-permute-done | bytes 4128 | tf_op jit(solution)/shard_map/ppermute | solution.py:307
  54.9 0.0 collective-permute-done.14
  54.9 3.1 %shard_map.73 = (f32[2,64,256]{2,1,0:T(8,128)S(1)}, f32[2,64,256]{2,1,0:T(8,128)S(1)}, f32[1024,128]{1,0:T(8,128)S(1)}, f32[8,2048]{1,0:T(8,128)S(1)}) custom-call(f32[1024,2048]{1,0:T(8,128)S(1)} %get-tuple-element.12.plan_ref, f32[1024,2048]{1,0:T(8,128)S(1)} %get-tuple-element.13.cot_ref, f32[64,2048]{1,0:T(8,128)S(1)} %bitcast.12, ...), custom_call_target="tpu_custom_call" | custom-call | flops 1073741824 | bytes 1048576 | tf_op jit(solution)/shard_map/pallas_call | solution.py:335
  58.0 2.4 %shard_map.74 = f32[8,64,256]{2,1,0:T(8,128)S(1)} custom-call(f32[1024,2048]{1,0:T(8,128)S(1)} %get-tuple-element.12.plan_ref, f32[1024,2048]{1,0:T(8,128)S(1)} %get-tuple-element.13.cot_ref, f32[64,1024]{1,0:T(8,128)S(1)} %bitcast.15, f32[1024,128]{1,0:T(8,128)S(1)} %get-tuple-element.18.spread_ref, f32[8,2048]{1,0:T(8,128)S(1)} %get-tuple-element.19.beta_ref), custom_call_target="tpu_custom_call" | custom-call | flops 8589934592 | bytes 1048576 | tf_op jit(solution)/shard_map/pallas_call | solution.py:335
  60.5 0.1 collective-permute-start.20
  60.5 0.7 collective-permute-start.17
  61.2 5.2 %collective-permute-done.17 = f32[2,64,256]{2,1,0:T(8,128)S(1)} collective-permute-done((f32[2,64,256]{2,1,0:T(8,128)S(1)}, f32[2,64,256]{2,1,0:T(8,128)S(1)}, u32[]{:S(2)}, u32[]{:S(2)}) %collective-permute-start.17) | collective-permute-done | bytes 131104 | tf_op jit(solution)/shard_map/ppermute | solution.py:307
  66.4 1.3 %collective-permute-start.18 = (f32[2,64,256]{2,1,0:T(8,128)S(1)}, f32[2,64,256]{2,1,0:T(8,128)S(1)}, u32[]{:S(2)}, u32[]{:S(2)}) collective-permute-start(f32[2,64,256]{2,1,0:T(8,128)S(1)} %add.80), channel_id=1, source_target_pairs={{0,2},{1,3},{2,0},{3,1},{4,6},{5,7},{6,4},{7,5},{8,10},{9,11},{10,... | collective-permute-start | bytes 393224 | tf_op jit(solution)/shard_map/ppermute | solution.py:307
  67.7 0.0 collective-permute-done.20
  67.8 1.1 %collective-permute-start.21 = (f32[2,64,256]{2,1,0:T(8,128)S(1)}, f32[2,64,256]{2,1,0:T(8,128)S(1)}, u32[]{:S(2)}, u32[]{:S(2)}) collective-permute-start(f32[2,64,256]{2,1,0:T(8,128)S(1)} %slice.27), channel_id=1, source_target_pairs={{0,8},{4,12},{8,0},{12,4},{16,24},{20,28},{24,16},{28,20},{1,9},{5... | collective-permute-start | bytes 393224 | tf_op jit(solution)/shard_map/ppermute | solution.py:307
  68.9 6.3 %collective-permute-done.18 = f32[2,64,256]{2,1,0:T(8,128)S(1)} collective-permute-done((f32[2,64,256]{2,1,0:T(8,128)S(1)}, f32[2,64,256]{2,1,0:T(8,128)S(1)}, u32[]{:S(2)}, u32[]{:S(2)}) %collective-permute-start.18) | collective-permute-done | bytes 131104 | tf_op jit(solution)/shard_map/ppermute | solution.py:307
  75.2 0.1 collective-permute-start.19
  75.3 0.0 collective-permute-done.21
  75.4 1.2 %collective-permute-start.22 = (f32[64,256]{1,0:T(8,128)S(1)}, f32[64,256]{1,0:T(8,128)S(1)}, u32[]{:S(2)}, u32[]{:S(2)}) collective-permute-start(f32[64,256]{1,0:T(8,128)S(1)} %get-tuple-element.22), channel_id=1, source_target_pairs={{0,16},{4,20},{8,24},{12,28},{16,0},{20,4},{24,8},{28,12},{1,17},{... | collective-permute-start | bytes 196616 | tf_op jit(solution)/shard_map/ppermute | solution.py:307
  76.5 4.1 %collective-permute-done.19.got_ref = f32[2,64,256]{2,1,0:T(8,128)S(1)} collective-permute-done((f32[2,64,256]{2,1,0:T(8,128)S(1)}, f32[2,64,256]{2,1,0:T(8,128)S(1)}, u32[]{:S(2)}, u32[]{:S(2)}) %collective-permute-start.19) | collective-permute-done | bytes 131104 | tf_op jit(solution)/shard_map/ppermute | solution.py:307
  80.6 0.0 collective-permute-done.22.theirs_ref
  80.6 0.7 shard_map.75
  (14 shorter events, 0.2 us)
Async XLA Ops:
  0.6 1.0 %copy-start = (f32[2048,64]{0,1:T(8,128)S(1)}, f32[2048,64]{0,1:T(8,128)}, u32[]{:S(2)}) copy-start(f32[2048,64]{0,1:T(8,128)} %param.6) | copy-start | bytes 1572868
  1.7 0.9 %copy-start.1 = (f32[1024,64]{0,1:T(8,128)S(1)}, f32[1024,64]{0,1:T(8,128)}, u32[]{:S(2)}) copy-start(f32[1024,64]{0,1:T(8,128)} %param.9) | copy-start | bytes 786436
  2.6 0.9 %copy-start.2 = (f32[1024,64]{0,1:T(8,128)S(1)}, f32[1024,64]{0,1:T(8,128)}, u32[]{:S(2)}) copy-start(f32[1024,64]{0,1:T(8,128)} %param.5) | copy-start | bytes 786436
  3.6 0.7 copy-start.3
  4.3 0.7 copy-start.4
  9.8 5.8 %collective-permute-start.1 = (f32[16,128]{1,0:T(8,128)S(1)}, f32[16,128]{1,0:T(8,128)S(1)}, u32[]{:S(2)}, u32[]{:S(2)}) collective-permute-start(f32[16,128]{1,0:T(8,128)S(1)} %get-tuple-element.14), channel_id=1, source_target_pairs={{0,2},{1,3},{2,0},{3,1},{4,6},{5,7},{6,4},{7,5},{8,10},{9,11},{10,... | collective-permute-start | bytes 24584 | tf_op jit(solution)/shard_map/ppermute | solution.py:307
  13.9 5.4 %collective-permute-start.2 = (f32[16,128]{1,0:T(8,128)S(1)}, f32[16,128]{1,0:T(8,128)S(1)}, u32[]{:S(2)}, u32[]{:S(2)}) collective-permute-start(f32[16,128]{1,0:T(8,128)S(1)} %get-tuple-element.14), channel_id=1, source_target_pairs={{0,3},{1,2},{2,1},{3,0},{4,7},{5,6},{6,5},{7,4},{8,11},{9,10},{10,... | collective-permute-start | bytes 24584 | tf_op jit(solution)/shard_map/ppermute | solution.py:307
  15.3 4.1 %collective-permute-start = (f32[16,128]{1,0:T(8,128)S(1)}, f32[16,128]{1,0:T(8,128)S(1)}, u32[]{:S(2)}, u32[]{:S(2)}) collective-permute-start(f32[16,128]{1,0:T(8,128)S(1)} %get-tuple-element.14), channel_id=1, source_target_pairs={{0,1},{1,0},{2,3},{3,2},{4,5},{5,4},{6,7},{7,6},{8,9},{9,8},{10,11... | collective-permute-start | bytes 24584 | tf_op jit(solution)/shard_map/ppermute | solution.py:307
  20.6 1.3 %collective-permute-start.3 = (f32[48,128]{1,0:T(8,128)S(1)}, f32[48,128]{1,0:T(8,128)S(1)}, u32[]{:S(2)}, u32[]{:S(2)}) collective-permute-start(f32[48,128]{1,0:T(8,128)S(1)} %shard_map.69), channel_id=1, source_target_pairs={{0,4},{4,0},{8,12},{12,8},{16,20},{20,16},{24,28},{28,24},{1,5},{5... | collective-permute-start | bytes 73736 | tf_op jit(solution)/shard_map/ppermute | solution.py:307
  21.9 3.8 %collective-permute-start.5 = (f32[48,128]{1,0:T(8,128)S(1)}, f32[48,128]{1,0:T(8,128)S(1)}, u32[]{:S(2)}, u32[]{:S(2)}) collective-permute-start(f32[48,128]{1,0:T(8,128)S(1)} %add.66), channel_id=1, source_target_pairs={{0,16},{4,20},{8,24},{12,28},{16,0},{20,4},{24,8},{28,12},{1,17},{... | collective-permute-start | bytes 73736 | tf_op jit(solution)/shard_map/ppermute | solution.py:307
  23.4 4.9 %collective-permute-start.6 = (f32[48,128]{1,0:T(8,128)S(1)}, f32[48,128]{1,0:T(8,128)S(1)}, u32[]{:S(2)}, u32[]{:S(2)}) collective-permute-start(f32[48,128]{1,0:T(8,128)S(1)} %add.66), channel_id=1, source_target_pairs={{0,24},{4,28},{8,16},{12,20},{16,8},{20,12},{24,0},{28,4},{1,25},{... | collective-permute-start | bytes 73736 | tf_op jit(solution)/shard_map/ppermute | solution.py:307
  24.8 3.8 %collective-permute-start.4 = (f32[48,128]{1,0:T(8,128)S(1)}, f32[48,128]{1,0:T(8,128)S(1)}, u32[]{:S(2)}, u32[]{:S(2)}) collective-permute-start(f32[48,128]{1,0:T(8,128)S(1)} %add.66), channel_id=1, source_target_pairs={{0,8},{4,12},{8,0},{12,4},{16,24},{20,28},{24,16},{28,20},{1,9},{5... | collective-permute-start | bytes 73736 | tf_op jit(solution)/shard_map/ppermute | solution.py:307
  30.7 4.6 %collective-permute-start.8 = (f32[16,128]{1,0:T(8,128)S(1)}, f32[16,128]{1,0:T(8,128)S(1)}, u32[]{:S(2)}, u32[]{:S(2)}) collective-permute-start(f32[16,128]{1,0:T(8,128)S(1)} %shard_map.70), channel_id=1, source_target_pairs={{0,2},{1,3},{2,0},{3,1},{4,6},{5,7},{6,4},{7,5},{8,10},{9,11},{10,... | collective-permute-start | bytes 24584 | tf_op jit(solution)/shard_map/ppermute | solution.py:307
  32.0 5.4 %collective-permute-start.9 = (f32[16,128]{1,0:T(8,128)S(1)}, f32[16,128]{1,0:T(8,128)S(1)}, u32[]{:S(2)}, u32[]{:S(2)}) collective-permute-start(f32[16,128]{1,0:T(8,128)S(1)} %shard_map.70), channel_id=1, source_target_pairs={{0,3},{1,2},{2,1},{3,0},{4,7},{5,6},{6,5},{7,4},{8,11},{9,10},{10,... | collective-permute-start | bytes 24584 | tf_op jit(solution)/shard_map/ppermute | solution.py:307
  32.9 4.5 %collective-permute-start.7 = (f32[16,128]{1,0:T(8,128)S(1)}, f32[16,128]{1,0:T(8,128)S(1)}, u32[]{:S(2)}, u32[]{:S(2)}) collective-permute-start(f32[16,128]{1,0:T(8,128)S(1)} %shard_map.70), channel_id=1, source_target_pairs={{0,1},{1,0},{2,3},{3,2},{4,5},{5,4},{6,7},{7,6},{8,9},{9,8},{10,11... | collective-permute-start | bytes 24584 | tf_op jit(solution)/shard_map/ppermute | solution.py:307
  39.7 1.2 %collective-permute-start.10 = (f32[32,128]{1,0:T(8,128)S(1)}, f32[32,128]{1,0:T(8,128)S(1)}, u32[]{:S(2)}, u32[]{:S(2)}) collective-permute-start(f32[32,128]{1,0:T(8,128)S(1)} %shard_map.71), channel_id=1, source_target_pairs={{0,4},{4,0},{8,12},{12,8},{16,20},{20,16},{24,28},{28,24},{1,5},{5... | collective-permute-start | bytes 49160 | tf_op jit(solution)/shard_map/ppermute | solution.py:307
  41.0 3.7 %collective-permute-start.12 = (f32[32,128]{1,0:T(8,128)S(1)}, f32[32,128]{1,0:T(8,128)S(1)}, u32[]{:S(2)}, u32[]{:S(2)}) collective-permute-start(f32[32,128]{1,0:T(8,128)S(1)} %add.73), channel_id=1, source_target_pairs={{0,16},{4,20},{8,24},{12,28},{16,0},{20,4},{24,8},{28,12},{1,17},{... | collective-permute-start | bytes 49160 | tf_op jit(solution)/shard_map/ppermute | solution.py:307
  42.5 4.6 %collective-permute-start.13 = (f32[32,128]{1,0:T(8,128)S(1)}, f32[32,128]{1,0:T(8,128)S(1)}, u32[]{:S(2)}, u32[]{:S(2)}) collective-permute-start(f32[32,128]{1,0:T(8,128)S(1)} %add.73), channel_id=1, source_target_pairs={{0,24},{4,28},{8,16},{12,20},{16,8},{20,12},{24,0},{28,4},{1,25},{... | collective-permute-start | bytes 49160 | tf_op jit(solution)/shard_map/ppermute | solution.py:307
  43.4 3.7 %collective-permute-start.11 = (f32[32,128]{1,0:T(8,128)S(1)}, f32[32,128]{1,0:T(8,128)S(1)}, u32[]{:S(2)}, u32[]{:S(2)}) collective-permute-start(f32[32,128]{1,0:T(8,128)S(1)} %add.73), channel_id=1, source_target_pairs={{0,8},{4,12},{8,0},{12,4},{16,24},{20,28},{24,16},{28,20},{1,9},{5... | collective-permute-start | bytes 49160 | tf_op jit(solution)/shard_map/ppermute | solution.py:307
  48.4 4.6 %collective-permute-start.15 = (f32[8,128]{1,0:T(8,128)S(1)}, f32[8,128]{1,0:T(8,128)S(1)}, u32[]{:S(2)}, u32[]{:S(2)}) collective-permute-start(f32[8,128]{1,0:T(8,128)S(1)} %shard_map.72), channel_id=1, source_target_pairs={{0,2},{1,3},{2,0},{3,1},{4,6},{5,7},{6,4},{7,5},{8,10},{9,11},{10,... | collective-permute-start | bytes 12296 | tf_op jit(solution)/shard_map/ppermute | solution.py:307
  49.5 5.4 %collective-permute-start.16 = (f32[8,128]{1,0:T(8,128)S(1)}, f32[8,128]{1,0:T(8,128)S(1)}, u32[]{:S(2)}, u32[]{:S(2)}) collective-permute-start(f32[8,128]{1,0:T(8,128)S(1)} %shard_map.72), channel_id=1, source_target_pairs={{0,3},{1,2},{2,1},{3,0},{4,7},{5,6},{6,5},{7,4},{8,11},{9,10},{10,... | collective-permute-start | bytes 12296 | tf_op jit(solution)/shard_map/ppermute | solution.py:307
  51.3 3.6 %collective-permute-start.14 = (f32[8,128]{1,0:T(8,128)S(1)}, f32[8,128]{1,0:T(8,128)S(1)}, u32[]{:S(2)}, u32[]{:S(2)}) collective-permute-start(f32[8,128]{1,0:T(8,128)S(1)} %shard_map.72), channel_id=1, source_target_pairs={{0,1},{1,0},{2,3},{3,2},{4,5},{5,4},{6,7},{7,6},{8,9},{9,8},{10,11... | collective-permute-start | bytes 12296 | tf_op jit(solution)/shard_map/ppermute | solution.py:307
  60.5 7.3 %collective-permute-start.20 = (f32[4,64,256]{2,1,0:T(8,128)S(1)}, f32[4,64,256]{2,1,0:T(8,128)S(1)}, u32[]{:S(2)}, u32[]{:S(2)}) collective-permute-start(f32[4,64,256]{2,1,0:T(8,128)S(1)} %slice.25), channel_id=1, source_target_pairs={{0,4},{4,0},{8,12},{12,8},{16,20},{20,16},{24,28},{28,24},{1,5},{5... | collective-permute-start | bytes 786440 | tf_op jit(solution)/shard_map/ppermute | solution.py:307
  60.5 5.9 %collective-permute-start.17 = (f32[2,64,256]{2,1,0:T(8,128)S(1)}, f32[2,64,256]{2,1,0:T(8,128)S(1)}, u32[]{:S(2)}, u32[]{:S(2)}) collective-permute-start(f32[2,64,256]{2,1,0:T(8,128)S(1)} %get-tuple-element.17), channel_id=1, source_target_pairs={{0,1},{1,0},{2,3},{3,2},{4,5},{5,4},{6,7},{7,6},{8,9},{9,8},{10,11... | collective-permute-start | bytes 393224 | tf_op jit(solution)/shard_map/ppermute | solution.py:307
  66.4 8.7 %collective-permute-start.18 = (f32[2,64,256]{2,1,0:T(8,128)S(1)}, f32[2,64,256]{2,1,0:T(8,128)S(1)}, u32[]{:S(2)}, u32[]{:S(2)}) collective-permute-start(f32[2,64,256]{2,1,0:T(8,128)S(1)} %add.80), channel_id=1, source_target_pairs={{0,2},{1,3},{2,0},{3,1},{4,6},{5,7},{6,4},{7,5},{8,10},{9,11},{10,... | collective-permute-start | bytes 393224 | tf_op jit(solution)/shard_map/ppermute | solution.py:307
  67.8 7.5 %collective-permute-start.21 = (f32[2,64,256]{2,1,0:T(8,128)S(1)}, f32[2,64,256]{2,1,0:T(8,128)S(1)}, u32[]{:S(2)}, u32[]{:S(2)}) collective-permute-start(f32[2,64,256]{2,1,0:T(8,128)S(1)} %slice.27), channel_id=1, source_target_pairs={{0,8},{4,12},{8,0},{12,4},{16,24},{20,28},{24,16},{28,20},{1,9},{5... | collective-permute-start | bytes 393224 | tf_op jit(solution)/shard_map/ppermute | solution.py:307
  75.2 5.4 %collective-permute-start.19 = (f32[2,64,256]{2,1,0:T(8,128)S(1)}, f32[2,64,256]{2,1,0:T(8,128)S(1)}, u32[]{:S(2)}, u32[]{:S(2)}) collective-permute-start(f32[2,64,256]{2,1,0:T(8,128)S(1)} %add.81.own_ref), channel_id=1, source_target_pairs={{0,1},{1,0},{2,3},{3,2},{4,5},{5,4},{6,7},{7,6},{8,9},{9,8},{10,11... | collective-permute-start | bytes 393224 | tf_op jit(solution)/shard_map/ppermute | solution.py:307
  75.4 5.3 %collective-permute-start.22 = (f32[64,256]{1,0:T(8,128)S(1)}, f32[64,256]{1,0:T(8,128)S(1)}, u32[]{:S(2)}, u32[]{:S(2)}) collective-permute-start(f32[64,256]{1,0:T(8,128)S(1)} %get-tuple-element.22), channel_id=1, source_target_pairs={{0,16},{4,20},{8,24},{12,28},{16,0},{20,4},{24,8},{28,12},{1,17},{... | collective-permute-start | bytes 196616 | tf_op jit(solution)/shard_map/ppermute | solution.py:307

commit v2 on v1

--- a/solution.py
+++ b/solution.py
@@ -372,11 +372,10 @@
         ],
         24,
         [pl.BlockSpec(memory_space=pltpu.HBM)] * 5,
-        emb,
-        tgt,
-        ctr,
-        point_duals.reshape(groups, LANES),
-        centroid_duals.reshape(tiles, LANES),
+        *(
+            pltpu.with_memory_space_constraint(x, pltpu.HBM)
+            for x in (emb, tgt, ctr, point_duals.reshape(groups, LANES), centroid_duals.reshape(tiles, LANES))
+        ),
     )
     row_sums = sum_all(row_sums, "cen", cen, 2)
     col_all = call(

time: 81.7 us -> 78.5 us (0.961)
  local copies, waits for them, and re-layouts: 4.36 us -> 0.05 us
  Pallas kernels: 17.8 us -> 19.1 us
    unnamed x10 -> x4, local copies, waits for them, and re-layouts: 4.32 us -> 0.01 us
    pallas_call x8, Pallas kernels: 17.8 us -> 19.1 us  [call(): pl.pallas_call(body, out_shape=outs, in_specs=specs, out_specs=jax.tree.m...]
where the time goes in v2:
time: 78.5 us; the launch traced here: 78.3 us
  waiting for transfers between devices  33.9 us (43%)
  starting transfers between devices  24.3 us (31%)
  Pallas kernels  19.1 us (24%)
  between operations  0.81 us (1%)
    ppermute x23, waiting for transfers between devices, swap(): return lax.ppermute(value, axis, [(i, i ^ bit) for i in range(count)])  33.9 us
    ppermute x23, starting transfers between devices, swap(): return lax.ppermute(value, axis, [(i, i ^ bit) for i in range(count)])  24.3 us
    pallas_call x8, Pallas kernels, call(): pl.pallas_call(body, out_shape=outs, in_specs=specs, out_specs=jax.tree.m...  19.1 us
  transfers between devices with their start and end apart: 23, of which 16 were waited for; matrix products, arithmetic and copies ran while one was open for 0% of the time, Pallas kernels for 0%

profile of v2, /device:TPU:0, one launch (start us, length us, event | category | flops | bytes accessed | tf_op | source)
XLA Modules:
  0.0 78.3 jit_solution(15034876767763580965)
XLA Ops:
  0.6 6.0 %shard_map.68 = (f32[1024,2048]{1,0:T(8,128)S(1)}, f32[1024,2048]{1,0:T(8,128)S(1)}, f32[16,128]{1,0:T(8,128)S(1)}, f32[32,128]{1,0:T(8,128)S(1)}) custom-call(f32[64,1024]{1,0:T(8,128)} %bitcast.13, f32[64,1024]{1,0:T(8,128)} %bitcast.15, f32[64,2048]{1,0:T(8,128)} %bitcast.11, f32[8,128]{1,0:T(8,128)} %bitcast.17, f32[16,128]{1,0:T(8,128)} %bitcast.16), custom_call_target="tpu_custom_call" | custom-call | flops 1073741824 | bytes 1048576 | tf_op jit(solution)/shard_map/pallas_call | solution.py:335
  6.6 4.1 %collective-permute-start.1 = (f32[16,128]{1,0:T(8,128)S(1)}, f32[16,128]{1,0:T(8,128)S(1)}, u32[]{:S(2)}, u32[]{:S(2)}) collective-permute-start(f32[16,128]{1,0:T(8,128)S(1)} %get-tuple-element.14), channel_id=1, source_target_pairs={{0,2},{1,3},{2,0},{3,1},{4,6},{5,7},{6,4},{7,5},{8,10},{9,11},{10,... | collective-permute-start | bytes 24584 | tf_op jit(solution)/shard_map/ppermute | solution.py:307
  10.7 1.3 %collective-permute-start.2 = (f32[16,128]{1,0:T(8,128)S(1)}, f32[16,128]{1,0:T(8,128)S(1)}, u32[]{:S(2)}, u32[]{:S(2)}) collective-permute-start(f32[16,128]{1,0:T(8,128)S(1)} %get-tuple-element.14), channel_id=1, source_target_pairs={{0,3},{1,2},{2,1},{3,0},{4,7},{5,6},{6,5},{7,4},{8,11},{9,10},{10,... | collective-permute-start | bytes 24584 | tf_op jit(solution)/shard_map/ppermute | solution.py:307
  12.1 0.2 collective-permute-start
  12.3 0.1 collective-permute-done.1
  12.4 3.8 %collective-permute-done.2 = f32[16,128]{1,0:T(8,128)S(1)} collective-permute-done((f32[16,128]{1,0:T(8,128)S(1)}, f32[16,128]{1,0:T(8,128)S(1)}, u32[]{:S(2)}, u32[]{:S(2)}) %collective-permute-start.2) | collective-permute-done | bytes 8224 | tf_op jit(solution)/shard_map/ppermute | solution.py:307
  16.2 0.0 collective-permute-done
  16.2 1.2 %shard_map.69 = f32[48,128]{1,0:T(8,128)S(1)} custom-call(f32[1024,2048]{1,0:T(8,128)S(1)} %get-tuple-element.12.plan_ref, f32[16,128]{1,0:T(8,128)S(1)} %add_add_fusion.3.rows_ref, f32[32,128]{1,0:T(8,128)S(1)} %get-tuple-element.15.cols_ref), custom_call_target="tpu_custom_call" | custom-call | flops 1073741824 | bytes 1048576 | tf_op jit(solution)/shard_map/pallas_call | solution.py:335
  17.4 0.1 collective-permute-start.3
  17.5 1.2 %collective-permute-done.3 = f32[48,128]{1,0:T(8,128)S(1)} collective-permute-done((f32[48,128]{1,0:T(8,128)S(1)}, f32[48,128]{1,0:T(8,128)S(1)}, u32[]{:S(2)}, u32[]{:S(2)}) %collective-permute-start.3) | collective-permute-done | bytes 24608 | tf_op jit(solution)/shard_map/ppermute | solution.py:307
  18.7 1.5 %collective-permute-start.5 = (f32[48,128]{1,0:T(8,128)S(1)}, f32[48,128]{1,0:T(8,128)S(1)}, u32[]{:S(2)}, u32[]{:S(2)}) collective-permute-start(f32[48,128]{1,0:T(8,128)S(1)} %add.66), channel_id=1, source_target_pairs={{0,16},{4,20},{8,24},{12,28},{16,0},{20,4},{24,8},{28,12},{1,17},{... | collective-permute-start | bytes 73736 | tf_op jit(solution)/shard_map/ppermute | solution.py:307
  20.2 1.4 %collective-permute-start.6 = (f32[48,128]{1,0:T(8,128)S(1)}, f32[48,128]{1,0:T(8,128)S(1)}, u32[]{:S(2)}, u32[]{:S(2)}) collective-permute-start(f32[48,128]{1,0:T(8,128)S(1)} %add.66), channel_id=1, source_target_pairs={{0,24},{4,28},{8,16},{12,20},{16,8},{20,12},{24,0},{28,4},{1,25},{... | collective-permute-start | bytes 73736 | tf_op jit(solution)/shard_map/ppermute | solution.py:307
  21.6 0.5 collective-permute-start.4
  22.2 0.3 collective-permute-done.5
  22.5 2.6 %collective-permute-done.6 = f32[48,128]{1,0:T(8,128)S(1)} collective-permute-done((f32[48,128]{1,0:T(8,128)S(1)}, f32[48,128]{1,0:T(8,128)S(1)}, u32[]{:S(2)}, u32[]{:S(2)}) %collective-permute-start.6) | collective-permute-done | bytes 24608 | tf_op jit(solution)/shard_map/ppermute | solution.py:307
  25.0 0.4 collective-permute-done.4
  25.5 2.0 %shard_map.70 = f32[16,128]{1,0:T(8,128)S(1)} custom-call(f32[1024,2048]{1,0:T(8,128)S(1)} %get-tuple-element.12.plan_ref, f32[48,128]{1,0:T(8,128)S(1)} %add_add_fusion.cols_ref), custom_call_target="tpu_custom_call" | custom-call | flops 1073741824 | bytes 1048576 | tf_op jit(solution)/shard_map/pallas_call | solution.py:335
  27.5 1.3 %collective-permute-start.8 = (f32[16,128]{1,0:T(8,128)S(1)}, f32[16,128]{1,0:T(8,128)S(1)}, u32[]{:S(2)}, u32[]{:S(2)}) collective-permute-start(f32[16,128]{1,0:T(8,128)S(1)} %shard_map.70), channel_id=1, source_target_pairs={{0,2},{1,3},{2,0},{3,1},{4,6},{5,7},{6,4},{7,5},{8,10},{9,11},{10,... | collective-permute-start | bytes 24584 | tf_op jit(solution)/shard_map/ppermute | solution.py:307
  28.8 0.9 %collective-permute-start.9 = (f32[16,128]{1,0:T(8,128)S(1)}, f32[16,128]{1,0:T(8,128)S(1)}, u32[]{:S(2)}, u32[]{:S(2)}) collective-permute-start(f32[16,128]{1,0:T(8,128)S(1)} %shard_map.70), channel_id=1, source_target_pairs={{0,3},{1,2},{2,1},{3,0},{4,7},{5,6},{6,5},{7,4},{8,11},{9,10},{10,... | collective-permute-start | bytes 24584 | tf_op jit(solution)/shard_map/ppermute | solution.py:307
  29.7 1.3 %collective-permute-start.7 = (f32[16,128]{1,0:T(8,128)S(1)}, f32[16,128]{1,0:T(8,128)S(1)}, u32[]{:S(2)}, u32[]{:S(2)}) collective-permute-start(f32[16,128]{1,0:T(8,128)S(1)} %shard_map.70), channel_id=1, source_target_pairs={{0,1},{1,0},{2,3},{3,2},{4,5},{5,4},{6,7},{7,6},{8,9},{9,8},{10,11... | collective-permute-start | bytes 24584 | tf_op jit(solution)/shard_map/ppermute | solution.py:307
  31.0 1.1 %collective-permute-done.8 = f32[16,128]{1,0:T(8,128)S(1)} collective-permute-done((f32[16,128]{1,0:T(8,128)S(1)}, f32[16,128]{1,0:T(8,128)S(1)}, u32[]{:S(2)}, u32[]{:S(2)}) %collective-permute-start.8) | collective-permute-done | bytes 8224 | tf_op jit(solution)/shard_map/ppermute | solution.py:307
  32.1 2.1 %collective-permute-done.9 = f32[16,128]{1,0:T(8,128)S(1)} collective-permute-done((f32[16,128]{1,0:T(8,128)S(1)}, f32[16,128]{1,0:T(8,128)S(1)}, u32[]{:S(2)}, u32[]{:S(2)}) %collective-permute-start.9) | collective-permute-done | bytes 8224 | tf_op jit(solution)/shard_map/ppermute | solution.py:307
  34.2 0.0 collective-permute-done.7
  34.2 0.0 copy-start
  34.2 2.3 %shard_map.71 = f32[32,128]{1,0:T(8,128)S(1)} custom-call(f32[1024,2048]{1,0:T(8,128)S(1)} %get-tuple-element.12.plan_ref, f32[16,128]{1,0:T(8,128)S(1)} %add_add_fusion.3.rows_ref, f32[16,128]{1,0:T(8,128)S(1)} %add_add_fusion.2.terms_ref), custom_call_target="tpu_custom_call" | custom-call | flops 1073741824 | bytes 1048576 | tf_op jit(solution)/shard_map/pallas_call | solution.py:335
  36.5 0.1 collective-permute-start.10
  36.6 1.2 %collective-permute-done.10 = f32[32,128]{1,0:T(8,128)S(1)} collective-permute-done((f32[32,128]{1,0:T(8,128)S(1)}, f32[32,128]{1,0:T(8,128)S(1)}, u32[]{:S(2)}, u32[]{:S(2)}) %collective-permute-start.10) | collective-permute-done | bytes 16416 | tf_op jit(solution)/shard_map/ppermute | solution.py:307
  37.8 1.5 %collective-permute-start.12 = (f32[32,128]{1,0:T(8,128)S(1)}, f32[32,128]{1,0:T(8,128)S(1)}, u32[]{:S(2)}, u32[]{:S(2)}) collective-permute-start(f32[32,128]{1,0:T(8,128)S(1)} %add.73), channel_id=1, source_target_pairs={{0,16},{4,20},{8,24},{12,28},{16,0},{20,4},{24,8},{28,12},{1,17},{... | collective-permute-start | bytes 49160 | tf_op jit(solution)/shard_map/ppermute | solution.py:307
  39.3 0.9 %collective-permute-start.13 = (f32[32,128]{1,0:T(8,128)S(1)}, f32[32,128]{1,0:T(8,128)S(1)}, u32[]{:S(2)}, u32[]{:S(2)}) collective-permute-start(f32[32,128]{1,0:T(8,128)S(1)} %add.73), channel_id=1, source_target_pairs={{0,24},{4,28},{8,16},{12,20},{16,8},{20,12},{24,0},{28,4},{1,25},{... | collective-permute-start | bytes 49160 | tf_op jit(solution)/shard_map/ppermute | solution.py:307
  40.2 1.1 %collective-permute-start.11 = (f32[32,128]{1,0:T(8,128)S(1)}, f32[32,128]{1,0:T(8,128)S(1)}, u32[]{:S(2)}, u32[]{:S(2)}) collective-permute-start(f32[32,128]{1,0:T(8,128)S(1)} %add.73), channel_id=1, source_target_pairs={{0,8},{4,12},{8,0},{12,4},{16,24},{20,28},{24,16},{28,20},{1,9},{5... | collective-permute-start | bytes 49160 | tf_op jit(solution)/shard_map/ppermute | solution.py:307
  41.3 0.2 collective-permute-done.12
  41.5 2.4 %collective-permute-done.13 = f32[32,128]{1,0:T(8,128)S(1)} collective-permute-done((f32[32,128]{1,0:T(8,128)S(1)}, f32[32,128]{1,0:T(8,128)S(1)}, u32[]{:S(2)}, u32[]{:S(2)}) %collective-permute-start.13) | collective-permute-done | bytes 16416 | tf_op jit(solution)/shard_map/ppermute | solution.py:307
  44.0 0.0 collective-permute-done.11
  44.0 1.2 %shard_map.72 = f32[8,128]{1,0:T(8,128)S(1)} custom-call(f32[1024,2048]{1,0:T(8,128)S(1)} %get-tuple-element.12.plan_ref, f32[48,128]{1,0:T(8,128)S(1)} %add_add_fusion.cols_ref, f32[32,128]{1,0:T(8,128)S(1)} %add_add_fusion.1.terms_ref.bterms_ref), custom_call_target="tpu_custom_call" | custom-call | flops 1073741824 | bytes 1048576 | tf_op jit(solution)/shard_map/pallas_call | solution.py:335
  45.2 1.1 %collective-permute-start.15 = (f32[8,128]{1,0:T(8,128)S(1)}, f32[8,128]{1,0:T(8,128)S(1)}, u32[]{:S(2)}, u32[]{:S(2)}) collective-permute-start(f32[8,128]{1,0:T(8,128)S(1)} %shard_map.72), channel_id=1, source_target_pairs={{0,2},{1,3},{2,0},{3,1},{4,6},{5,7},{6,4},{7,5},{8,10},{9,11},{10,... | collective-permute-start | bytes 12296 | tf_op jit(solution)/shard_map/ppermute | solution.py:307
  46.3 1.8 %collective-permute-start.16 = (f32[8,128]{1,0:T(8,128)S(1)}, f32[8,128]{1,0:T(8,128)S(1)}, u32[]{:S(2)}, u32[]{:S(2)}) collective-permute-start(f32[8,128]{1,0:T(8,128)S(1)} %shard_map.72), channel_id=1, source_target_pairs={{0,3},{1,2},{2,1},{3,0},{4,7},{5,6},{6,5},{7,4},{8,11},{9,10},{10,... | collective-permute-start | bytes 12296 | tf_op jit(solution)/shard_map/ppermute | solution.py:307
  48.1 0.7 collective-permute-start.14
  48.8 1.0 %collective-permute-done.15 = f32[8,128]{1,0:T(8,128)S(1)} collective-permute-done((f32[8,128]{1,0:T(8,128)S(1)}, f32[8,128]{1,0:T(8,128)S(1)}, u32[]{:S(2)}, u32[]{:S(2)}) %collective-permute-start.15) | collective-permute-done | bytes 4128 | tf_op jit(solution)/shard_map/ppermute | solution.py:307
  49.8 1.9 %collective-permute-done.16 = f32[8,128]{1,0:T(8,128)S(1)} collective-permute-done((f32[8,128]{1,0:T(8,128)S(1)}, f32[8,128]{1,0:T(8,128)S(1)}, u32[]{:S(2)}, u32[]{:S(2)}) %collective-permute-start.16) | collective-permute-done | bytes 4128 | tf_op jit(solution)/shard_map/ppermute | solution.py:307
  51.7 0.0 collective-permute-done.14
  51.7 0.0 copy-done
  51.7 0.0 copy-start.1
  51.7 3.2 %shard_map.73 = (f32[2,64,256]{2,1,0:T(8,128)S(1)}, f32[2,64,256]{2,1,0:T(8,128)S(1)}, f32[1024,128]{1,0:T(8,128)S(1)}, f32[8,2048]{1,0:T(8,128)S(1)}) custom-call(f32[1024,2048]{1,0:T(8,128)S(1)} %get-tuple-element.12.plan_ref, f32[1024,2048]{1,0:T(8,128)S(1)} %get-tuple-element.13.cot_ref, f32[64,2048]{1,0:T(8,128)S(1)} %bitcast.12, ...), custom_call_target="tpu_custom_call" | custom-call | flops 1073741824 | bytes 1048576 | tf_op jit(solution)/shard_map/pallas_call | solution.py:335
  54.9 0.0 copy-done.1
  54.9 2.5 %shard_map.74 = f32[8,64,256]{2,1,0:T(8,128)S(1)} custom-call(f32[1024,2048]{1,0:T(8,128)S(1)} %get-tuple-element.12.plan_ref, f32[1024,2048]{1,0:T(8,128)S(1)} %get-tuple-element.13.cot_ref, f32[64,1024]{1,0:T(8,128)S(1)} %bitcast.14, f32[1024,128]{1,0:T(8,128)S(1)} %get-tuple-element.18.spread_ref, f32[8,2048]{1,0:T(8,128)S(1)} %get-tuple-element.19.beta_ref), custom_call_target="tpu_custom_call" | custom-call | flops 8589934592 | bytes 1048576 | tf_op jit(solution)/shard_map/pallas_call | solution.py:335
  57.4 0.1 collective-permute-start.20
  57.5 0.7 collective-permute-start.17
  58.2 5.2 %collective-permute-done.17 = f32[2,64,256]{2,1,0:T(8,128)S(1)} collective-permute-done((f32[2,64,256]{2,1,0:T(8,128)S(1)}, f32[2,64,256]{2,1,0:T(8,128)S(1)}, u32[]{:S(2)}, u32[]{:S(2)}) %collective-permute-start.17) | collective-permute-done | bytes 131104 | tf_op jit(solution)/shard_map/ppermute | solution.py:307
  63.4 1.3 %collective-permute-start.18 = (f32[2,64,256]{2,1,0:T(8,128)S(1)}, f32[2,64,256]{2,1,0:T(8,128)S(1)}, u32[]{:S(2)}, u32[]{:S(2)}) collective-permute-start(f32[2,64,256]{2,1,0:T(8,128)S(1)} %add.80), channel_id=1, source_target_pairs={{0,2},{1,3},{2,0},{3,1},{4,6},{5,7},{6,4},{7,5},{8,10},{9,11},{10,... | collective-permute-start | bytes 393224 | tf_op jit(solution)/shard_map/ppermute | solution.py:307
  64.7 0.0 collective-permute-done.20
  64.7 1.1 %collective-permute-start.21 = (f32[2,64,256]{2,1,0:T(8,128)S(1)}, f32[2,64,256]{2,1,0:T(8,128)S(1)}, u32[]{:S(2)}, u32[]{:S(2)}) collective-permute-start(f32[2,64,256]{2,1,0:T(8,128)S(1)} %slice.27), channel_id=1, source_target_pairs={{0,8},{4,12},{8,0},{12,4},{16,24},{20,28},{24,16},{28,20},{1,9},{5... | collective-permute-start | bytes 393224 | tf_op jit(solution)/shard_map/ppermute | solution.py:307
  65.9 6.3 %collective-permute-done.18 = f32[2,64,256]{2,1,0:T(8,128)S(1)} collective-permute-done((f32[2,64,256]{2,1,0:T(8,128)S(1)}, f32[2,64,256]{2,1,0:T(8,128)S(1)}, u32[]{:S(2)}, u32[]{:S(2)}) %collective-permute-start.18) | collective-permute-done | bytes 131104 | tf_op jit(solution)/shard_map/ppermute | solution.py:307
  72.2 0.1 collective-permute-start.19
  72.3 0.0 collective-permute-done.21
  72.3 1.2 %collective-permute-start.22 = (f32[64,256]{1,0:T(8,128)S(1)}, f32[64,256]{1,0:T(8,128)S(1)}, u32[]{:S(2)}, u32[]{:S(2)}) collective-permute-start(f32[64,256]{1,0:T(8,128)S(1)} %get-tuple-element.22), channel_id=1, source_target_pairs={{0,16},{4,20},{8,24},{12,28},{16,0},{20,4},{24,8},{28,12},{1,17},{... | collective-permute-start | bytes 196616 | tf_op jit(solution)/shard_map/ppermute | solution.py:307
  73.5 4.1 %collective-permute-done.19.got_ref = f32[2,64,256]{2,1,0:T(8,128)S(1)} collective-permute-done((f32[2,64,256]{2,1,0:T(8,128)S(1)}, f32[2,64,256]{2,1,0:T(8,128)S(1)}, u32[]{:S(2)}, u32[]{:S(2)}) %collective-permute-start.19) | collective-permute-done | bytes 131104 | tf_op jit(solution)/shard_map/ppermute | solution.py:307
  77.6 0.0 collective-permute-done.22.theirs_ref
  77.6 0.7 shard_map.75
  (14 shorter events, 0.2 us)
Async XLA Ops:
  6.6 5.8 %collective-permute-start.1 = (f32[16,128]{1,0:T(8,128)S(1)}, f32[16,128]{1,0:T(8,128)S(1)}, u32[]{:S(2)}, u32[]{:S(2)}) collective-permute-start(f32[16,128]{1,0:T(8,128)S(1)} %get-tuple-element.14), channel_id=1, source_target_pairs={{0,2},{1,3},{2,0},{3,1},{4,6},{5,7},{6,4},{7,5},{8,10},{9,11},{10,... | collective-permute-start | bytes 24584 | tf_op jit(solution)/shard_map/ppermute | solution.py:307
  10.7 5.4 %collective-permute-start.2 = (f32[16,128]{1,0:T(8,128)S(1)}, f32[16,128]{1,0:T(8,128)S(1)}, u32[]{:S(2)}, u32[]{:S(2)}) collective-permute-start(f32[16,128]{1,0:T(8,128)S(1)} %get-tuple-element.14), channel_id=1, source_target_pairs={{0,3},{1,2},{2,1},{3,0},{4,7},{5,6},{6,5},{7,4},{8,11},{9,10},{10,... | collective-permute-start | bytes 24584 | tf_op jit(solution)/shard_map/ppermute | solution.py:307
  12.1 4.1 %collective-permute-start = (f32[16,128]{1,0:T(8,128)S(1)}, f32[16,128]{1,0:T(8,128)S(1)}, u32[]{:S(2)}, u32[]{:S(2)}) collective-permute-start(f32[16,128]{1,0:T(8,128)S(1)} %get-tuple-element.14), channel_id=1, source_target_pairs={{0,1},{1,0},{2,3},{3,2},{4,5},{5,4},{6,7},{7,6},{8,9},{9,8},{10,11... | collective-permute-start | bytes 24584 | tf_op jit(solution)/shard_map/ppermute | solution.py:307
  17.4 1.3 %collective-permute-start.3 = (f32[48,128]{1,0:T(8,128)S(1)}, f32[48,128]{1,0:T(8,128)S(1)}, u32[]{:S(2)}, u32[]{:S(2)}) collective-permute-start(f32[48,128]{1,0:T(8,128)S(1)} %shard_map.69), channel_id=1, source_target_pairs={{0,4},{4,0},{8,12},{12,8},{16,20},{20,16},{24,28},{28,24},{1,5},{5... | collective-permute-start | bytes 73736 | tf_op jit(solution)/shard_map/ppermute | solution.py:307
  18.7 3.8 %collective-permute-start.5 = (f32[48,128]{1,0:T(8,128)S(1)}, f32[48,128]{1,0:T(8,128)S(1)}, u32[]{:S(2)}, u32[]{:S(2)}) collective-permute-start(f32[48,128]{1,0:T(8,128)S(1)} %add.66), channel_id=1, source_target_pairs={{0,16},{4,20},{8,24},{12,28},{16,0},{20,4},{24,8},{28,12},{1,17},{... | collective-permute-start | bytes 73736 | tf_op jit(solution)/shard_map/ppermute | solution.py:307
  20.2 4.9 %collective-permute-start.6 = (f32[48,128]{1,0:T(8,128)S(1)}, f32[48,128]{1,0:T(8,128)S(1)}, u32[]{:S(2)}, u32[]{:S(2)}) collective-permute-start(f32[48,128]{1,0:T(8,128)S(1)} %add.66), channel_id=1, source_target_pairs={{0,24},{4,28},{8,16},{12,20},{16,8},{20,12},{24,0},{28,4},{1,25},{... | collective-permute-start | bytes 73736 | tf_op jit(solution)/shard_map/ppermute | solution.py:307
  21.6 3.8 %collective-permute-start.4 = (f32[48,128]{1,0:T(8,128)S(1)}, f32[48,128]{1,0:T(8,128)S(1)}, u32[]{:S(2)}, u32[]{:S(2)}) collective-permute-start(f32[48,128]{1,0:T(8,128)S(1)} %add.66), channel_id=1, source_target_pairs={{0,8},{4,12},{8,0},{12,4},{16,24},{20,28},{24,16},{28,20},{1,9},{5... | collective-permute-start | bytes 73736 | tf_op jit(solution)/shard_map/ppermute | solution.py:307
  27.5 4.6 %collective-permute-start.8 = (f32[16,128]{1,0:T(8,128)S(1)}, f32[16,128]{1,0:T(8,128)S(1)}, u32[]{:S(2)}, u32[]{:S(2)}) collective-permute-start(f32[16,128]{1,0:T(8,128)S(1)} %shard_map.70), channel_id=1, source_target_pairs={{0,2},{1,3},{2,0},{3,1},{4,6},{5,7},{6,4},{7,5},{8,10},{9,11},{10,... | collective-permute-start | bytes 24584 | tf_op jit(solution)/shard_map/ppermute | solution.py:307
  28.8 5.4 %collective-permute-start.9 = (f32[16,128]{1,0:T(8,128)S(1)}, f32[16,128]{1,0:T(8,128)S(1)}, u32[]{:S(2)}, u32[]{:S(2)}) collective-permute-start(f32[16,128]{1,0:T(8,128)S(1)} %shard_map.70), channel_id=1, source_target_pairs={{0,3},{1,2},{2,1},{3,0},{4,7},{5,6},{6,5},{7,4},{8,11},{9,10},{10,... | collective-permute-start | bytes 24584 | tf_op jit(solution)/shard_map/ppermute | solution.py:307
  29.7 4.5 %collective-permute-start.7 = (f32[16,128]{1,0:T(8,128)S(1)}, f32[16,128]{1,0:T(8,128)S(1)}, u32[]{:S(2)}, u32[]{:S(2)}) collective-permute-start(f32[16,128]{1,0:T(8,128)S(1)} %shard_map.70), channel_id=1, source_target_pairs={{0,1},{1,0},{2,3},{3,2},{4,5},{5,4},{6,7},{7,6},{8,9},{9,8},{10,11... | collective-permute-start | bytes 24584 | tf_op jit(solution)/shard_map/ppermute | solution.py:307
  34.2 17.5 %copy-start = (f32[2048,64]{0,1:T(8,128)S(1)}, f32[2048,64]{0,1:T(8,128)}, u32[]{:S(2)}) copy-start(f32[2048,64]{0,1:T(8,128)} %param.6) | copy-start | bytes 1572868
  36.5 1.2 %collective-permute-start.10 = (f32[32,128]{1,0:T(8,128)S(1)}, f32[32,128]{1,0:T(8,128)S(1)}, u32[]{:S(2)}, u32[]{:S(2)}) collective-permute-start(f32[32,128]{1,0:T(8,128)S(1)} %shard_map.71), channel_id=1, source_target_pairs={{0,4},{4,0},{8,12},{12,8},{16,20},{20,16},{24,28},{28,24},{1,5},{5... | collective-permute-start | bytes 49160 | tf_op jit(solution)/shard_map/ppermute | solution.py:307
  37.8 3.7 %collective-permute-start.12 = (f32[32,128]{1,0:T(8,128)S(1)}, f32[32,128]{1,0:T(8,128)S(1)}, u32[]{:S(2)}, u32[]{:S(2)}) collective-permute-start(f32[32,128]{1,0:T(8,128)S(1)} %add.73), channel_id=1, source_target_pairs={{0,16},{4,20},{8,24},{12,28},{16,0},{20,4},{24,8},{28,12},{1,17},{... | collective-permute-start | bytes 49160 | tf_op jit(solution)/shard_map/ppermute | solution.py:307
  39.3 4.6 %collective-permute-start.13 = (f32[32,128]{1,0:T(8,128)S(1)}, f32[32,128]{1,0:T(8,128)S(1)}, u32[]{:S(2)}, u32[]{:S(2)}) collective-permute-start(f32[32,128]{1,0:T(8,128)S(1)} %add.73), channel_id=1, source_target_pairs={{0,24},{4,28},{8,16},{12,20},{16,8},{20,12},{24,0},{28,4},{1,25},{... | collective-permute-start | bytes 49160 | tf_op jit(solution)/shard_map/ppermute | solution.py:307
  40.2 3.7 %collective-permute-start.11 = (f32[32,128]{1,0:T(8,128)S(1)}, f32[32,128]{1,0:T(8,128)S(1)}, u32[]{:S(2)}, u32[]{:S(2)}) collective-permute-start(f32[32,128]{1,0:T(8,128)S(1)} %add.73), channel_id=1, source_target_pairs={{0,8},{4,12},{8,0},{12,4},{16,24},{20,28},{24,16},{28,20},{1,9},{5... | collective-permute-start | bytes 49160 | tf_op jit(solution)/shard_map/ppermute | solution.py:307
  45.2 4.6 %collective-permute-start.15 = (f32[8,128]{1,0:T(8,128)S(1)}, f32[8,128]{1,0:T(8,128)S(1)}, u32[]{:S(2)}, u32[]{:S(2)}) collective-permute-start(f32[8,128]{1,0:T(8,128)S(1)} %shard_map.72), channel_id=1, source_target_pairs={{0,2},{1,3},{2,0},{3,1},{4,6},{5,7},{6,4},{7,5},{8,10},{9,11},{10,... | collective-permute-start | bytes 12296 | tf_op jit(solution)/shard_map/ppermute | solution.py:307
  46.3 5.4 %collective-permute-start.16 = (f32[8,128]{1,0:T(8,128)S(1)}, f32[8,128]{1,0:T(8,128)S(1)}, u32[]{:S(2)}, u32[]{:S(2)}) collective-permute-start(f32[8,128]{1,0:T(8,128)S(1)} %shard_map.72), channel_id=1, source_target_pairs={{0,3},{1,2},{2,1},{3,0},{4,7},{5,6},{6,5},{7,4},{8,11},{9,10},{10,... | collective-permute-start | bytes 12296 | tf_op jit(solution)/shard_map/ppermute | solution.py:307
  48.1 3.6 %collective-permute-start.14 = (f32[8,128]{1,0:T(8,128)S(1)}, f32[8,128]{1,0:T(8,128)S(1)}, u32[]{:S(2)}, u32[]{:S(2)}) collective-permute-start(f32[8,128]{1,0:T(8,128)S(1)} %shard_map.72), channel_id=1, source_target_pairs={{0,1},{1,0},{2,3},{3,2},{4,5},{5,4},{6,7},{7,6},{8,9},{9,8},{10,11... | collective-permute-start | bytes 12296 | tf_op jit(solution)/shard_map/ppermute | solution.py:307
  51.7 3.2 %copy-start.1 = (f32[1024,64]{0,1:T(8,128)S(1)}, f32[1024,64]{0,1:T(8,128)}, u32[]{:S(2)}) copy-start(f32[1024,64]{0,1:T(8,128)} %param.5) | copy-start | bytes 786436
  57.4 7.3 %collective-permute-start.20 = (f32[4,64,256]{2,1,0:T(8,128)S(1)}, f32[4,64,256]{2,1,0:T(8,128)S(1)}, u32[]{:S(2)}, u32[]{:S(2)}) collective-permute-start(f32[4,64,256]{2,1,0:T(8,128)S(1)} %slice.25), channel_id=1, source_target_pairs={{0,4},{4,0},{8,12},{12,8},{16,20},{20,16},{24,28},{28,24},{1,5},{5... | collective-permute-start | bytes 786440 | tf_op jit(solution)/shard_map/ppermute | solution.py:307
  57.5 5.9 %collective-permute-start.17 = (f32[2,64,256]{2,1,0:T(8,128)S(1)}, f32[2,64,256]{2,1,0:T(8,128)S(1)}, u32[]{:S(2)}, u32[]{:S(2)}) collective-permute-start(f32[2,64,256]{2,1,0:T(8,128)S(1)} %get-tuple-element.17), channel_id=1, source_target_pairs={{0,1},{1,0},{2,3},{3,2},{4,5},{5,4},{6,7},{7,6},{8,9},{9,8},{10,11... | collective-permute-start | bytes 393224 | tf_op jit(solution)/shard_map/ppermute | solution.py:307
  63.4 8.7 %collective-permute-start.18 = (f32[2,64,256]{2,1,0:T(8,128)S(1)}, f32[2,64,256]{2,1,0:T(8,128)S(1)}, u32[]{:S(2)}, u32[]{:S(2)}) collective-permute-start(f32[2,64,256]{2,1,0:T(8,128)S(1)} %add.80), channel_id=1, source_target_pairs={{0,2},{1,3},{2,0},{3,1},{4,6},{5,7},{6,4},{7,5},{8,10},{9,11},{10,... | collective-permute-start | bytes 393224 | tf_op jit(solution)/shard_map/ppermute | solution.py:307
  64.7 7.5 %collective-permute-start.21 = (f32[2,64,256]{2,1,0:T(8,128)S(1)}, f32[2,64,256]{2,1,0:T(8,128)S(1)}, u32[]{:S(2)}, u32[]{:S(2)}) collective-permute-start(f32[2,64,256]{2,1,0:T(8,128)S(1)} %slice.27), channel_id=1, source_target_pairs={{0,8},{4,12},{8,0},{12,4},{16,24},{20,28},{24,16},{28,20},{1,9},{5... | collective-permute-start | bytes 393224 | tf_op jit(solution)/shard_map/ppermute | solution.py:307
  72.2 5.4 %collective-permute-start.19 = (f32[2,64,256]{2,1,0:T(8,128)S(1)}, f32[2,64,256]{2,1,0:T(8,128)S(1)}, u32[]{:S(2)}, u32[]{:S(2)}) collective-permute-start(f32[2,64,256]{2,1,0:T(8,128)S(1)} %add.81.own_ref), channel_id=1, source_target_pairs={{0,1},{1,0},{2,3},{3,2},{4,5},{5,4},{6,7},{7,6},{8,9},{9,8},{10,11... | collective-permute-start | bytes 393224 | tf_op jit(solution)/shard_map/ppermute | solution.py:307
  72.3 5.3 %collective-permute-start.22 = (f32[64,256]{1,0:T(8,128)S(1)}, f32[64,256]{1,0:T(8,128)S(1)}, u32[]{:S(2)}, u32[]{:S(2)}) collective-permute-start(f32[64,256]{1,0:T(8,128)S(1)} %get-tuple-element.22), channel_id=1, source_target_pairs={{0,16},{4,20},{8,24},{12,28},{16,0},{20,4},{24,8},{28,12},{1,17},{... | collective-permute-start | bytes 196616 | tf_op jit(solution)/shard_map/ppermute | solution.py:307

commit v3 on v2

--- a/solution.py
+++ b/solution.py
@@ -10,6 +10,7 @@
 
 EPSILON = 0.08
 LANES = 128
+LOG2_E = math.log2(math.e)
 F32 = jnp.float32
 BF16 = jnp.bfloat16
 VMEM = pl.BlockSpec(memory_space=pltpu.VMEM)
@@ -73,7 +74,7 @@
 
 
 def first_kernel(total, emb_hbm, tgt_hbm, cen_hbm, pd_hbm, cd_hbm, plan_ref, cot_ref, rows_ref, cols_ref,
-                 emb_ref, tgt_ref, cen_ref, pd_ref, cd_ref, sems, lhs_ref, tlhs_ref, rhs_ref, rm_ref, rl_ref, cm_ref, cl_ref, pdual_ref, cdual_ref):
+                 emb_ref, tgt_ref, cen_ref, pd_ref, cd_ref, sems, lhs_ref, rhs_ref, rm_ref, rl_ref, cm_ref, cl_ref, pdual_ref, cdual_ref):
     rows, cols = plan_ref.shape
     copies = [
         pltpu.make_async_copy(source, target, sems.at[k])
@@ -87,14 +88,14 @@
     cl_ref[...] = jnp.zeros_like(cl_ref)
     for copy in copies:
         copy.wait()
-    flat_row(pd_ref[...], pdual_ref)
-    flat_row(cd_ref[...] - math.log(total), cdual_ref)
-    eh, el = (part.astype(F32) for part in split2(emb_ref[...] * (1.0 / EPSILON)))
+    flat_row(pd_ref[...] * LOG2_E, pdual_ref)
+    flat_row(cd_ref[...] * LOG2_E - math.log2(total), cdual_ref)
+    eh, el = (part.astype(F32) for part in split2(emb_ref[...] * (LOG2_E / EPSILON)))
     th, tl = (part.astype(F32) for part in split2(tgt_ref[...]))
-    transpose_into(lhs_ref, jnp.concatenate([eh, eh], axis=0))
-    transpose_into(lhs_ref, jnp.concatenate([el, dual_rows(pdual_ref[...], True)], axis=0), LANES)
-    transpose_into(tlhs_ref, jnp.concatenate([th, th], axis=0))
-    transpose_into(tlhs_ref, jnp.concatenate([tl, jnp.zeros_like(tl)], axis=0), LANES)
+    transpose_into(lhs_ref.at[0], jnp.concatenate([eh, eh], axis=0))
+    transpose_into(lhs_ref.at[0], jnp.concatenate([el, dual_rows(pdual_ref[...], True)], axis=0), LANES)
+    transpose_into(lhs_ref.at[1], jnp.concatenate([th, th], axis=0))
+    transpose_into(lhs_ref.at[1], jnp.concatenate([tl, jnp.zeros_like(tl)], axis=0), LANES)
     ch, cl = split2(cen_ref[...])
     rhs_ref[...] = jnp.concatenate([ch, cl, ch, dual_rows(cdual_ref[...], False).astype(BF16)], axis=0)
     tm, tn = 128, 256
@@ -102,15 +103,15 @@
     @pl.loop(0, rows // tm)
     def _(i):
         at = pl.ds(pl.multiple_of(i * tm, tm), tm)
-        left = lhs_ref[at, :]
-        tleft = tlhs_ref[at, :]
+        left = lhs_ref[:, at, :].reshape(2 * tm, 2 * LANES)
         mass = jnp.zeros((tm, LANES), F32)
         load = jnp.zeros((tm, LANES), F32)
         for j in range(cols // tn):
             js = slice(j * tn, (j + 1) * tn)
             right = rhs_ref[:, js]
-            plan = jnp.exp(dot(left, right))
-            cot = dot(tleft, right)
+            both = dot(left, right)
+            plan = jnp.exp2(both[:tm])
+            cot = both[tm:]
             plan_ref[at, js] = plan
             cot_ref[at, js] = cot
             weighted = plan * cot
@@ -142,14 +143,14 @@
     for k, scale in enumerate(scales):
         for g in range(rows // LANES):
             spread_ref[k, g * LANES : (g + 1) * LANES, :] = spread_rows(scale[g : g + 1, :])
-    wide = 16 // count
+    wide = 16
     for t0 in range(0, tiles, wide):
         span = min(wide, tiles - t0)
 
         def step(i, acc, t0=t0, span=span):
             acc = list(acc)
-            for r in range(2):
-                at = pl.ds(pl.multiple_of(i * 16 + r * 8, 8), 8)
+            for r in range(8):
+                at = pl.ds(pl.multiple_of(i * 64 + r * 8, 8), 8)
                 scale_rows = [spread_ref[k, at, :] for k in range(count)]
                 for t in range(span):
                     tile = plan_ref[at, (t0 + t) * LANES : (t0 + t + 1) * LANES]
@@ -158,7 +159,7 @@
             return tuple(acc)
 
         zero = jnp.zeros((8, LANES), F32)
-        acc = lax.fori_loop(0, rows // 16, step, (zero,) * (count * span))
+        acc = lax.fori_loop(0, rows // 64, step, (zero,) * (count * span))
         for k in range(count):
             for t in range(span):
                 at = k * tiles + t0 + t
@@ -174,10 +175,10 @@
         [jnp.broadcast_to(scale[t : t + 1, :], (8, LANES)) for t in range(tiles)] for scale in scales
     ]
 
-    @pl.loop(0, rows // 16)
+    @pl.loop(0, rows // 64)
     def _(i):
-        for r in range(2):
-            at = pl.ds(pl.multiple_of(i * 16 + r * 8, 8), 8)
+        for r in range(8):
+            at = pl.ds(pl.multiple_of(i * 64 + r * 8, 8), 8)
             sums = [[None, None] for _ in range(count)]
             for t in range(tiles):
                 tile = plan_ref[at, t * LANES : (t + 1) * LANES]
@@ -234,42 +235,56 @@
     return split2(plan_ref[at, js] * (cot_ref[at, js] - shift.reshape(tm, tn)))
 
 
-def scales_of(rows_ref, aterms_ref, cols_ref, bterms_ref, spread_ref, beta_ref):
-    groups = rows_ref.shape[0] // 2
+def right_of(cen_ref, right_ref):
+    ch, cl = split2(cen_ref[...])
+    transpose_into(right_ref, jnp.concatenate([ch.astype(F32), cl.astype(F32)], axis=0))
+
+
+def fold_into(out_ref, at, total):
+    flipped = total.T
+    out_ref[:, at] = flipped[: LANES // 2] + flipped[LANES // 2 :]
+
+
+def bary_kernel(plan_ref, cen_ref, out_ref, right_ref):
+    right_of(cen_ref, right_ref)
+    for g in range(plan_ref.shape[0] // LANES):
+        at = slice(g * LANES, (g + 1) * LANES)
+        both = jnp.concatenate(split2(plan_ref[at, :]), axis=0)
+        total = dot(both, right_ref[...])
+        fold_into(out_ref, at, total[:LANES] + total[LANES:])
+
+
+def pre_kernel(plan_ref, cot_ref, right_ref, cols_ref, bterms_ref, out_ref, beta_ref):
     tiles = cols_ref.shape[0] // 3
-    alpha = (rows_ref[groups:, :] - aterms_ref[...]) / rows_ref[:groups, :]
-    for g in range(groups):
-        spread_ref[g * LANES : (g + 1) * LANES, :] = spread_rows(alpha[g : g + 1, :])
     beta = (cols_ref[tiles : 2 * tiles, :] - bterms_ref[tiles:, :]) / cols_ref[:tiles, :]
     for t in range(tiles):
         beta_ref[:, t * LANES : (t + 1) * LANES] = jnp.broadcast_to(beta[t : t + 1, :], (8, LANES))
-
-
-def emb_kernel(plan_ref, cot_ref, cen_ref, rows_ref, aterms_ref, cols_ref, bterms_ref,
-               keep_ref, send_ref, spread_out_ref, beta_ref, right_ref):
-    _, cols = plan_ref.shape
-    scales_of(rows_ref, aterms_ref, cols_ref, bterms_ref, spread_out_ref, beta_ref)
-    ch, cl = split2(cen_ref[...])
-    transpose_into(right_ref, jnp.concatenate([ch.astype(F32), cl.astype(F32)], axis=0))
-    tn = 256
-    half, width, span = keep_ref.shape
-    chunks = 2 * half
+    cols = plan_ref.shape[1]
+    low = beta_ref[...][None]
+    for g in range(plan_ref.shape[0] // LANES):
+        at = slice(g * LANES, (g + 1) * LANES)
+        shifted = cot_ref[at, :].reshape(LANES // 8, 8, cols) - low
+        both = jnp.concatenate(split2(plan_ref[at, :] * shifted.reshape(LANES, cols)), axis=0)
+        total = dot(both, right_ref[...])
+        fold_into(out_ref, at, total[:LANES] + total[LANES:])
+
+
+def post_kernel(pre_ref, bary_ref, rows_ref, aterms_ref, keep_ref, send_ref, alpha_ref, flat_ref):
+    groups = rows_ref.shape[0] // 2
+    alpha_ref[...] = (rows_ref[groups:, :] - aterms_ref[...]) / rows_ref[:groups, :]
+    flat_row(alpha_ref[...], flat_ref)
+    half, _, span = keep_ref.shape
     me = lax.axis_index("cen") & (half - 1)
-    for q in range(chunks):
-        at = pl.ds(pl.multiple_of((me ^ reverse_bits(q, chunks)) * span, span), span)
-        acc = jnp.zeros((span, LANES), F32)
-        for j in range(cols // tn):
-            js = slice(j * tn, (j + 1) * tn)
-            wh, wl = weights_of(plan_ref, cot_ref, spread_out_ref, beta_ref[:, js], at, js)
-            right = right_ref[js, :]
-            acc = acc + dot(wh, right) + dot(wl, right)
-        flipped = acc.T
+    for q in range(2 * half):
+        at = pl.ds(pl.multiple_of((me ^ reverse_bits(q, 2 * half)) * span, span), span)
         to_ref = keep_ref if q < half else send_ref
-        to_ref[q % half] = flipped[:width] + flipped[width:]
-
-
-def cen_kernel(plan_ref, cot_ref, emb_ref, spread_ref, beta_ref, gcen_ref):
+        to_ref[q % half] = pre_ref[:, at] - flat_ref[:, at] * bary_ref[:, at]
+
+
+def cen_kernel(plan_ref, cot_ref, emb_ref, alpha_ref, beta_ref, gcen_ref, spread_ref):
     rows, cols = plan_ref.shape
+    for g in range(rows // LANES):
+        spread_ref[g * LANES : (g + 1) * LANES, :] = spread_rows(alpha_ref[g : g + 1, :])
     left = jnp.concatenate(split2(emb_ref[...]), axis=0)
     tn = 256
     tm = 256
@@ -360,9 +375,8 @@
             pltpu.VMEM((groups, LANES), F32),
             pltpu.VMEM((tiles, LANES), F32),
             pltpu.SemaphoreType.DMA((5,)),
-            pltpu.VMEM((rows, 256), BF16),
-            pltpu.VMEM((rows, 256), BF16),
-            pltpu.VMEM((256, cols), BF16),
+            pltpu.VMEM((2, rows, 2 * LANES), BF16),
+            pltpu.VMEM((2 * LANES, cols), BF16),
             pltpu.VMEM((rows, LANES), F32),
             pltpu.VMEM((rows, LANES), F32),
             pltpu.VMEM((8, cols), F32),
@@ -398,6 +412,15 @@
         plan,
         col_all,
     )
+    bary, right = call(
+        bary_kernel,
+        (pltpu.VMEM((width, rows), F32), pltpu.VMEM((cols, LANES), BF16)),
+        [],
+        12,
+        [VMEM] * 2,
+        plan,
+        ctr,
+    )
     row_terms = sum_all(row_terms, "cen", cen, 2)
     col_terms = call(
         fourth_kernel,
@@ -420,37 +443,45 @@
         col_all,
         col_terms,
     )
+    pre, beta = call(
+        pre_kernel,
+        (pltpu.VMEM((width, rows), F32), pltpu.VMEM((8, cols), F32)),
+        [],
+        12,
+        [VMEM] * 5,
+        plan,
+        cot,
+        right,
+        col_all,
+        col_terms,
+    )
     last_terms = sum_all(last_terms, "cen", cen, 2)
-    gemb, sent, spread, beta = call(
-        emb_kernel,
+    gemb, sent, alpha = call(
+        post_kernel,
         (
             pltpu.VMEM((cen // 2, width, rows // cen), F32),
             pltpu.VMEM((cen // 2, width, rows // cen), F32),
-            pltpu.VMEM((rows, LANES), F32),
-            pltpu.VMEM((8, cols), F32),
+            pltpu.VMEM((groups, LANES), F32),
         ),
-        [pltpu.VMEM((cols, LANES), BF16)],
-        12,
-        [VMEM] * 7,
-        plan,
-        cot,
-        ctr,
+        [pltpu.VMEM((1, rows), F32)],
+        6,
+        [VMEM] * 4,
+        pre,
+        bary,
         row_sums,
         last_terms,
-        col_all,
-        col_terms,
     )
     sent = swap(sent, "cen", cen, 1)
     gcen = call(
         cen_kernel,
         pltpu.VMEM((pts, width, cols // pts), F32),
-        [],
+        [pltpu.VMEM((rows, LANES), F32)],
         12,
         [VMEM] * 5,
         plan,
         cot,
         emb,
-        spread,
+        alpha,
         beta,
         flops=1 << 33,
     )

time: 78.5 us -> 73.3 us (0.934)
  waiting for transfers between devices: 33.9 us -> 26.5 us
  starting transfers between devices: 24.3 us -> 25.9 us
    ppermute x23, waiting for transfers between devices: 33.9 us -> 26.5 us  [swap(): return lax.ppermute(value, axis, [(i, i ^ bit) for i in range(count)])]
    ppermute x23, starting transfers between devices: 24.3 us -> 25.9 us  [swap(): return lax.ppermute(value, axis, [(i, i ^ bit) for i in range(count)])]
    pallas_call x8 -> x10, Pallas kernels: 19.1 us -> 19.6 us  [call(): pl.pallas_call(body, out_shape=outs, in_specs=specs, out_specs=jax.tree.m...]
  transfers between devices with their start and end apart: 23 -> 23, of which waited for: 16 -> 12; matrix products, arithmetic and copies ran while one was open for 0% -> 0% of each run, Pallas kernels for 0% -> 7%
where the time goes in v3:
time: 73.3 us; the launch traced here: 73.1 us
  waiting for transfers between devices  26.5 us (36%)
  starting transfers between devices  25.9 us (35%)
  Pallas kernels  19.6 us (27%)
  between operations  0.84 us (1%)
    ppermute x23, waiting for transfers between devices, swap(): return lax.ppermute(value, axis, [(i, i ^ bit) for i in range(count)])  26.5 us
    ppermute x23, starting transfers between devices, swap(): return lax.ppermute(value, axis, [(i, i ^ bit) for i in range(count)])  25.9 us
    pallas_call x10, Pallas kernels, call(): pl.pallas_call(body, out_shape=outs, in_specs=specs, out_specs=jax.tree.m...  19.6 us
  transfers between devices with their start and end apart: 23, of which 12 were waited for; matrix products, arithmetic and copies ran while one was open for 0% of the time, Pallas kernels for 7%

profile of v3, /device:TPU:0, one launch (start us, length us, event | category | flops | bytes accessed | tf_op | source)
XLA Modules:
  0.0 73.1 jit_solution(15527074865477151763)
XLA Ops:
  0.6 5.8 %shard_map.68 = (f32[1024,2048]{1,0:T(8,128)S(1)}, f32[1024,2048]{1,0:T(8,128)S(1)}, f32[16,128]{1,0:T(8,128)S(1)}, f32[32,128]{1,0:T(8,128)S(1)}) custom-call(f32[64,1024]{1,0:T(8,128)} %bitcast.13, f32[64,1024]{1,0:T(8,128)} %bitcast.15, f32[64,2048]{1,0:T(8,128)} %bitcast.11, f32[8,128]{1,0:T(8,128)} %bitcast.17, f32[16,128]{1,0:T(8,128)} %bitcast.16), custom_call_target="tpu_custom_call" | custom-call | flops 1073741824 | bytes 1048576 | tf_op jit(solution)/shard_map/pallas_call | solution.py:350
  6.5 4.1 %collective-permute-start.1 = (f32[16,128]{1,0:T(8,128)S(1)}, f32[16,128]{1,0:T(8,128)S(1)}, u32[]{:S(2)}, u32[]{:S(2)}) collective-permute-start(f32[16,128]{1,0:T(8,128)S(1)} %get-tuple-element.18), channel_id=1, source_target_pairs={{0,2},{1,3},{2,0},{3,1},{4,6},{5,7},{6,4},{7,5},{8,10},{9,11},{10,... | collective-permute-start | bytes 24584 | tf_op jit(solution)/shard_map/ppermute | solution.py:322
  10.6 1.3 %collective-permute-start.2 = (f32[16,128]{1,0:T(8,128)S(1)}, f32[16,128]{1,0:T(8,128)S(1)}, u32[]{:S(2)}, u32[]{:S(2)}) collective-permute-start(f32[16,128]{1,0:T(8,128)S(1)} %get-tuple-element.18), channel_id=1, source_target_pairs={{0,3},{1,2},{2,1},{3,0},{4,7},{5,6},{6,5},{7,4},{8,11},{9,10},{10,... | collective-permute-start | bytes 24584 | tf_op jit(solution)/shard_map/ppermute | solution.py:322
  11.9 0.2 collective-permute-start
  12.2 0.0 collective-permute-done.1
  12.2 3.8 %collective-permute-done.2 = f32[16,128]{1,0:T(8,128)S(1)} collective-permute-done((f32[16,128]{1,0:T(8,128)S(1)}, f32[16,128]{1,0:T(8,128)S(1)}, u32[]{:S(2)}, u32[]{:S(2)}) %collective-permute-start.2) | collective-permute-done | bytes 8224 | tf_op jit(solution)/shard_map/ppermute | solution.py:322
  16.0 0.0 collective-permute-done
  16.1 0.9 %shard_map.70 = f32[48,128]{1,0:T(8,128)S(1)} custom-call(f32[1024,2048]{1,0:T(8,128)S(1)} %get-tuple-element.15.plan_ref, f32[16,128]{1,0:T(8,128)S(1)} %add_add_fusion.3.rows_ref, f32[32,128]{1,0:T(8,128)S(1)} %get-tuple-element.19.cols_ref), custom_call_target="tpu_custom_call" | custom-call | flops 1073741824 | bytes 1048576 | tf_op jit(solution)/shard_map/pallas_call | solution.py:350
  16.9 0.1 collective-permute-start.3
  17.0 1.2 %collective-permute-done.3 = f32[48,128]{1,0:T(8,128)S(1)} collective-permute-done((f32[48,128]{1,0:T(8,128)S(1)}, f32[48,128]{1,0:T(8,128)S(1)}, u32[]{:S(2)}, u32[]{:S(2)}) %collective-permute-start.3) | collective-permute-done | bytes 24608 | tf_op jit(solution)/shard_map/ppermute | solution.py:322
  18.2 1.5 %collective-permute-start.5 = (f32[48,128]{1,0:T(8,128)S(1)}, f32[48,128]{1,0:T(8,128)S(1)}, u32[]{:S(2)}, u32[]{:S(2)}) collective-permute-start(f32[48,128]{1,0:T(8,128)S(1)} %add.66), channel_id=1, source_target_pairs={{0,16},{4,20},{8,24},{12,28},{16,0},{20,4},{24,8},{28,12},{1,17},{... | collective-permute-start | bytes 73736 | tf_op jit(solution)/shard_map/ppermute | solution.py:322
  19.7 1.4 %collective-permute-start.6 = (f32[48,128]{1,0:T(8,128)S(1)}, f32[48,128]{1,0:T(8,128)S(1)}, u32[]{:S(2)}, u32[]{:S(2)}) collective-permute-start(f32[48,128]{1,0:T(8,128)S(1)} %add.66), channel_id=1, source_target_pairs={{0,24},{4,28},{8,16},{12,20},{16,8},{20,12},{24,0},{28,4},{1,25},{... | collective-permute-start | bytes 73736 | tf_op jit(solution)/shard_map/ppermute | solution.py:322
  21.1 0.5 collective-permute-start.4
  21.7 0.3 collective-permute-done.5
  22.0 2.5 %collective-permute-done.6 = f32[48,128]{1,0:T(8,128)S(1)} collective-permute-done((f32[48,128]{1,0:T(8,128)S(1)}, f32[48,128]{1,0:T(8,128)S(1)}, u32[]{:S(2)}, u32[]{:S(2)}) %collective-permute-start.6) | collective-permute-done | bytes 24608 | tf_op jit(solution)/shard_map/ppermute | solution.py:322
  24.6 0.4 collective-permute-done.4
  25.0 0.0 copy-start
  25.0 1.7 %shard_map.71 = f32[16,128]{1,0:T(8,128)S(1)} custom-call(f32[1024,2048]{1,0:T(8,128)S(1)} %get-tuple-element.15.plan_ref, f32[48,128]{1,0:T(8,128)S(1)} %add_add_fusion.cols_ref), custom_call_target="tpu_custom_call" | custom-call | flops 1073741824 | bytes 1048576 | tf_op jit(solution)/shard_map/pallas_call | solution.py:350
  26.7 1.3 %collective-permute-start.8 = (f32[16,128]{1,0:T(8,128)S(1)}, f32[16,128]{1,0:T(8,128)S(1)}, u32[]{:S(2)}, u32[]{:S(2)}) collective-permute-start(f32[16,128]{1,0:T(8,128)S(1)} %shard_map.71), channel_id=1, source_target_pairs={{0,2},{1,3},{2,0},{3,1},{4,6},{5,7},{6,4},{7,5},{8,10},{9,11},{10,... | collective-permute-start | bytes 24584 | tf_op jit(solution)/shard_map/ppermute | solution.py:322
  28.0 0.9 %collective-permute-start.9 = (f32[16,128]{1,0:T(8,128)S(1)}, f32[16,128]{1,0:T(8,128)S(1)}, u32[]{:S(2)}, u32[]{:S(2)}) collective-permute-start(f32[16,128]{1,0:T(8,128)S(1)} %shard_map.71), channel_id=1, source_target_pairs={{0,3},{1,2},{2,1},{3,0},{4,7},{5,6},{6,5},{7,4},{8,11},{9,10},{10,... | collective-permute-start | bytes 24584 | tf_op jit(solution)/shard_map/ppermute | solution.py:322
  28.9 1.3 %collective-permute-start.7 = (f32[16,128]{1,0:T(8,128)S(1)}, f32[16,128]{1,0:T(8,128)S(1)}, u32[]{:S(2)}, u32[]{:S(2)}) collective-permute-start(f32[16,128]{1,0:T(8,128)S(1)} %shard_map.71), channel_id=1, source_target_pairs={{0,1},{1,0},{2,3},{3,2},{4,5},{5,4},{6,7},{7,6},{8,9},{9,8},{10,11... | collective-permute-start | bytes 24584 | tf_op jit(solution)/shard_map/ppermute | solution.py:322
  30.3 1.1 %collective-permute-done.8 = f32[16,128]{1,0:T(8,128)S(1)} collective-permute-done((f32[16,128]{1,0:T(8,128)S(1)}, f32[16,128]{1,0:T(8,128)S(1)}, u32[]{:S(2)}, u32[]{:S(2)}) %collective-permute-start.8) | collective-permute-done | bytes 8224 | tf_op jit(solution)/shard_map/ppermute | solution.py:322
  31.3 2.1 %collective-permute-done.9 = f32[16,128]{1,0:T(8,128)S(1)} collective-permute-done((f32[16,128]{1,0:T(8,128)S(1)}, f32[16,128]{1,0:T(8,128)S(1)}, u32[]{:S(2)}, u32[]{:S(2)}) %collective-permute-start.9) | collective-permute-done | bytes 8224 | tf_op jit(solution)/shard_map/ppermute | solution.py:322
  33.5 0.0 collective-permute-done.7
  33.5 1.6 %shard_map.72 = f32[32,128]{1,0:T(8,128)S(1)} custom-call(f32[1024,2048]{1,0:T(8,128)S(1)} %get-tuple-element.15.plan_ref, f32[16,128]{1,0:T(8,128)S(1)} %add_add_fusion.3.rows_ref, f32[16,128]{1,0:T(8,128)S(1)} %add_add_fusion.2.terms_ref), custom_call_target="tpu_custom_call" | custom-call | flops 1073741824 | bytes 1048576 | tf_op jit(solution)/shard_map/pallas_call | solution.py:350
  35.1 0.1 collective-permute-start.10
  35.2 1.2 %collective-permute-done.10 = f32[32,128]{1,0:T(8,128)S(1)} collective-permute-done((f32[32,128]{1,0:T(8,128)S(1)}, f32[32,128]{1,0:T(8,128)S(1)}, u32[]{:S(2)}, u32[]{:S(2)}) %collective-permute-start.10) | collective-permute-done | bytes 16416 | tf_op jit(solution)/shard_map/ppermute | solution.py:322
  36.4 1.5 %collective-permute-start.12 = (f32[32,128]{1,0:T(8,128)S(1)}, f32[32,128]{1,0:T(8,128)S(1)}, u32[]{:S(2)}, u32[]{:S(2)}) collective-permute-start(f32[32,128]{1,0:T(8,128)S(1)} %add.73), channel_id=1, source_target_pairs={{0,16},{4,20},{8,24},{12,28},{16,0},{20,4},{24,8},{28,12},{1,17},{... | collective-permute-start | bytes 49160 | tf_op jit(solution)/shard_map/ppermute | solution.py:322
  37.9 0.9 %collective-permute-start.13 = (f32[32,128]{1,0:T(8,128)S(1)}, f32[32,128]{1,0:T(8,128)S(1)}, u32[]{:S(2)}, u32[]{:S(2)}) collective-permute-start(f32[32,128]{1,0:T(8,128)S(1)} %add.73), channel_id=1, source_target_pairs={{0,24},{4,28},{8,16},{12,20},{16,8},{20,12},{24,0},{28,4},{1,25},{... | collective-permute-start | bytes 49160 | tf_op jit(solution)/shard_map/ppermute | solution.py:322
  38.8 1.1 %collective-permute-start.11 = (f32[32,128]{1,0:T(8,128)S(1)}, f32[32,128]{1,0:T(8,128)S(1)}, u32[]{:S(2)}, u32[]{:S(2)}) collective-permute-start(f32[32,128]{1,0:T(8,128)S(1)} %add.73), channel_id=1, source_target_pairs={{0,8},{4,12},{8,0},{12,4},{16,24},{20,28},{24,16},{28,20},{1,9},{5... | collective-permute-start | bytes 49160 | tf_op jit(solution)/shard_map/ppermute | solution.py:322
  39.9 0.0 copy-done
  39.9 2.6 %shard_map.69 = (f32[64,1024]{1,0:T(8,128)S(1)}, bf16[2048,128]{1,0:T(8,128)(2,1)S(1)}) custom-call(f32[1024,2048]{1,0:T(8,128)S(1)} %get-tuple-element.15.plan_ref, f32[64,2048]{1,0:T(8,128)S(1)} %bitcast.12), custom_call_target="tpu_custom_call" | custom-call | flops 1073741824 | bytes 1048576 | tf_op jit(solution)/shard_map/pallas_call | solution.py:350
  42.5 0.0 collective-permute-done.12
  42.5 0.0 collective-permute-done.13
  42.5 0.0 collective-permute-done.11
  42.6 0.9 %shard_map.74 = f32[8,128]{1,0:T(8,128)S(1)} custom-call(f32[1024,2048]{1,0:T(8,128)S(1)} %get-tuple-element.15.plan_ref, f32[48,128]{1,0:T(8,128)S(1)} %add_add_fusion.cols_ref, f32[32,128]{1,0:T(8,128)S(1)} %add_add_fusion.1.bterms_ref.terms_ref), custom_call_target="tpu_custom_call" | custom-call | flops 1073741824 | bytes 1048576 | tf_op jit(solution)/shard_map/pallas_call | solution.py:350
  43.4 1.1 %collective-permute-start.15 = (f32[8,128]{1,0:T(8,128)S(1)}, f32[8,128]{1,0:T(8,128)S(1)}, u32[]{:S(2)}, u32[]{:S(2)}) collective-permute-start(f32[8,128]{1,0:T(8,128)S(1)} %shard_map.74), channel_id=1, source_target_pairs={{0,2},{1,3},{2,0},{3,1},{4,6},{5,7},{6,4},{7,5},{8,10},{9,11},{10,... | collective-permute-start | bytes 12296 | tf_op jit(solution)/shard_map/ppermute | solution.py:322
  44.5 1.8 %collective-permute-start.16 = (f32[8,128]{1,0:T(8,128)S(1)}, f32[8,128]{1,0:T(8,128)S(1)}, u32[]{:S(2)}, u32[]{:S(2)}) collective-permute-start(f32[8,128]{1,0:T(8,128)S(1)} %shard_map.74), channel_id=1, source_target_pairs={{0,3},{1,2},{2,1},{3,0},{4,7},{5,6},{6,5},{7,4},{8,11},{9,10},{10,... | collective-permute-start | bytes 12296 | tf_op jit(solution)/shard_map/ppermute | solution.py:322
  46.3 0.7 collective-permute-start.14
  47.0 0.0 copy-start.1
  47.0 2.8 %shard_map.73 = (f32[64,1024]{1,0:T(8,128)S(1)}, f32[8,2048]{1,0:T(8,128)S(1)}) custom-call(f32[1024,2048]{1,0:T(8,128)S(1)} %get-tuple-element.15.plan_ref, f32[1024,2048]{1,0:T(8,128)S(1)} %get-tuple-element.16.cot_ref, bf16[2048,128]{1,0:T(8,128)(2,1)S(1)} %get-tuple-element.17.right_ref, f32[48,128]{1,0:T(8,128)S(1)} %add_add_fusion.cols_ref, ...), custom_call_target="tpu_custom_call" | custom-call | flops 1073741824 | bytes 1048576 | tf_op jit(solution)/shard_map/pallas_call | solution.py:350
  49.8 0.0 collective-permute-done.15
  49.8 0.1 collective-permute-done.16
  49.9 0.0 collective-permute-done.14
  50.0 0.0 copy-done.1
  50.0 2.5 %shard_map.76 = f32[8,64,256]{2,1,0:T(8,128)S(1)} custom-call(f32[1024,2048]{1,0:T(8,128)S(1)} %get-tuple-element.15.plan_ref, f32[1024,2048]{1,0:T(8,128)S(1)} %get-tuple-element.16.cot_ref, f32[64,1024]{1,0:T(8,128)S(1)} %bitcast.14, f32[8,128]{1,0:T(8,128)S(1)} %get-tuple-element.24.alpha_ref, f32[8,2048]{1,0:T(8,128)S(1)} %get-tuple-element.25.beta_ref), custom_call_target="tpu_custom_call" | custom-call | flops 8589934592 | bytes 1048576 | tf_op jit(solution)/shard_map/pallas_call | solution.py:350
  52.6 0.1 collective-permute-start.20
  52.6 1.3 %collective-permute-start.17 = (f32[2,64,256]{2,1,0:T(8,128)S(1)}, f32[2,64,256]{2,1,0:T(8,128)S(1)}, u32[]{:S(2)}, u32[]{:S(2)}) collective-permute-start(f32[2,64,256]{2,1,0:T(8,128)S(1)} %get-tuple-element.23), channel_id=1, source_target_pairs={{0,1},{1,0},{2,3},{3,2},{4,5},{5,4},{6,7},{7,6},{8,9},{9,8},{10,11... | collective-permute-start | bytes 393224 | tf_op jit(solution)/shard_map/ppermute | solution.py:322
  53.9 4.6 %collective-permute-done.17 = f32[2,64,256]{2,1,0:T(8,128)S(1)} collective-permute-done((f32[2,64,256]{2,1,0:T(8,128)S(1)}, f32[2,64,256]{2,1,0:T(8,128)S(1)}, u32[]{:S(2)}, u32[]{:S(2)}) %collective-permute-start.17) | collective-permute-done | bytes 131104 | tf_op jit(solution)/shard_map/ppermute | solution.py:322
  58.6 1.9 %collective-permute-start.18 = (f32[2,64,256]{2,1,0:T(8,128)S(1)}, f32[2,64,256]{2,1,0:T(8,128)S(1)}, u32[]{:S(2)}, u32[]{:S(2)}) collective-permute-start(f32[2,64,256]{2,1,0:T(8,128)S(1)} %add.80), channel_id=1, source_target_pairs={{0,2},{1,3},{2,0},{3,1},{4,6},{5,7},{6,4},{7,5},{8,10},{9,11},{10,... | collective-permute-start | bytes 393224 | tf_op jit(solution)/shard_map/ppermute | solution.py:322
  60.4 0.0 collective-permute-done.20
  60.5 1.1 %collective-permute-start.21 = (f32[2,64,256]{2,1,0:T(8,128)S(1)}, f32[2,64,256]{2,1,0:T(8,128)S(1)}, u32[]{:S(2)}, u32[]{:S(2)}) collective-permute-start(f32[2,64,256]{2,1,0:T(8,128)S(1)} %slice.27), channel_id=1, source_target_pairs={{0,8},{4,12},{8,0},{12,4},{16,24},{20,28},{24,16},{28,20},{1,9},{5... | collective-permute-start | bytes 393224 | tf_op jit(solution)/shard_map/ppermute | solution.py:322
  61.6 5.7 %collective-permute-done.18 = f32[2,64,256]{2,1,0:T(8,128)S(1)} collective-permute-done((f32[2,64,256]{2,1,0:T(8,128)S(1)}, f32[2,64,256]{2,1,0:T(8,128)S(1)}, u32[]{:S(2)}, u32[]{:S(2)}) %collective-permute-start.18) | collective-permute-done | bytes 131104 | tf_op jit(solution)/shard_map/ppermute | solution.py:322
  67.3 0.1 collective-permute-start.19
  67.4 0.0 collective-permute-done.21
  67.5 1.6 %collective-permute-start.22 = (f32[64,256]{1,0:T(8,128)S(1)}, f32[64,256]{1,0:T(8,128)S(1)}, u32[]{:S(2)}, u32[]{:S(2)}) collective-permute-start(f32[64,256]{1,0:T(8,128)S(1)} %get-tuple-element.28), channel_id=1, source_target_pairs={{0,16},{4,20},{8,24},{12,28},{16,0},{20,4},{24,8},{28,12},{1,17},{... | collective-permute-start | bytes 196616 | tf_op jit(solution)/shard_map/ppermute | solution.py:322
  69.0 3.3 %collective-permute-done.19.got_ref = f32[2,64,256]{2,1,0:T(8,128)S(1)} collective-permute-done((f32[2,64,256]{2,1,0:T(8,128)S(1)}, f32[2,64,256]{2,1,0:T(8,128)S(1)}, u32[]{:S(2)}, u32[]{:S(2)}) %collective-permute-start.19) | collective-permute-done | bytes 131104 | tf_op jit(solution)/shard_map/ppermute | solution.py:322
  72.4 0.0 collective-permute-done.22.theirs_ref
  72.4 0.7 %shard_map.77 = (f32[64,1024]{1,0:T(8,128)}, f32[64,256]{1,0:T(8,128)}) custom-call(f32[2,64,256]{2,1,0:T(8,128)S(1)} %add.81.own_ref, f32[2,64,256]{2,1,0:T(8,128)S(1)} %collective-permute-done.19.got_ref, f32[64,256]{1,0:T(8,128)S(1)} %get-tuple-element.29.mine_ref, f32[64,256]{1,0:T(8,128)S(1)} %collective-permute-done.22.theirs_ref), custom_call_target="tpu_custom_call" | custom-call | flops 1073741824 | bytes 1048576 | tf_op jit(solution)/shard_map/pallas_call | solution.py:350
  (15 shorter events, 0.2 us)
Async XLA Ops:
  6.5 5.8 %collective-permute-start.1 = (f32[16,128]{1,0:T(8,128)S(1)}, f32[16,128]{1,0:T(8,128)S(1)}, u32[]{:S(2)}, u32[]{:S(2)}) collective-permute-start(f32[16,128]{1,0:T(8,128)S(1)} %get-tuple-element.18), channel_id=1, source_target_pairs={{0,2},{1,3},{2,0},{3,1},{4,6},{5,7},{6,4},{7,5},{8,10},{9,11},{10,... | collective-permute-start | bytes 24584 | tf_op jit(solution)/shard_map/ppermute | solution.py:322
  10.6 5.4 %collective-permute-start.2 = (f32[16,128]{1,0:T(8,128)S(1)}, f32[16,128]{1,0:T(8,128)S(1)}, u32[]{:S(2)}, u32[]{:S(2)}) collective-permute-start(f32[16,128]{1,0:T(8,128)S(1)} %get-tuple-element.18), channel_id=1, source_target_pairs={{0,3},{1,2},{2,1},{3,0},{4,7},{5,6},{6,5},{7,4},{8,11},{9,10},{10,... | collective-permute-start | bytes 24584 | tf_op jit(solution)/shard_map/ppermute | solution.py:322
  11.9 4.1 %collective-permute-start = (f32[16,128]{1,0:T(8,128)S(1)}, f32[16,128]{1,0:T(8,128)S(1)}, u32[]{:S(2)}, u32[]{:S(2)}) collective-permute-start(f32[16,128]{1,0:T(8,128)S(1)} %get-tuple-element.18), channel_id=1, source_target_pairs={{0,1},{1,0},{2,3},{3,2},{4,5},{5,4},{6,7},{7,6},{8,9},{9,8},{10,11... | collective-permute-start | bytes 24584 | tf_op jit(solution)/shard_map/ppermute | solution.py:322
  16.9 1.3 %collective-permute-start.3 = (f32[48,128]{1,0:T(8,128)S(1)}, f32[48,128]{1,0:T(8,128)S(1)}, u32[]{:S(2)}, u32[]{:S(2)}) collective-permute-start(f32[48,128]{1,0:T(8,128)S(1)} %shard_map.70), channel_id=1, source_target_pairs={{0,4},{4,0},{8,12},{12,8},{16,20},{20,16},{24,28},{28,24},{1,5},{5... | collective-permute-start | bytes 73736 | tf_op jit(solution)/shard_map/ppermute | solution.py:322
  18.2 3.8 %collective-permute-start.5 = (f32[48,128]{1,0:T(8,128)S(1)}, f32[48,128]{1,0:T(8,128)S(1)}, u32[]{:S(2)}, u32[]{:S(2)}) collective-permute-start(f32[48,128]{1,0:T(8,128)S(1)} %add.66), channel_id=1, source_target_pairs={{0,16},{4,20},{8,24},{12,28},{16,0},{20,4},{24,8},{28,12},{1,17},{... | collective-permute-start | bytes 73736 | tf_op jit(solution)/shard_map/ppermute | solution.py:322
  19.7 4.9 %collective-permute-start.6 = (f32[48,128]{1,0:T(8,128)S(1)}, f32[48,128]{1,0:T(8,128)S(1)}, u32[]{:S(2)}, u32[]{:S(2)}) collective-permute-start(f32[48,128]{1,0:T(8,128)S(1)} %add.66), channel_id=1, source_target_pairs={{0,24},{4,28},{8,16},{12,20},{16,8},{20,12},{24,0},{28,4},{1,25},{... | collective-permute-start | bytes 73736 | tf_op jit(solution)/shard_map/ppermute | solution.py:322
  21.1 3.8 %collective-permute-start.4 = (f32[48,128]{1,0:T(8,128)S(1)}, f32[48,128]{1,0:T(8,128)S(1)}, u32[]{:S(2)}, u32[]{:S(2)}) collective-permute-start(f32[48,128]{1,0:T(8,128)S(1)} %add.66), channel_id=1, source_target_pairs={{0,8},{4,12},{8,0},{12,4},{16,24},{20,28},{24,16},{28,20},{1,9},{5... | collective-permute-start | bytes 73736 | tf_op jit(solution)/shard_map/ppermute | solution.py:322
  25.0 14.9 %copy-start = (f32[2048,64]{0,1:T(8,128)S(1)}, f32[2048,64]{0,1:T(8,128)}, u32[]{:S(2)}) copy-start(f32[2048,64]{0,1:T(8,128)} %param.6) | copy-start | bytes 1572868
  26.7 4.6 %collective-permute-start.8 = (f32[16,128]{1,0:T(8,128)S(1)}, f32[16,128]{1,0:T(8,128)S(1)}, u32[]{:S(2)}, u32[]{:S(2)}) collective-permute-start(f32[16,128]{1,0:T(8,128)S(1)} %shard_map.71), channel_id=1, source_target_pairs={{0,2},{1,3},{2,0},{3,1},{4,6},{5,7},{6,4},{7,5},{8,10},{9,11},{10,... | collective-permute-start | bytes 24584 | tf_op jit(solution)/shard_map/ppermute | solution.py:322
  28.0 5.4 %collective-permute-start.9 = (f32[16,128]{1,0:T(8,128)S(1)}, f32[16,128]{1,0:T(8,128)S(1)}, u32[]{:S(2)}, u32[]{:S(2)}) collective-permute-start(f32[16,128]{1,0:T(8,128)S(1)} %shard_map.71), channel_id=1, source_target_pairs={{0,3},{1,2},{2,1},{3,0},{4,7},{5,6},{6,5},{7,4},{8,11},{9,10},{10,... | collective-permute-start | bytes 24584 | tf_op jit(solution)/shard_map/ppermute | solution.py:322
  28.9 4.5 %collective-permute-start.7 = (f32[16,128]{1,0:T(8,128)S(1)}, f32[16,128]{1,0:T(8,128)S(1)}, u32[]{:S(2)}, u32[]{:S(2)}) collective-permute-start(f32[16,128]{1,0:T(8,128)S(1)} %shard_map.71), channel_id=1, source_target_pairs={{0,1},{1,0},{2,3},{3,2},{4,5},{5,4},{6,7},{7,6},{8,9},{9,8},{10,11... | collective-permute-start | bytes 24584 | tf_op jit(solution)/shard_map/ppermute | solution.py:322
  35.1 1.2 %collective-permute-start.10 = (f32[32,128]{1,0:T(8,128)S(1)}, f32[32,128]{1,0:T(8,128)S(1)}, u32[]{:S(2)}, u32[]{:S(2)}) collective-permute-start(f32[32,128]{1,0:T(8,128)S(1)} %shard_map.72), channel_id=1, source_target_pairs={{0,4},{4,0},{8,12},{12,8},{16,20},{20,16},{24,28},{28,24},{1,5},{5... | collective-permute-start | bytes 49160 | tf_op jit(solution)/shard_map/ppermute | solution.py:322
  36.4 6.1 %collective-permute-start.12 = (f32[32,128]{1,0:T(8,128)S(1)}, f32[32,128]{1,0:T(8,128)S(1)}, u32[]{:S(2)}, u32[]{:S(2)}) collective-permute-start(f32[32,128]{1,0:T(8,128)S(1)} %add.73), channel_id=1, source_target_pairs={{0,16},{4,20},{8,24},{12,28},{16,0},{20,4},{24,8},{28,12},{1,17},{... | collective-permute-start | bytes 49160 | tf_op jit(solution)/shard_map/ppermute | solution.py:322
  37.9 4.6 %collective-permute-start.13 = (f32[32,128]{1,0:T(8,128)S(1)}, f32[32,128]{1,0:T(8,128)S(1)}, u32[]{:S(2)}, u32[]{:S(2)}) collective-permute-start(f32[32,128]{1,0:T(8,128)S(1)} %add.73), channel_id=1, source_target_pairs={{0,24},{4,28},{8,16},{12,20},{16,8},{20,12},{24,0},{28,4},{1,25},{... | collective-permute-start | bytes 49160 | tf_op jit(solution)/shard_map/ppermute | solution.py:322
  38.8 3.7 %collective-permute-start.11 = (f32[32,128]{1,0:T(8,128)S(1)}, f32[32,128]{1,0:T(8,128)S(1)}, u32[]{:S(2)}, u32[]{:S(2)}) collective-permute-start(f32[32,128]{1,0:T(8,128)S(1)} %add.73), channel_id=1, source_target_pairs={{0,8},{4,12},{8,0},{12,4},{16,24},{20,28},{24,16},{28,20},{1,9},{5... | collective-permute-start | bytes 49160 | tf_op jit(solution)/shard_map/ppermute | solution.py:322
  43.4 6.4 %collective-permute-start.15 = (f32[8,128]{1,0:T(8,128)S(1)}, f32[8,128]{1,0:T(8,128)S(1)}, u32[]{:S(2)}, u32[]{:S(2)}) collective-permute-start(f32[8,128]{1,0:T(8,128)S(1)} %shard_map.74), channel_id=1, source_target_pairs={{0,2},{1,3},{2,0},{3,1},{4,6},{5,7},{6,4},{7,5},{8,10},{9,11},{10,... | collective-permute-start | bytes 12296 | tf_op jit(solution)/shard_map/ppermute | solution.py:322
  44.5 5.4 %collective-permute-start.16 = (f32[8,128]{1,0:T(8,128)S(1)}, f32[8,128]{1,0:T(8,128)S(1)}, u32[]{:S(2)}, u32[]{:S(2)}) collective-permute-start(f32[8,128]{1,0:T(8,128)S(1)} %shard_map.74), channel_id=1, source_target_pairs={{0,3},{1,2},{2,1},{3,0},{4,7},{5,6},{6,5},{7,4},{8,11},{9,10},{10,... | collective-permute-start | bytes 12296 | tf_op jit(solution)/shard_map/ppermute | solution.py:322
  46.3 3.6 %collective-permute-start.14 = (f32[8,128]{1,0:T(8,128)S(1)}, f32[8,128]{1,0:T(8,128)S(1)}, u32[]{:S(2)}, u32[]{:S(2)}) collective-permute-start(f32[8,128]{1,0:T(8,128)S(1)} %shard_map.74), channel_id=1, source_target_pairs={{0,1},{1,0},{2,3},{3,2},{4,5},{5,4},{6,7},{7,6},{8,9},{9,8},{10,11... | collective-permute-start | bytes 12296 | tf_op jit(solution)/shard_map/ppermute | solution.py:322
  47.0 3.0 %copy-start.1 = (f32[1024,64]{0,1:T(8,128)S(1)}, f32[1024,64]{0,1:T(8,128)}, u32[]{:S(2)}) copy-start(f32[1024,64]{0,1:T(8,128)} %param.5) | copy-start | bytes 786436
  52.6 7.9 %collective-permute-start.20 = (f32[4,64,256]{2,1,0:T(8,128)S(1)}, f32[4,64,256]{2,1,0:T(8,128)S(1)}, u32[]{:S(2)}, u32[]{:S(2)}) collective-permute-start(f32[4,64,256]{2,1,0:T(8,128)S(1)} %slice.25), channel_id=1, source_target_pairs={{0,4},{4,0},{8,12},{12,8},{16,20},{20,16},{24,28},{28,24},{1,5},{5... | collective-permute-start | bytes 786440 | tf_op jit(solution)/shard_map/ppermute | solution.py:322
  52.6 5.9 %collective-permute-start.17 = (f32[2,64,256]{2,1,0:T(8,128)S(1)}, f32[2,64,256]{2,1,0:T(8,128)S(1)}, u32[]{:S(2)}, u32[]{:S(2)}) collective-permute-start(f32[2,64,256]{2,1,0:T(8,128)S(1)} %get-tuple-element.23), channel_id=1, source_target_pairs={{0,1},{1,0},{2,3},{3,2},{4,5},{5,4},{6,7},{7,6},{8,9},{9,8},{10,11... | collective-permute-start | bytes 393224 | tf_op jit(solution)/shard_map/ppermute | solution.py:322
  58.6 8.7 %collective-permute-start.18 = (f32[2,64,256]{2,1,0:T(8,128)S(1)}, f32[2,64,256]{2,1,0:T(8,128)S(1)}, u32[]{:S(2)}, u32[]{:S(2)}) collective-permute-start(f32[2,64,256]{2,1,0:T(8,128)S(1)} %add.80), channel_id=1, source_target_pairs={{0,2},{1,3},{2,0},{3,1},{4,6},{5,7},{6,4},{7,5},{8,10},{9,11},{10,... | collective-permute-start | bytes 393224 | tf_op jit(solution)/shard_map/ppermute | solution.py:322
  60.5 6.9 %collective-permute-start.21 = (f32[2,64,256]{2,1,0:T(8,128)S(1)}, f32[2,64,256]{2,1,0:T(8,128)S(1)}, u32[]{:S(2)}, u32[]{:S(2)}) collective-permute-start(f32[2,64,256]{2,1,0:T(8,128)S(1)} %slice.27), channel_id=1, source_target_pairs={{0,8},{4,12},{8,0},{12,4},{16,24},{20,28},{24,16},{28,20},{1,9},{5... | collective-permute-start | bytes 393224 | tf_op jit(solution)/shard_map/ppermute | solution.py:322
  67.3 5.0 %collective-permute-start.19 = (f32[2,64,256]{2,1,0:T(8,128)S(1)}, f32[2,64,256]{2,1,0:T(8,128)S(1)}, u32[]{:S(2)}, u32[]{:S(2)}) collective-permute-start(f32[2,64,256]{2,1,0:T(8,128)S(1)} %add.81.own_ref), channel_id=1, source_target_pairs={{0,1},{1,0},{2,3},{3,2},{4,5},{5,4},{6,7},{7,6},{8,9},{9,8},{10,11... | collective-permute-start | bytes 393224 | tf_op jit(solution)/shard_map/ppermute | solution.py:322
  67.5 4.9 %collective-permute-start.22 = (f32[64,256]{1,0:T(8,128)S(1)}, f32[64,256]{1,0:T(8,128)S(1)}, u32[]{:S(2)}, u32[]{:S(2)}) collective-permute-start(f32[64,256]{1,0:T(8,128)S(1)} %get-tuple-element.28), channel_id=1, source_target_pairs={{0,16},{4,20},{8,24},{12,28},{16,0},{20,4},{24,8},{28,12},{1,17},{... | collective-permute-start | bytes 196616 | tf_op jit(solution)/shard_map/ppermute | solution.py:322

commit v4 on v3

--- a/solution.py
+++ b/solution.py
@@ -269,16 +269,18 @@
         fold_into(out_ref, at, total[:LANES] + total[LANES:])
 
 
-def post_kernel(pre_ref, bary_ref, rows_ref, aterms_ref, keep_ref, send_ref, alpha_ref, flat_ref):
+def post_kernel(pre_ref, bary_ref, rows_ref, aterms_ref, *out_refs):
+    *piece_refs, alpha_ref, flat_ref = out_refs
     groups = rows_ref.shape[0] // 2
     alpha_ref[...] = (rows_ref[groups:, :] - aterms_ref[...]) / rows_ref[:groups, :]
     flat_row(alpha_ref[...], flat_ref)
-    half, _, span = keep_ref.shape
+    quarter, _, span = piece_refs[0].shape
+    half = 2 * quarter
     me = lax.axis_index("cen") & (half - 1)
     for q in range(2 * half):
         at = pl.ds(pl.multiple_of((me ^ reverse_bits(q, 2 * half)) * span, span), span)
-        to_ref = keep_ref if q < half else send_ref
-        to_ref[q % half] = pre_ref[:, at] - flat_ref[:, at] * bary_ref[:, at]
+        to_ref = piece_refs[q % 2 if q < half else 2 + q % 2]
+        to_ref[q % half // 2] = pre_ref[:, at] - flat_ref[:, at] * bary_ref[:, at]
 
 
 def cen_kernel(plan_ref, cot_ref, emb_ref, alpha_ref, beta_ref, gcen_ref, spread_ref):
@@ -306,15 +308,16 @@
             ]
 
 
-def last_kernel(own_ref, got_ref, mine_ref, theirs_ref, emb_ref, cen_ref):
-    half, _, span = own_ref.shape
-    chunks = 2 * half
+def last_kernel(*refs):
+    *piece_refs, mine_ref, theirs_ref, emb_ref, cen_ref = refs
+    quarter, _, span = piece_refs[0].shape
+    half = 2 * quarter
     me = lax.axis_index("cen") & (half - 1)
-    for q in range(chunks):
-        place = me ^ reverse_bits(q, chunks)
+    for q in range(2 * half):
+        place = me ^ reverse_bits(q, 2 * half)
         at = pl.ds(pl.multiple_of(place * span, span), span)
-        from_ref = own_ref if q < half else got_ref
-        emb_ref[:, at] = from_ref[q % half]
+        from_ref = piece_refs[q % 2 if q < half else 2 + q % 2]
+        emb_ref[:, at] = from_ref[q % half // 2]
     cen_ref[...] = mine_ref[...] + theirs_ref[...]
 
 
@@ -413,13 +416,7 @@
         col_all,
     )
     bary, right = call(
-        bary_kernel,
-        (pltpu.VMEM((width, rows), F32), pltpu.VMEM((cols, LANES), BF16)),
-        [],
-        12,
-        [VMEM] * 2,
-        plan,
-        ctr,
+        bary_kernel, (pltpu.VMEM((width, rows), F32), pltpu.VMEM((cols, LANES), BF16)), [], 12, [VMEM] * 2, plan, ctr
     )
     row_terms = sum_all(row_terms, "cen", cen, 2)
     col_terms = call(
@@ -456,13 +453,9 @@
         col_terms,
     )
     last_terms = sum_all(last_terms, "cen", cen, 2)
-    gemb, sent, alpha = call(
+    *pieces, alpha = call(
         post_kernel,
-        (
-            pltpu.VMEM((cen // 2, width, rows // cen), F32),
-            pltpu.VMEM((cen // 2, width, rows // cen), F32),
-            pltpu.VMEM((groups, LANES), F32),
-        ),
+        (pltpu.VMEM((cen // 4, width, rows // cen), F32),) * 4 + (pltpu.VMEM((groups, LANES), F32),),
         [pltpu.VMEM((1, rows), F32)],
         6,
         [VMEM] * 4,
@@ -471,7 +464,8 @@
         row_sums,
         last_terms,
     )
-    sent = swap(sent, "cen", cen, 1)
+    even = swap(pieces[2], "cen", cen, 1)
+    odd = swap(pieces[3], "cen", cen, 1)
     gcen = call(
         cen_kernel,
         pltpu.VMEM((pts, width, cols // pts), F32),
@@ -486,14 +480,17 @@
         flops=1 << 33,
     )
     cbits, pbits = bits_of(cen), bits_of(pts)
-    gemb = gemb + sent
-    for bit in cbits[1:-1]:
-        keep = gemb.shape[0] // 2
-        gemb = gemb[:keep] + swap(gemb[keep:], "cen", cen, bit)
-    gemb = gemb + swap(gemb, "cen", cen, cbits[-1])
-    for bit in reversed(cbits[1:-1]):
-        gemb = jnp.concatenate([gemb, swap(gemb, "cen", cen, bit)], axis=0)
-    got = swap(gemb, "cen", cen, cbits[0])
+    owns, gots = [], []
+    for own, sent in ((pieces[0], even), (pieces[1], odd)):
+        own = own + sent
+        for bit in cbits[1:-1]:
+            keep = own.shape[0] // 2
+            own = own[:keep] + swap(own[keep:], "cen", cen, bit)
+        own = own + swap(own, "cen", cen, cbits[-1])
+        for bit in reversed(cbits[1:-1]):
+            own = jnp.concatenate([own, swap(own, "cen", cen, bit)], axis=0)
+        owns.append(own)
+        gots.append(swap(own, "cen", cen, cbits[0]))
     for bit in pbits[:-1]:
         keep = gcen.shape[0] // 2
         gcen = gcen[:keep] + swap(gcen[keep:], "pts", pts, bit)
@@ -503,9 +500,9 @@
         (sds((width, rows), F32), sds((width, cols // pts), F32)),
         [],
         6,
-        [VMEM] * 4,
-        gemb,
-        got,
+        [VMEM] * 6,
+        *owns,
+        *gots,
         gcen[0],
         theirs,
     )

time: 73.3 us -> 72.8 us (level)
  waiting for transfers between devices: 26.5 us -> 22.6 us
  starting transfers between devices: 25.9 us -> 29.4 us
    ppermute x23 -> x26, waiting for transfers between devices: 26.5 us -> 22.6 us  [swap(): return lax.ppermute(value, axis, [(i, i ^ bit) for i in range(count)])]
    ppermute x23 -> x26, starting transfers between devices: 25.9 us -> 29.4 us  [swap(): return lax.ppermute(value, axis, [(i, i ^ bit) for i in range(count)])]
  transfers between devices with their start and end apart: 23 -> 26, of which waited for: 12 -> 15; matrix products, arithmetic and copies ran while one was open for 0% -> 0% of each run, Pallas kernels for 7% -> 7%
where the time goes in v4:
time: 72.8 us; the launch traced here: 72.6 us
  starting transfers between devices  29.4 us (40%)
  waiting for transfers between devices  22.6 us (31%)
  Pallas kernels  19.6 us (27%)
  between operations  0.83 us (1%)
    ppermute x26, starting transfers between devices, swap(): return lax.ppermute(value, axis, [(i, i ^ bit) for i in range(count)])  29.4 us
    ppermute x26, waiting for transfers between devices, swap(): return lax.ppermute(value, axis, [(i, i ^ bit) for i in range(count)])  22.6 us
    pallas_call x10, Pallas kernels, call(): pl.pallas_call(body, out_shape=outs, in_specs=specs, out_specs=jax.tree.m...  19.6 us
  transfers between devices with their start and end apart: 26, of which 15 were waited for; matrix products, arithmetic and copies ran while one was open for 0% of the time, Pallas kernels for 7%

profile of v4, /device:TPU:0, one launch (start us, length us, event | category | flops | bytes accessed | tf_op | source)
XLA Modules:
  0.0 72.6 jit_solution(13277243376478544618)
XLA Ops:
  0.6 5.8 %shard_map.68 = (f32[1024,2048]{1,0:T(8,128)S(1)}, f32[1024,2048]{1,0:T(8,128)S(1)}, f32[16,128]{1,0:T(8,128)S(1)}, f32[32,128]{1,0:T(8,128)S(1)}) custom-call(f32[64,1024]{1,0:T(8,128)} %bitcast.13, f32[64,1024]{1,0:T(8,128)} %bitcast.15, f32[64,2048]{1,0:T(8,128)} %bitcast.11, f32[8,128]{1,0:T(8,128)} %bitcast.17, f32[16,128]{1,0:T(8,128)} %bitcast.16), custom_call_target="tpu_custom_call" | custom-call | flops 1073741824 | bytes 1048576 | tf_op jit(solution)/shard_map/pallas_call | solution.py:353
  6.5 4.1 %collective-permute-start.1 = (f32[16,128]{1,0:T(8,128)S(1)}, f32[16,128]{1,0:T(8,128)S(1)}, u32[]{:S(2)}, u32[]{:S(2)}) collective-permute-start(f32[16,128]{1,0:T(8,128)S(1)} %get-tuple-element.20), channel_id=1, source_target_pairs={{0,2},{1,3},{2,0},{3,1},{4,6},{5,7},{6,4},{7,5},{8,10},{9,11},{10,... | collective-permute-start | bytes 24584 | tf_op jit(solution)/shard_map/ppermute | solution.py:325
  10.6 1.3 %collective-permute-start.2 = (f32[16,128]{1,0:T(8,128)S(1)}, f32[16,128]{1,0:T(8,128)S(1)}, u32[]{:S(2)}, u32[]{:S(2)}) collective-permute-start(f32[16,128]{1,0:T(8,128)S(1)} %get-tuple-element.20), channel_id=1, source_target_pairs={{0,3},{1,2},{2,1},{3,0},{4,7},{5,6},{6,5},{7,4},{8,11},{9,10},{10,... | collective-permute-start | bytes 24584 | tf_op jit(solution)/shard_map/ppermute | solution.py:325
  11.9 0.2 collective-permute-start
  12.2 0.0 collective-permute-done.1
  12.2 3.8 %collective-permute-done.2 = f32[16,128]{1,0:T(8,128)S(1)} collective-permute-done((f32[16,128]{1,0:T(8,128)S(1)}, f32[16,128]{1,0:T(8,128)S(1)}, u32[]{:S(2)}, u32[]{:S(2)}) %collective-permute-start.2) | collective-permute-done | bytes 8224 | tf_op jit(solution)/shard_map/ppermute | solution.py:325
  16.0 0.0 collective-permute-done
  16.1 0.9 %shard_map.70 = f32[48,128]{1,0:T(8,128)S(1)} custom-call(f32[1024,2048]{1,0:T(8,128)S(1)} %get-tuple-element.17.plan_ref, f32[16,128]{1,0:T(8,128)S(1)} %add_add_fusion.3.rows_ref, f32[32,128]{1,0:T(8,128)S(1)} %get-tuple-element.21.cols_ref), custom_call_target="tpu_custom_call" | custom-call | flops 1073741824 | bytes 1048576 | tf_op jit(solution)/shard_map/pallas_call | solution.py:353
  16.9 0.1 collective-permute-start.3
  17.0 1.2 %collective-permute-done.3 = f32[48,128]{1,0:T(8,128)S(1)} collective-permute-done((f32[48,128]{1,0:T(8,128)S(1)}, f32[48,128]{1,0:T(8,128)S(1)}, u32[]{:S(2)}, u32[]{:S(2)}) %collective-permute-start.3) | collective-permute-done | bytes 24608 | tf_op jit(solution)/shard_map/ppermute | solution.py:325
  18.2 1.5 %collective-permute-start.5 = (f32[48,128]{1,0:T(8,128)S(1)}, f32[48,128]{1,0:T(8,128)S(1)}, u32[]{:S(2)}, u32[]{:S(2)}) collective-permute-start(f32[48,128]{1,0:T(8,128)S(1)} %add.72), channel_id=1, source_target_pairs={{0,16},{4,20},{8,24},{12,28},{16,0},{20,4},{24,8},{28,12},{1,17},{... | collective-permute-start | bytes 73736 | tf_op jit(solution)/shard_map/ppermute | solution.py:325
  19.7 1.4 %collective-permute-start.6 = (f32[48,128]{1,0:T(8,128)S(1)}, f32[48,128]{1,0:T(8,128)S(1)}, u32[]{:S(2)}, u32[]{:S(2)}) collective-permute-start(f32[48,128]{1,0:T(8,128)S(1)} %add.72), channel_id=1, source_target_pairs={{0,24},{4,28},{8,16},{12,20},{16,8},{20,12},{24,0},{28,4},{1,25},{... | collective-permute-start | bytes 73736 | tf_op jit(solution)/shard_map/ppermute | solution.py:325
  21.1 0.5 collective-permute-start.4
  21.7 0.3 collective-permute-done.5
  22.0 2.5 %collective-permute-done.6 = f32[48,128]{1,0:T(8,128)S(1)} collective-permute-done((f32[48,128]{1,0:T(8,128)S(1)}, f32[48,128]{1,0:T(8,128)S(1)}, u32[]{:S(2)}, u32[]{:S(2)}) %collective-permute-start.6) | collective-permute-done | bytes 24608 | tf_op jit(solution)/shard_map/ppermute | solution.py:325
  24.6 0.4 collective-permute-done.4
  25.0 0.0 copy-start
  25.0 1.7 %shard_map.71 = f32[16,128]{1,0:T(8,128)S(1)} custom-call(f32[1024,2048]{1,0:T(8,128)S(1)} %get-tuple-element.17.plan_ref, f32[48,128]{1,0:T(8,128)S(1)} %add_add_fusion.cols_ref), custom_call_target="tpu_custom_call" | custom-call | flops 1073741824 | bytes 1048576 | tf_op jit(solution)/shard_map/pallas_call | solution.py:353
  26.7 1.3 %collective-permute-start.8 = (f32[16,128]{1,0:T(8,128)S(1)}, f32[16,128]{1,0:T(8,128)S(1)}, u32[]{:S(2)}, u32[]{:S(2)}) collective-permute-start(f32[16,128]{1,0:T(8,128)S(1)} %shard_map.71), channel_id=1, source_target_pairs={{0,2},{1,3},{2,0},{3,1},{4,6},{5,7},{6,4},{7,5},{8,10},{9,11},{10,... | collective-permute-start | bytes 24584 | tf_op jit(solution)/shard_map/ppermute | solution.py:325
  28.0 0.9 %collective-permute-start.9 = (f32[16,128]{1,0:T(8,128)S(1)}, f32[16,128]{1,0:T(8,128)S(1)}, u32[]{:S(2)}, u32[]{:S(2)}) collective-permute-start(f32[16,128]{1,0:T(8,128)S(1)} %shard_map.71), channel_id=1, source_target_pairs={{0,3},{1,2},{2,1},{3,0},{4,7},{5,6},{6,5},{7,4},{8,11},{9,10},{10,... | collective-permute-start | bytes 24584 | tf_op jit(solution)/shard_map/ppermute | solution.py:325
  28.9 1.3 %collective-permute-start.7 = (f32[16,128]{1,0:T(8,128)S(1)}, f32[16,128]{1,0:T(8,128)S(1)}, u32[]{:S(2)}, u32[]{:S(2)}) collective-permute-start(f32[16,128]{1,0:T(8,128)S(1)} %shard_map.71), channel_id=1, source_target_pairs={{0,1},{1,0},{2,3},{3,2},{4,5},{5,4},{6,7},{7,6},{8,9},{9,8},{10,11... | collective-permute-start | bytes 24584 | tf_op jit(solution)/shard_map/ppermute | solution.py:325
  30.3 1.1 %collective-permute-done.8 = f32[16,128]{1,0:T(8,128)S(1)} collective-permute-done((f32[16,128]{1,0:T(8,128)S(1)}, f32[16,128]{1,0:T(8,128)S(1)}, u32[]{:S(2)}, u32[]{:S(2)}) %collective-permute-start.8) | collective-permute-done | bytes 8224 | tf_op jit(solution)/shard_map/ppermute | solution.py:325
  31.3 2.1 %collective-permute-done.9 = f32[16,128]{1,0:T(8,128)S(1)} collective-permute-done((f32[16,128]{1,0:T(8,128)S(1)}, f32[16,128]{1,0:T(8,128)S(1)}, u32[]{:S(2)}, u32[]{:S(2)}) %collective-permute-start.9) | collective-permute-done | bytes 8224 | tf_op jit(solution)/shard_map/ppermute | solution.py:325
  33.5 0.0 collective-permute-done.7
  33.5 1.6 %shard_map.72 = f32[32,128]{1,0:T(8,128)S(1)} custom-call(f32[1024,2048]{1,0:T(8,128)S(1)} %get-tuple-element.17.plan_ref, f32[16,128]{1,0:T(8,128)S(1)} %add_add_fusion.3.rows_ref, f32[16,128]{1,0:T(8,128)S(1)} %add_add_fusion.2.terms_ref), custom_call_target="tpu_custom_call" | custom-call | flops 1073741824 | bytes 1048576 | tf_op jit(solution)/shard_map/pallas_call | solution.py:353
  35.1 0.1 collective-permute-start.10
  35.2 1.2 %collective-permute-done.10 = f32[32,128]{1,0:T(8,128)S(1)} collective-permute-done((f32[32,128]{1,0:T(8,128)S(1)}, f32[32,128]{1,0:T(8,128)S(1)}, u32[]{:S(2)}, u32[]{:S(2)}) %collective-permute-start.10) | collective-permute-done | bytes 16416 | tf_op jit(solution)/shard_map/ppermute | solution.py:325
  36.4 1.5 %collective-permute-start.12 = (f32[32,128]{1,0:T(8,128)S(1)}, f32[32,128]{1,0:T(8,128)S(1)}, u32[]{:S(2)}, u32[]{:S(2)}) collective-permute-start(f32[32,128]{1,0:T(8,128)S(1)} %add.79), channel_id=1, source_target_pairs={{0,16},{4,20},{8,24},{12,28},{16,0},{20,4},{24,8},{28,12},{1,17},{... | collective-permute-start | bytes 49160 | tf_op jit(solution)/shard_map/ppermute | solution.py:325
  37.9 0.9 %collective-permute-start.13 = (f32[32,128]{1,0:T(8,128)S(1)}, f32[32,128]{1,0:T(8,128)S(1)}, u32[]{:S(2)}, u32[]{:S(2)}) collective-permute-start(f32[32,128]{1,0:T(8,128)S(1)} %add.79), channel_id=1, source_target_pairs={{0,24},{4,28},{8,16},{12,20},{16,8},{20,12},{24,0},{28,4},{1,25},{... | collective-permute-start | bytes 49160 | tf_op jit(solution)/shard_map/ppermute | solution.py:325
  38.8 1.1 %collective-permute-start.11 = (f32[32,128]{1,0:T(8,128)S(1)}, f32[32,128]{1,0:T(8,128)S(1)}, u32[]{:S(2)}, u32[]{:S(2)}) collective-permute-start(f32[32,128]{1,0:T(8,128)S(1)} %add.79), channel_id=1, source_target_pairs={{0,8},{4,12},{8,0},{12,4},{16,24},{20,28},{24,16},{28,20},{1,9},{5... | collective-permute-start | bytes 49160 | tf_op jit(solution)/shard_map/ppermute | solution.py:325
  39.9 0.0 copy-done
  39.9 2.6 %shard_map.69 = (f32[64,1024]{1,0:T(8,128)S(1)}, bf16[2048,128]{1,0:T(8,128)(2,1)S(1)}) custom-call(f32[1024,2048]{1,0:T(8,128)S(1)} %get-tuple-element.17.plan_ref, f32[64,2048]{1,0:T(8,128)S(1)} %bitcast.12), custom_call_target="tpu_custom_call" | custom-call | flops 1073741824 | bytes 1048576 | tf_op jit(solution)/shard_map/pallas_call | solution.py:353
  42.5 0.0 collective-permute-done.12
  42.5 0.0 collective-permute-done.13
  42.5 0.0 collective-permute-done.11
  42.6 0.9 %shard_map.74 = f32[8,128]{1,0:T(8,128)S(1)} custom-call(f32[1024,2048]{1,0:T(8,128)S(1)} %get-tuple-element.17.plan_ref, f32[48,128]{1,0:T(8,128)S(1)} %add_add_fusion.cols_ref, f32[32,128]{1,0:T(8,128)S(1)} %add_add_fusion.1.bterms_ref.terms_ref), custom_call_target="tpu_custom_call" | custom-call | flops 1073741824 | bytes 1048576 | tf_op jit(solution)/shard_map/pallas_call | solution.py:353
  43.4 1.1 %collective-permute-start.15 = (f32[8,128]{1,0:T(8,128)S(1)}, f32[8,128]{1,0:T(8,128)S(1)}, u32[]{:S(2)}, u32[]{:S(2)}) collective-permute-start(f32[8,128]{1,0:T(8,128)S(1)} %shard_map.74), channel_id=1, source_target_pairs={{0,2},{1,3},{2,0},{3,1},{4,6},{5,7},{6,4},{7,5},{8,10},{9,11},{10,... | collective-permute-start | bytes 12296 | tf_op jit(solution)/shard_map/ppermute | solution.py:325
  44.5 1.8 %collective-permute-start.16 = (f32[8,128]{1,0:T(8,128)S(1)}, f32[8,128]{1,0:T(8,128)S(1)}, u32[]{:S(2)}, u32[]{:S(2)}) collective-permute-start(f32[8,128]{1,0:T(8,128)S(1)} %shard_map.74), channel_id=1, source_target_pairs={{0,3},{1,2},{2,1},{3,0},{4,7},{5,6},{6,5},{7,4},{8,11},{9,10},{10,... | collective-permute-start | bytes 12296 | tf_op jit(solution)/shard_map/ppermute | solution.py:325
  46.3 0.7 collective-permute-start.14
  47.0 2.8 %shard_map.73 = (f32[64,1024]{1,0:T(8,128)S(1)}, f32[8,2048]{1,0:T(8,128)S(1)}) custom-call(f32[1024,2048]{1,0:T(8,128)S(1)} %get-tuple-element.17.plan_ref, f32[1024,2048]{1,0:T(8,128)S(1)} %get-tuple-element.18.cot_ref, bf16[2048,128]{1,0:T(8,128)(2,1)S(1)} %get-tuple-element.19.right_ref, f32[48,128]{1,0:T(8,128)S(1)} %add_add_fusion.cols_ref, ...), custom_call_target="tpu_custom_call" | custom-call | flops 1073741824 | bytes 1048576 | tf_op jit(solution)/shard_map/pallas_call | solution.py:353
  49.8 0.0 collective-permute-done.15
  49.8 0.1 collective-permute-done.16
  49.9 0.0 collective-permute-done.14
  50.0 0.0 copy-done.1
  50.0 2.5 %shard_map.76 = f32[8,64,256]{2,1,0:T(8,128)S(1)} custom-call(f32[1024,2048]{1,0:T(8,128)S(1)} %get-tuple-element.17.plan_ref, f32[1024,2048]{1,0:T(8,128)S(1)} %get-tuple-element.18.cot_ref, f32[64,1024]{1,0:T(8,128)S(1)} %bitcast.14, f32[8,128]{1,0:T(8,128)S(1)} %get-tuple-element.28.alpha_ref, f32[8,2048]{1,0:T(8,128)S(1)} %get-tuple-element.29.beta_ref), custom_call_target="tpu_custom_call" | custom-call | flops 8589934592 | bytes 1048576 | tf_op jit(solution)/shard_map/pallas_call | solution.py:353
  52.5 0.1 collective-permute-start.23
  52.6 1.3 %collective-permute-start.17 = (f32[1,64,256]{2,1,0:T(8,128)S(1)}, f32[1,64,256]{2,1,0:T(8,128)S(1)}, u32[]{:S(2)}, u32[]{:S(2)}) collective-permute-start(f32[1,64,256]{2,1,0:T(8,128)S(1)} %get-tuple-element.25), channel_id=1, source_target_pairs={{0,1},{1,0},{2,3},{3,2},{4,5},{5,4},{6,7},{7,6},{8,9},{9,8},{10,11... | collective-permute-start | bytes 196616 | tf_op jit(solution)/shard_map/ppermute | solution.py:325
  53.9 0.8 %collective-permute-start.19 = (f32[1,64,256]{2,1,0:T(8,128)S(1)}, f32[1,64,256]{2,1,0:T(8,128)S(1)}, u32[]{:S(2)}, u32[]{:S(2)}) collective-permute-start(f32[1,64,256]{2,1,0:T(8,128)S(1)} %get-tuple-element.27), channel_id=1, source_target_pairs={{0,1},{1,0},{2,3},{3,2},{4,5},{5,4},{6,7},{7,6},{8,9},{9,8},{10,11... | collective-permute-start | bytes 196616 | tf_op jit(solution)/shard_map/ppermute | solution.py:325
  54.7 0.0 collective-permute-done.23
  54.8 1.1 %collective-permute-start.24 = (f32[2,64,256]{2,1,0:T(8,128)S(1)}, f32[2,64,256]{2,1,0:T(8,128)S(1)}, u32[]{:S(2)}, u32[]{:S(2)}) collective-permute-start(f32[2,64,256]{2,1,0:T(8,128)S(1)} %slice.27), channel_id=1, source_target_pairs={{0,8},{4,12},{8,0},{12,4},{16,24},{20,28},{24,16},{28,20},{1,9},{5... | collective-permute-start | bytes 393224 | tf_op jit(solution)/shard_map/ppermute | solution.py:325
  55.9 1.7 %collective-permute-done.17 = f32[1,64,256]{2,1,0:T(8,128)S(1)} collective-permute-done((f32[1,64,256]{2,1,0:T(8,128)S(1)}, f32[1,64,256]{2,1,0:T(8,128)S(1)}, u32[]{:S(2)}, u32[]{:S(2)}) %collective-permute-start.17) | collective-permute-done | bytes 65568 | tf_op jit(solution)/shard_map/ppermute | solution.py:325
  57.6 1.9 %collective-permute-start.18 = (f32[1,64,256]{2,1,0:T(8,128)S(1)}, f32[1,64,256]{2,1,0:T(8,128)S(1)}, u32[]{:S(2)}, u32[]{:S(2)}) collective-permute-start(f32[1,64,256]{2,1,0:T(8,128)S(1)} %add.86), channel_id=1, source_target_pairs={{0,2},{1,3},{2,0},{3,1},{4,6},{5,7},{6,4},{7,5},{8,10},{9,11},{10,... | collective-permute-start | bytes 196616 | tf_op jit(solution)/shard_map/ppermute | solution.py:325
  59.5 0.0 collective-permute-done.19
  59.5 1.2 %collective-permute-start.20 = (f32[1,64,256]{2,1,0:T(8,128)S(1)}, f32[1,64,256]{2,1,0:T(8,128)S(1)}, u32[]{:S(2)}, u32[]{:S(2)}) collective-permute-start(f32[1,64,256]{2,1,0:T(8,128)S(1)} %add.88), channel_id=1, source_target_pairs={{0,2},{1,3},{2,0},{3,1},{4,6},{5,7},{6,4},{7,5},{8,10},{9,11},{10,... | collective-permute-start | bytes 196616 | tf_op jit(solution)/shard_map/ppermute | solution.py:325
  60.7 4.7 %collective-permute-done.18 = f32[1,64,256]{2,1,0:T(8,128)S(1)} collective-permute-done((f32[1,64,256]{2,1,0:T(8,128)S(1)}, f32[1,64,256]{2,1,0:T(8,128)S(1)}, u32[]{:S(2)}, u32[]{:S(2)}) %collective-permute-start.18) | collective-permute-done | bytes 65568 | tf_op jit(solution)/shard_map/ppermute | solution.py:325
  65.3 0.1 collective-permute-start.21
  65.4 0.6 collective-permute-done.20
  66.0 1.5 %collective-permute-start.22 = (f32[1,64,256]{2,1,0:T(8,128)S(1)}, f32[1,64,256]{2,1,0:T(8,128)S(1)}, u32[]{:S(2)}, u32[]{:S(2)}) collective-permute-start(f32[1,64,256]{2,1,0:T(8,128)S(1)} %add.89.refs_1_), channel_id=1, source_target_pairs={{0,1},{1,0},{2,3},{3,2},{4,5},{5,4},{6,7},{7,6},{8,9},{9,8},{10,11... | collective-permute-start | bytes 196616 | tf_op jit(solution)/shard_map/ppermute | solution.py:325
  67.5 0.0 collective-permute-done.24
  67.6 1.6 %collective-permute-start.25 = (f32[64,256]{1,0:T(8,128)S(1)}, f32[64,256]{1,0:T(8,128)S(1)}, u32[]{:S(2)}, u32[]{:S(2)}) collective-permute-start(f32[64,256]{1,0:T(8,128)S(1)} %get-tuple-element.32), channel_id=1, source_target_pairs={{0,16},{4,20},{8,24},{12,28},{16,0},{20,4},{24,8},{28,12},{1,17},{... | collective-permute-start | bytes 196616 | tf_op jit(solution)/shard_map/ppermute | solution.py:325
  69.1 0.5 collective-permute-done.21.refs_2_
  69.7 0.7 collective-permute-done.22.refs_3_
  70.4 1.5 %collective-permute-done.25.refs_5_ = f32[64,256]{1,0:T(8,128)S(1)} collective-permute-done((f32[64,256]{1,0:T(8,128)S(1)}, f32[64,256]{1,0:T(8,128)S(1)}, u32[]{:S(2)}, u32[]{:S(2)}) %collective-permute-start.25) | collective-permute-done | bytes 65568 | tf_op jit(solution)/shard_map/ppermute | solution.py:325
  71.9 0.7 %shard_map.77 = (f32[64,1024]{1,0:T(8,128)}, f32[64,256]{1,0:T(8,128)}) custom-call(f32[1,64,256]{2,1,0:T(8,128)S(1)} %add.87.refs_0_, f32[1,64,256]{2,1,0:T(8,128)S(1)} %add.89.refs_1_, f32[1,64,256]{2,1,0:T(8,128)S(1)} %collective-permute-done.21.refs_2_, f32[1,64,256]{2,1,0:T(8,128)S(1)} %collective-permute-done.22.refs_3_, ...), custom_call_target="tpu_custom_call" | custom-call | flops 1073741824 | bytes 1048576 | tf_op jit(solution)/shard_map/pallas_call | solution.py:353
  (18 shorter events, 0.2 us)
Async XLA Ops:
  6.5 5.8 %collective-permute-start.1 = (f32[16,128]{1,0:T(8,128)S(1)}, f32[16,128]{1,0:T(8,128)S(1)}, u32[]{:S(2)}, u32[]{:S(2)}) collective-permute-start(f32[16,128]{1,0:T(8,128)S(1)} %get-tuple-element.20), channel_id=1, source_target_pairs={{0,2},{1,3},{2,0},{3,1},{4,6},{5,7},{6,4},{7,5},{8,10},{9,11},{10,... | collective-permute-start | bytes 24584 | tf_op jit(solution)/shard_map/ppermute | solution.py:325
  10.6 5.4 %collective-permute-start.2 = (f32[16,128]{1,0:T(8,128)S(1)}, f32[16,128]{1,0:T(8,128)S(1)}, u32[]{:S(2)}, u32[]{:S(2)}) collective-permute-start(f32[16,128]{1,0:T(8,128)S(1)} %get-tuple-element.20), channel_id=1, source_target_pairs={{0,3},{1,2},{2,1},{3,0},{4,7},{5,6},{6,5},{7,4},{8,11},{9,10},{10,... | collective-permute-start | bytes 24584 | tf_op jit(solution)/shard_map/ppermute | solution.py:325
  11.9 4.1 %collective-permute-start = (f32[16,128]{1,0:T(8,128)S(1)}, f32[16,128]{1,0:T(8,128)S(1)}, u32[]{:S(2)}, u32[]{:S(2)}) collective-permute-start(f32[16,128]{1,0:T(8,128)S(1)} %get-tuple-element.20), channel_id=1, source_target_pairs={{0,1},{1,0},{2,3},{3,2},{4,5},{5,4},{6,7},{7,6},{8,9},{9,8},{10,11... | collective-permute-start | bytes 24584 | tf_op jit(solution)/shard_map/ppermute | solution.py:325
  16.9 1.3 %collective-permute-start.3 = (f32[48,128]{1,0:T(8,128)S(1)}, f32[48,128]{1,0:T(8,128)S(1)}, u32[]{:S(2)}, u32[]{:S(2)}) collective-permute-start(f32[48,128]{1,0:T(8,128)S(1)} %shard_map.70), channel_id=1, source_target_pairs={{0,4},{4,0},{8,12},{12,8},{16,20},{20,16},{24,28},{28,24},{1,5},{5... | collective-permute-start | bytes 73736 | tf_op jit(solution)/shard_map/ppermute | solution.py:325
  18.2 3.8 %collective-permute-start.5 = (f32[48,128]{1,0:T(8,128)S(1)}, f32[48,128]{1,0:T(8,128)S(1)}, u32[]{:S(2)}, u32[]{:S(2)}) collective-permute-start(f32[48,128]{1,0:T(8,128)S(1)} %add.72), channel_id=1, source_target_pairs={{0,16},{4,20},{8,24},{12,28},{16,0},{20,4},{24,8},{28,12},{1,17},{... | collective-permute-start | bytes 73736 | tf_op jit(solution)/shard_map/ppermute | solution.py:325
  19.7 4.9 %collective-permute-start.6 = (f32[48,128]{1,0:T(8,128)S(1)}, f32[48,128]{1,0:T(8,128)S(1)}, u32[]{:S(2)}, u32[]{:S(2)}) collective-permute-start(f32[48,128]{1,0:T(8,128)S(1)} %add.72), channel_id=1, source_target_pairs={{0,24},{4,28},{8,16},{12,20},{16,8},{20,12},{24,0},{28,4},{1,25},{... | collective-permute-start | bytes 73736 | tf_op jit(solution)/shard_map/ppermute | solution.py:325
  21.1 3.8 %collective-permute-start.4 = (f32[48,128]{1,0:T(8,128)S(1)}, f32[48,128]{1,0:T(8,128)S(1)}, u32[]{:S(2)}, u32[]{:S(2)}) collective-permute-start(f32[48,128]{1,0:T(8,128)S(1)} %add.72), channel_id=1, source_target_pairs={{0,8},{4,12},{8,0},{12,4},{16,24},{20,28},{24,16},{28,20},{1,9},{5... | collective-permute-start | bytes 73736 | tf_op jit(solution)/shard_map/ppermute | solution.py:325
  25.0 14.9 %copy-start = (f32[2048,64]{0,1:T(8,128)S(1)}, f32[2048,64]{0,1:T(8,128)}, u32[]{:S(2)}) copy-start(f32[2048,64]{0,1:T(8,128)} %param.6) | copy-start | bytes 1572868
  26.7 4.6 %collective-permute-start.8 = (f32[16,128]{1,0:T(8,128)S(1)}, f32[16,128]{1,0:T(8,128)S(1)}, u32[]{:S(2)}, u32[]{:S(2)}) collective-permute-start(f32[16,128]{1,0:T(8,128)S(1)} %shard_map.71), channel_id=1, source_target_pairs={{0,2},{1,3},{2,0},{3,1},{4,6},{5,7},{6,4},{7,5},{8,10},{9,11},{10,... | collective-permute-start | bytes 24584 | tf_op jit(solution)/shard_map/ppermute | solution.py:325
  28.0 5.4 %collective-permute-start.9 = (f32[16,128]{1,0:T(8,128)S(1)}, f32[16,128]{1,0:T(8,128)S(1)}, u32[]{:S(2)}, u32[]{:S(2)}) collective-permute-start(f32[16,128]{1,0:T(8,128)S(1)} %shard_map.71), channel_id=1, source_target_pairs={{0,3},{1,2},{2,1},{3,0},{4,7},{5,6},{6,5},{7,4},{8,11},{9,10},{10,... | collective-permute-start | bytes 24584 | tf_op jit(solution)/shard_map/ppermute | solution.py:325
  28.9 4.5 %collective-permute-start.7 = (f32[16,128]{1,0:T(8,128)S(1)}, f32[16,128]{1,0:T(8,128)S(1)}, u32[]{:S(2)}, u32[]{:S(2)}) collective-permute-start(f32[16,128]{1,0:T(8,128)S(1)} %shard_map.71), channel_id=1, source_target_pairs={{0,1},{1,0},{2,3},{3,2},{4,5},{5,4},{6,7},{7,6},{8,9},{9,8},{10,11... | collective-permute-start | bytes 24584 | tf_op jit(solution)/shard_map/ppermute | solution.py:325
  35.1 1.2 %collective-permute-start.10 = (f32[32,128]{1,0:T(8,128)S(1)}, f32[32,128]{1,0:T(8,128)S(1)}, u32[]{:S(2)}, u32[]{:S(2)}) collective-permute-start(f32[32,128]{1,0:T(8,128)S(1)} %shard_map.72), channel_id=1, source_target_pairs={{0,4},{4,0},{8,12},{12,8},{16,20},{20,16},{24,28},{28,24},{1,5},{5... | collective-permute-start | bytes 49160 | tf_op jit(solution)/shard_map/ppermute | solution.py:325
  36.4 6.1 %collective-permute-start.12 = (f32[32,128]{1,0:T(8,128)S(1)}, f32[32,128]{1,0:T(8,128)S(1)}, u32[]{:S(2)}, u32[]{:S(2)}) collective-permute-start(f32[32,128]{1,0:T(8,128)S(1)} %add.79), channel_id=1, source_target_pairs={{0,16},{4,20},{8,24},{12,28},{16,0},{20,4},{24,8},{28,12},{1,17},{... | collective-permute-start | bytes 49160 | tf_op jit(solution)/shard_map/ppermute | solution.py:325
  37.9 4.6 %collective-permute-start.13 = (f32[32,128]{1,0:T(8,128)S(1)}, f32[32,128]{1,0:T(8,128)S(1)}, u32[]{:S(2)}, u32[]{:S(2)}) collective-permute-start(f32[32,128]{1,0:T(8,128)S(1)} %add.79), channel_id=1, source_target_pairs={{0,24},{4,28},{8,16},{12,20},{16,8},{20,12},{24,0},{28,4},{1,25},{... | collective-permute-start | bytes 49160 | tf_op jit(solution)/shard_map/ppermute | solution.py:325
  38.8 3.7 %collective-permute-start.11 = (f32[32,128]{1,0:T(8,128)S(1)}, f32[32,128]{1,0:T(8,128)S(1)}, u32[]{:S(2)}, u32[]{:S(2)}) collective-permute-start(f32[32,128]{1,0:T(8,128)S(1)} %add.79), channel_id=1, source_target_pairs={{0,8},{4,12},{8,0},{12,4},{16,24},{20,28},{24,16},{28,20},{1,9},{5... | collective-permute-start | bytes 49160 | tf_op jit(solution)/shard_map/ppermute | solution.py:325
  43.4 6.4 %collective-permute-start.15 = (f32[8,128]{1,0:T(8,128)S(1)}, f32[8,128]{1,0:T(8,128)S(1)}, u32[]{:S(2)}, u32[]{:S(2)}) collective-permute-start(f32[8,128]{1,0:T(8,128)S(1)} %shard_map.74), channel_id=1, source_target_pairs={{0,2},{1,3},{2,0},{3,1},{4,6},{5,7},{6,4},{7,5},{8,10},{9,11},{10,... | collective-permute-start | bytes 12296 | tf_op jit(solution)/shard_map/ppermute | solution.py:325
  44.5 5.4 %collective-permute-start.16 = (f32[8,128]{1,0:T(8,128)S(1)}, f32[8,128]{1,0:T(8,128)S(1)}, u32[]{:S(2)}, u32[]{:S(2)}) collective-permute-start(f32[8,128]{1,0:T(8,128)S(1)} %shard_map.74), channel_id=1, source_target_pairs={{0,3},{1,2},{2,1},{3,0},{4,7},{5,6},{6,5},{7,4},{8,11},{9,10},{10,... | collective-permute-start | bytes 12296 | tf_op jit(solution)/shard_map/ppermute | solution.py:325
  46.3 3.6 %collective-permute-start.14 = (f32[8,128]{1,0:T(8,128)S(1)}, f32[8,128]{1,0:T(8,128)S(1)}, u32[]{:S(2)}, u32[]{:S(2)}) collective-permute-start(f32[8,128]{1,0:T(8,128)S(1)} %shard_map.74), channel_id=1, source_target_pairs={{0,1},{1,0},{2,3},{3,2},{4,5},{5,4},{6,7},{7,6},{8,9},{9,8},{10,11... | collective-permute-start | bytes 12296 | tf_op jit(solution)/shard_map/ppermute | solution.py:325
  47.0 3.0 %copy-start.1 = (f32[1024,64]{0,1:T(8,128)S(1)}, f32[1024,64]{0,1:T(8,128)}, u32[]{:S(2)}) copy-start(f32[1024,64]{0,1:T(8,128)} %param.5) | copy-start | bytes 786436
  52.5 2.2 %collective-permute-start.23 = (f32[4,64,256]{2,1,0:T(8,128)S(1)}, f32[4,64,256]{2,1,0:T(8,128)S(1)}, u32[]{:S(2)}, u32[]{:S(2)}) collective-permute-start(f32[4,64,256]{2,1,0:T(8,128)S(1)} %slice.25), channel_id=1, source_target_pairs={{0,4},{4,0},{8,12},{12,8},{16,20},{20,16},{24,28},{28,24},{1,5},{5... | collective-permute-start | bytes 786440 | tf_op jit(solution)/shard_map/ppermute | solution.py:325
  52.6 5.0 %collective-permute-start.17 = (f32[1,64,256]{2,1,0:T(8,128)S(1)}, f32[1,64,256]{2,1,0:T(8,128)S(1)}, u32[]{:S(2)}, u32[]{:S(2)}) collective-permute-start(f32[1,64,256]{2,1,0:T(8,128)S(1)} %get-tuple-element.25), channel_id=1, source_target_pairs={{0,1},{1,0},{2,3},{3,2},{4,5},{5,4},{6,7},{7,6},{8,9},{9,8},{10,11... | collective-permute-start | bytes 196616 | tf_op jit(solution)/shard_map/ppermute | solution.py:325
  53.9 5.6 %collective-permute-start.19 = (f32[1,64,256]{2,1,0:T(8,128)S(1)}, f32[1,64,256]{2,1,0:T(8,128)S(1)}, u32[]{:S(2)}, u32[]{:S(2)}) collective-permute-start(f32[1,64,256]{2,1,0:T(8,128)S(1)} %get-tuple-element.27), channel_id=1, source_target_pairs={{0,1},{1,0},{2,3},{3,2},{4,5},{5,4},{6,7},{7,6},{8,9},{9,8},{10,11... | collective-permute-start | bytes 196616 | tf_op jit(solution)/shard_map/ppermute | solution.py:325
  54.8 12.8 %collective-permute-start.24 = (f32[2,64,256]{2,1,0:T(8,128)S(1)}, f32[2,64,256]{2,1,0:T(8,128)S(1)}, u32[]{:S(2)}, u32[]{:S(2)}) collective-permute-start(f32[2,64,256]{2,1,0:T(8,128)S(1)} %slice.27), channel_id=1, source_target_pairs={{0,8},{4,12},{8,0},{12,4},{16,24},{20,28},{24,16},{28,20},{1,9},{5... | collective-permute-start | bytes 393224 | tf_op jit(solution)/shard_map/ppermute | solution.py:325
  57.6 7.7 %collective-permute-start.18 = (f32[1,64,256]{2,1,0:T(8,128)S(1)}, f32[1,64,256]{2,1,0:T(8,128)S(1)}, u32[]{:S(2)}, u32[]{:S(2)}) collective-permute-start(f32[1,64,256]{2,1,0:T(8,128)S(1)} %add.86), channel_id=1, source_target_pairs={{0,2},{1,3},{2,0},{3,1},{4,6},{5,7},{6,4},{7,5},{8,10},{9,11},{10,... | collective-permute-start | bytes 196616 | tf_op jit(solution)/shard_map/ppermute | solution.py:325
  59.5 6.5 %collective-permute-start.20 = (f32[1,64,256]{2,1,0:T(8,128)S(1)}, f32[1,64,256]{2,1,0:T(8,128)S(1)}, u32[]{:S(2)}, u32[]{:S(2)}) collective-permute-start(f32[1,64,256]{2,1,0:T(8,128)S(1)} %add.88), channel_id=1, source_target_pairs={{0,2},{1,3},{2,0},{3,1},{4,6},{5,7},{6,4},{7,5},{8,10},{9,11},{10,... | collective-permute-start | bytes 196616 | tf_op jit(solution)/shard_map/ppermute | solution.py:325
  65.3 4.3 %collective-permute-start.21 = (f32[1,64,256]{2,1,0:T(8,128)S(1)}, f32[1,64,256]{2,1,0:T(8,128)S(1)}, u32[]{:S(2)}, u32[]{:S(2)}) collective-permute-start(f32[1,64,256]{2,1,0:T(8,128)S(1)} %add.87.refs_0_), channel_id=1, source_target_pairs={{0,1},{1,0},{2,3},{3,2},{4,5},{5,4},{6,7},{7,6},{8,9},{9,8},{10,11... | collective-permute-start | bytes 196616 | tf_op jit(solution)/shard_map/ppermute | solution.py:325
  66.0 4.3 %collective-permute-start.22 = (f32[1,64,256]{2,1,0:T(8,128)S(1)}, f32[1,64,256]{2,1,0:T(8,128)S(1)}, u32[]{:S(2)}, u32[]{:S(2)}) collective-permute-start(f32[1,64,256]{2,1,0:T(8,128)S(1)} %add.89.refs_1_), channel_id=1, source_target_pairs={{0,1},{1,0},{2,3},{3,2},{4,5},{5,4},{6,7},{7,6},{8,9},{9,8},{10,11... | collective-permute-start | bytes 196616 | tf_op jit(solution)/shard_map/ppermute | solution.py:325
  67.6 4.3 %collective-permute-start.25 = (f32[64,256]{1,0:T(8,128)S(1)}, f32[64,256]{1,0:T(8,128)S(1)}, u32[]{:S(2)}, u32[]{:S(2)}) collective-permute-start(f32[64,256]{1,0:T(8,128)S(1)} %get-tuple-element.32), channel_id=1, source_target_pairs={{0,16},{4,20},{8,24},{12,28},{16,0},{20,4},{24,8},{28,12},{1,17},{... | collective-permute-start | bytes 196616 | tf_op jit(solution)/shard_map/ppermute | solution.py:325
